TPU v7x, 32 devices: a whole 2x2x4 slice. The times are simulated.
32 devices in a mesh: fsdp: 8 (over z, x), ctx: 2 (over core), tp: 2 (over y).
Axes of the slice: x: 2, y: 2, z: 4, core: 2. Of those that a mesh axis runs over, the one named last changes fastest.
Arguments:
- hidden: bfloat16 [8, 448, 1024], P('fsdp', 'ctx'), may hold values from -6 to 6
- encoder: bfloat16 [8, 1500, 1024], P('fsdp', 'ctx'), may hold values from -6 to 6
- cotangent: bfloat16 [8, 448, 1024], P('fsdp', 'ctx'), may hold values from -6 to 6
- adapter_index: int32 [8], P('fsdp'), may hold values from 0 to 7
- ln_gains: float32 [3, 1024], replicated, may hold values from 0.25 to 1.75
- attn_in_weight: bfloat16 [6, 1024, 1024], P(None, 'fsdp', 'tp'), may hold values from -0.1875 to 0.1875
- attn_out_weight: bfloat16 [2, 1024, 1024], P(None, 'fsdp', 'tp'), may hold values from -0.75 to 0.75
- up_weight: bfloat16 [1024, 4096], P('fsdp', 'tp'), may hold values from -0.1875 to 0.1875
- down_weight: bfloat16 [1024, 4096], P('fsdp', 'tp'), may hold values from -0.09375 to 0.09375
- attn_adapt_in: bfloat16 [8, 8, 16, 1024], replicated, may hold values from -0.1875 to 0.1875
- attn_adapt_out: bfloat16 [8, 8, 16, 1024], replicated, may hold values from -2 to 2
- up_adapt_in: bfloat16 [8, 16, 1024], replicated, may hold values from -0.1875 to 0.1875
- up_adapt_out: bfloat16 [8, 16, 4096], replicated, may hold values from -2 to 2
- down_adapt_in: bfloat16 [8, 16, 4096], replicated, may hold values from -0.09375 to 0.09375
- down_adapt_out: bfloat16 [8, 16, 1024], replicated, may hold values from -2 to 2
Outputs:
- layer_out: bfloat16 [8, 448, 1024], P('fsdp', 'ctx')
- grad_hidden: float32 [8, 448, 1024], P('fsdp', 'ctx')
- grad_encoder: float32 [8, 1500, 1024], P('fsdp', 'ctx')
- grad_attn_adapt_in: float32 [8, 8, 16, 1024], P(None, None, None, ('fsdp', 'ctx', 'tp'))
- grad_attn_adapt_out: float32 [8, 8, 16, 1024], P(None, None, None, ('fsdp', 'ctx', 'tp'))
- grad_up_adapt_in: float32 [8, 16, 1024], P(None, None, ('fsdp', 'ctx', 'tp'))
- grad_up_adapt_out: float32 [8, 16, 4096], P(None, None, ('fsdp', 'ctx', 'tp'))
- grad_down_adapt_in: float32 [8, 16, 4096], P(None, None, ('fsdp', 'ctx', 'tp'))
- grad_down_adapt_out: float32 [8, 16, 1024], P(None, None, ('fsdp', 'ctx', 'tp'))
All inputs are finite; a program needn't handle non-finite values.
Results may differ from a plain program's by a relative error of at most 0.029.
Values may be sent and summed in bfloat16 or wider, within the bound.
No kernel may reach another device: no remote copies, remote signals or barrier semaphores. Data moves between devices by JAX's collectives and lax.ppermute only.
A program may use at most 128 MiB of HBM per device.

v0:
```python
import jax
import jax.numpy as jnp
from jax import lax
from jax.experimental import pallas as pl
from jax.experimental.pallas import tpu as pltpu
from jax.sharding import PartitionSpec as P

HEAD_DIM = 64
PAIR = 2 * HEAD_DIM
EPSILON = 1e-05
MASKED_SCORE = -1000000000.0
SCALE = HEAD_DIM ** (-0.5)
BF = jnp.bfloat16
F32 = jnp.float32


def mm(a, b):
    return lax.dot_general(a, b, (((1,), (0,)), ((), ())), preferred_element_type=F32)


def mm_nt(a, b):
    return lax.dot_general(a, b, (((1,), (1,)), ((), ())), preferred_element_type=F32)


def mm_tn(a, b):
    return lax.dot_general(a, b, (((0,), (0,)), ((), ())), preferred_element_type=F32)


def norm_parts(rows):
    centred = rows - jnp.mean(rows, axis=-1, keepdims=True)
    spread = jnp.mean(centred * centred, axis=-1, keepdims=True)
    inverse = lax.rsqrt(spread + EPSILON)
    return centred * inverse, inverse


def normalize(rows, gain):
    return norm_parts(rows)[0] * gain


def normalize_back(rows, gain, gradient):
    unit, inverse = norm_parts(rows)
    scaled = gradient * gain
    first = jnp.mean(scaled, axis=-1, keepdims=True)
    second = jnp.mean(scaled * unit, axis=-1, keepdims=True)
    return (scaled - first - unit * second) * inverse


def swap(value, axis):
    return lax.ppermute(value, axis, [(0, 1), (1, 0)])


def with_other(partial_value, axis):
    if lax.axis_size(axis) == 2:
        return partial_value, swap(partial_value, axis)
    return lax.psum(partial_value, axis), jnp.zeros_like(partial_value)


def matrix(ref):
    block = ref[...]
    return block.reshape(block.shape[0] * block.shape[2], block.shape[3])


def half_masks(rows):
    lane = lax.broadcasted_iota(jnp.int32, (rows, PAIR), 1)
    return lane < HEAD_DIM, lane >= HEAD_DIM


def pick_half(rows, keep):
    return jnp.where(keep, rows, jnp.zeros_like(rows))


def join_halves(first, second):
    row = lax.broadcasted_iota(jnp.int32, first.shape, 0)
    return jnp.where(row < HEAD_DIM, first, second).T


def pair_forward(queries, keys, values, limit):
    mixed, logsums = [], []
    for keep in half_masks(queries.shape[0]):
        mine = pick_half(queries, keep)
        scores = [limit(i, mm_nt(k, mine) * SCALE) for i, k in enumerate(keys)]
        top = jnp.max(scores[0], axis=0, keepdims=True)
        for s in scores[1:]:
            top = jnp.maximum(top, jnp.max(s, axis=0, keepdims=True))
        powers = [jnp.exp(s - top) for s in scores]
        total = sum(jnp.sum(e, axis=0, keepdims=True) for e in powers)
        share = 1.0 / total
        out = sum(mm_tn(v, (e * share).astype(BF)) for v, e in zip(values, powers))
        mixed.append(out)
        logsums.append(top + jnp.log(total))
    return join_halves(*mixed), logsums


def pair_backward(grad, queries, keys, values, logsums, limit):
    grad_query, grad_keys, grad_values = [], [0.0] * len(keys), [0.0] * len(keys)
    for keep, logsum in zip(half_masks(queries.shape[0]), logsums):
        mine = pick_half(queries, keep)
        grad_mine = pick_half(grad, keep)
        weights = [
            jnp.exp(limit(i, mm_nt(k, mine) * SCALE) - logsum) for i, k in enumerate(keys)
        ]
        grad_weights = [mm_nt(v, grad_mine) for v in values]
        inner = sum(
            jnp.sum(g * w, axis=0, keepdims=True) for g, w in zip(grad_weights, weights)
        )
        part = 0.0
        for i, key in enumerate(keys):
            grad_scores = (weights[i] * (grad_weights[i] - inner)).astype(BF)
            part = part + mm_tn(key, grad_scores)
            grad_keys[i] = grad_keys[i] + mm(grad_scores, mine)
            grad_values[i] = grad_values[i] + mm(weights[i].astype(BF), grad_mine)
        grad_query.append(part)
    return (
        (join_halves(*grad_query) * SCALE).astype(BF),
        [(g * SCALE).astype(BF) for g in grad_keys],
        [g.astype(BF) for g in grad_values],
    )


def no_limit(index, scores):
    return scores


def causal_limit(context):
    def limit(index, scores):
        if index == 0:
            key = lax.broadcasted_iota(jnp.int32, scores.shape, 0)
            query = lax.broadcasted_iota(jnp.int32, scores.shape, 1)
            return jnp.where(key <= query, scores, MASKED_SCORE)
        return jnp.where(context == 1, scores, MASKED_SCORE)

    return limit


def at_first(step=0):
    return pl.when(pl.program_id(0) == step)


def at_last():
    return pl.when(pl.program_id(0) == pl.num_programs(0) - 1)


def qkv_kernel(hidden, gains, weight, low_in, low_out, normed, query, key_value, low):
    @at_first()
    def _():
        normed[...] = normalize(hidden[...].astype(F32), gains[0:1, :]).astype(BF)

    rows = normed[...]
    rank_rows = mm_nt(rows, low_in[0]).astype(BF)
    low[0] = rank_rows
    value = (mm(rows, matrix(weight)) + mm(rank_rows, low_out[0])).astype(BF)

    @at_first()
    def _():
        query[...] = value

    @pl.when(pl.program_id(0) > 0)
    def _():
        key_value[0] = value


def frames_kernel(frames, weight, low_in, low_out, key_value, low):
    rows = frames[...]
    rank_rows = mm_nt(rows, low_in[0]).astype(BF)
    low[0] = rank_rows
    key_value[0] = (mm(rows, matrix(weight)) + mm(rank_rows, low_out[0])).astype(BF)


def self_kernel(
    where, query, mine, other, weight, low_in, low_out, mixed, logsum, branch, low, acc, low_acc
):
    @at_first()
    def _():
        acc[...] = jnp.zeros_like(acc)
        low_acc[...] = jnp.zeros_like(low_acc)

    out, logs = pair_forward(
        query[...], (mine[0], other[0]), (mine[1], other[1]), causal_limit(where[0])
    )
    out = out.astype(BF)
    mixed[...] = out
    logsum[0, 0:1, :] = logs[0]
    logsum[0, 1:2, :] = logs[1]
    acc[...] += mm_nt(out, matrix(weight))
    low_acc[...] += mm_nt(out, low_in[0])

    @at_last()
    def _():
        rank_rows = low_acc[...].astype(BF)
        low[...] = rank_rows
        branch[...] = (acc[...] + mm(rank_rows, low_out[0])).astype(BF)


def cross_kernel(
    hidden, branch_mine, branch_other, gains, query_weight, query_in, query_out, mine, other,
    weight, low_in, low_out,
    middle, normed, query, query_low, mixed, logsum, branch, low, acc, low_acc,
):
    @at_first()
    def _():
        acc[...] = jnp.zeros_like(acc)
        low_acc[...] = jnp.zeros_like(low_acc)
        total = hidden[...].astype(F32) + (
            branch_mine[...].astype(F32) + branch_other[...].astype(F32)
        )
        middle[...] = total
        rows = normalize(total, gains[1:2, :]).astype(BF)
        normed[...] = rows
        query_low[...] = mm_nt(rows, query_in[0]).astype(BF)

    queries = (
        mm(normed[...], matrix(query_weight)) + mm(query_low[...], query_out[0])
    ).astype(BF)
    query[...] = queries
    out, logs = pair_forward(queries, (mine[0], other[0]), (mine[1], other[1]), no_limit)
    out = out.astype(BF)
    mixed[...] = out
    logsum[0, 0:1, :] = logs[0]
    logsum[0, 1:2, :] = logs[1]
    acc[...] += mm_nt(out, matrix(weight))
    low_acc[...] += mm_nt(out, low_in[0])

    @at_last()
    def _():
        rank_rows = low_acc[...].astype(BF)
        low[...] = rank_rows
        branch[...] = (acc[...] + mm(rank_rows, low_out[0])).astype(BF)


def units_kernel(
    middle, branch_mine, branch_other, gains, cotangent, up, down, up_in, up_out, down_in,
    down_out,
    second, branch, grad_normed, table_up_in, table_up_out, table_down_in, table_down_out,
    normed, up_low, down_back, acc, back, low_acc, back_low,
):
    @at_first()
    def _():
        total = middle[...] + (branch_mine[...].astype(F32) + branch_other[...].astype(F32))
        second[...] = total
        rows = normalize(total, gains[2:3, :]).astype(BF)
        normed[...] = rows
        up_low[...] = mm_nt(rows, up_in[...]).astype(BF)
        down_back[...] = mm_nt(cotangent[...], down_out[...]).astype(BF)
        acc[...] = jnp.zeros_like(acc)
        back[...] = jnp.zeros_like(back)
        low_acc[...] = jnp.zeros_like(low_acc)
        back_low[...] = jnp.zeros_like(back_low)

    up_rows, down_rows = matrix(up), matrix(down)
    value = mm(normed[...], up_rows) + mm(up_low[...], up_out[...])
    spread = 1.0 + lax.erf(value * 0.7071067811865476)
    act = (0.5 * value * spread).astype(BF)
    slope = 0.5 * spread + value * (0.3989422804014327 * jnp.exp(-0.5 * value * value))
    acc[...] += mm_nt(act, down_rows)
    low_acc[...] += mm_nt(act, down_in[...])
    grad_act = mm(cotangent[...], down_rows) + mm(down_back[...], down_in[...])
    grad = (grad_act * slope).astype(BF)
    back[...] += mm_nt(grad, up_rows)
    back_low[...] += mm_nt(grad, up_out[...])
    table_up_out[...] = mm_tn(up_low[...], grad)
    table_down_in[...] = mm_tn(down_back[...], act)

    @at_last()
    def _():
        down_low = low_acc[...].astype(BF)
        branch[...] = (acc[...] + mm(down_low, down_out[...])).astype(BF)
        up_back = back_low[...].astype(BF)
        grad_normed[...] = (back[...] + mm(up_back, up_in[...])).astype(BF)
        table_up_in[...] = mm_tn(up_back, normed[...])
        table_down_out[...] = mm_tn(down_low, cotangent[...])


def attention_back(
    limit, slot, carried, rows, gains, grad_mine, grad_other, weight, low_in, low_out,
    query_weight, query_in, query_out, query, mixed, mine, other, logsum, normed, query_low, low,
    carry, grad_normed, grad_kv, grad_kv_other,
    table_in, table_out, table_query_in, table_query_out,
    narrow, back_low, acc, query_back,
):
    @at_first()
    def _():
        total = carried[...].astype(F32) + normalize_back(
            rows[...],
            gains[slot : slot + 1, :],
            grad_mine[...].astype(F32) + grad_other[...].astype(F32),
        )
        carry[...] = total
        narrow[...] = total.astype(BF)
        back_low[...] = mm_nt(narrow[...], low_out[0]).astype(BF)
        acc[...] = jnp.zeros_like(acc)
        query_back[...] = jnp.zeros_like(query_back)
        table_out[...] = mm_tn(low[...], narrow[...])

    grad = (mm(narrow[...], matrix(weight)) + mm(back_low[...], low_in[0])).astype(BF)
    table_in[...] = mm_tn(back_low[...], mixed[...])
    grad_query, grad_keys, grad_values = pair_backward(
        grad,
        query[...],
        (mine[0], other[0]),
        (mine[1], other[1]),
        (logsum[0, 0:1, :], logsum[0, 1:2, :]),
        limit,
    )
    grad_kv[0], grad_kv_other[0] = grad_keys
    grad_kv[1], grad_kv_other[1] = grad_values
    acc[...] += mm_nt(grad_query, matrix(query_weight))
    query_back[...] += mm_nt(grad_query, query_out[0])
    table_query_out[...] = mm_tn(query_low[...], grad_query)

    @at_last()
    def _():
        rank_rows = query_back[...].astype(BF)
        total = acc[...] + mm(rank_rows, query_in[0])
        grad_normed[...] = total.astype(grad_normed.dtype)
        table_query_in[...] = mm_tn(rank_rows, normed[...])


def cross_back_kernel(*refs):
    attention_back(no_limit, 2, *refs)


def self_back_kernel(where, *refs):
    attention_back(causal_limit(where[0]), 1, *refs)


def pair_project_kernel(
    grad_mine, grad_other, weight, low_in, low_out, rows, low, start, total, table_in, table_out,
    acc,
):
    @at_first()
    def _():
        acc[...] = start[...]

    pair_project_step(
        grad_mine, grad_other, weight, low_in, low_out, rows, low, total, table_in, table_out, acc
    )


def frames_back_kernel(
    grad_mine, grad_other, weight, low_in, low_out, rows, low, total, table_in, table_out, acc
):
    @at_first()
    def _():
        acc[...] = jnp.zeros_like(acc)

    pair_project_step(
        grad_mine, grad_other, weight, low_in, low_out, rows, low, total, table_in, table_out, acc
    )


def pair_project_step(
    grad_mine, grad_other, weight, low_in, low_out, rows, low, total, table_in, table_out, acc
):
    grad = (grad_mine[0].astype(F32) + grad_other[0].astype(F32)).astype(BF)
    rank_rows = mm_nt(grad, low_out[0]).astype(BF)
    acc[...] += mm_nt(grad, matrix(weight)) + mm(rank_rows, low_in[0])
    table_in[0] = mm_tn(rank_rows, rows[...])
    table_out[0] = mm_tn(low[0], grad)

    @at_last()
    def _():
        total[...] = acc[...].astype(BF)


LANE = 128
PIECE = 32


def pack_kernel(fulls, shares, wides, order, tagged, *refs):
    where = refs[0]
    tables = refs[1 : 1 + fulls + shares]
    broad = refs[1 + fulls + shares : 1 + fulls + shares + wides]
    keep, send = refs[1 + fulls + shares + wides :]
    context, tensor = where[0], where[1]
    blocks = keep.shape[0]
    per_group = (len(order) + 3) // 4
    rows = per_group * 16
    lane = lax.broadcasted_iota(jnp.int32, (rows, LANE), 1) // PIECE
    for f in range(blocks):
        shard = f * 2 // blocks
        local = f % (blocks // 2)

        def table_of(k):
            if k is None:
                return jnp.zeros((16, LANE), F32)
            if k < fulls:
                return tables[k][:, f * LANE : (f + 1) * LANE]
            part = tables[k][:, local * LANE : (local + 1) * LANE]
            return jnp.where(tensor == shard, part, 0.0)

        padded = list(order) + [None] * (4 * per_group - len(order))
        groups = [
            jnp.concatenate(
                [table_of(k) for k in padded[g * per_group : (g + 1) * per_group]], axis=0
            )
            for g in range(4)
        ]
        for p in range(4):
            value = jnp.zeros((rows, LANE), F32)
            for g in range(4):
                turned = pltpu.roll(groups[g], (PIECE * (g - p)) % LANE, 1)
                value = jnp.where(lane == g, turned, value)
            pieces = [value]
            for w in broad:
                at = local * 4 * LANE + p * LANE
                pieces.append(jnp.where(tensor == shard, w[:, at : at + LANE], 0.0))
            if tagged:
                tag = where[2].astype(F32) * 0.25
                pieces.append(jnp.full((16, LANE), 1.0, F32) * tag)
            whole = jnp.concatenate(pieces, axis=0)

            @pl.when(context == p // 2)
            def _(whole=whole, f=f, p=p):
                keep[f, p % 2] = whole

            @pl.when(context != p // 2)
            def _(whole=whole, f=f, p=p):
                send[f, p % 2] = whole


def unpack_kernel(early, late, attn_in, attn_out, up_in, up_out, down_in, down_out):
    clips = early.shape[0]
    adapters = attn_in.shape[1]
    tag_row = early.shape[1] - 16
    tags = [early[c, tag_row : tag_row + 1, :].astype(F32) for c in range(clips)]
    early_rows = [early[c].astype(F32) for c in range(clips)]
    late_rows = [late[c].astype(F32) for c in range(clips)]
    for a in range(adapters):
        first = jnp.zeros(early_rows[0].shape, F32)
        second = jnp.zeros(late_rows[0].shape, F32)
        for c in range(clips):
            same = (tags[c] > a - 0.5) & (tags[c] < a + 0.5)
            weight = jnp.where(same, 1.0, 0.0)
            first = first + early_rows[c] * weight
            second = second + late_rows[c] * weight

        def piece(block, k, per_group):
            g, at = k // per_group, 16 * (k % per_group)
            return block[at : at + 16, PIECE * g : PIECE * (g + 1)]

        for j in range(4):
            attn_in[j, a] = piece(second, j, 2)
            attn_out[j, a] = piece(second, 4 + j, 2)
            attn_in[4 + j, a] = piece(first, j, 3)
            attn_out[4 + j, a] = piece(first, 4 + j, 3)
        up_in[a] = piece(first, 8, 3)
        down_out[a] = piece(first, 9, 3)
        up_out[a] = first[48:64]
        down_in[a] = first[64:80]


def shape(dims, dtype):
    return jax.ShapeDtypeStruct(tuple(dims), dtype)


def fixed(array):
    zeros = (0,) * array.ndim
    return pl.BlockSpec(array.shape, lambda *_: zeros)


def fixed_out(*dims):
    zeros = (0,) * len(dims)
    return pl.BlockSpec(dims, lambda *_: zeros)


def call(kernel, steps, ins, outs, scratch=(), scalars=None, name=None):
    arrays = [a for a, _ in ins]
    spec = pltpu.PrefetchScalarGridSpec(
        num_scalar_prefetch=0 if scalars is None else 1,
        grid=(steps,),
        in_specs=[s for _, s in ins],
        out_specs=[s for _, s in outs],
        scratch_shapes=list(scratch),
    )
    run = pl.pallas_call(
        kernel,
        grid_spec=spec,
        out_shape=[o for o, _ in outs],
        compiler_params=pltpu.CompilerParams(dimension_semantics=("arbitrary",)),
        name=name,
    )
    return run(*arrays) if scalars is None else run(scalars, *arrays)


def on_device(
    hidden,
    encoder,
    cotangent,
    adapter_index,
    ln_gains,
    attn_in_weight,
    attn_out_weight,
    up_weight,
    down_weight,
    attn_adapt_in,
    attn_adapt_out,
    up_adapt_in,
    up_adapt_out,
    down_adapt_in,
    down_adapt_out,
):
    fsdp_size = lax.axis_size("fsdp")
    ctx_size = lax.axis_size("ctx")
    tp_size = lax.axis_size("tp")
    tensor_index = lax.axis_index("tp")
    context_index = lax.axis_index("ctx")
    hidden, encoder, cotangent = hidden[0], encoder[0], cotangent[0]
    rows, width = hidden.shape
    frames = encoder.shape[0]
    wide = up_adapt_out.shape[2]
    cols = attn_in_weight.shape[2]
    units = up_weight.shape[1]
    rank = attn_adapt_in.shape[2]
    adapters = attn_adapt_in.shape[1]
    pairs = cols // PAIR
    head_start = tensor_index * cols
    unit_start = tensor_index * units
    mine = adapter_index[0]
    scalars = jnp.stack(
        [context_index.astype(jnp.int32), tensor_index.astype(jnp.int32), mine]
    )

    half_rows = attn_in_weight.shape[1] // ctx_size
    shards = fsdp_size * ctx_size

    def my_half(table):
        return lax.dynamic_slice_in_dim(
            table, context_index * half_rows, half_rows, axis=table.ndim - 2
        )

    attn_half = jnp.concatenate([my_half(attn_in_weight), my_half(attn_out_weight)], axis=0)
    ff_half = jnp.stack([my_half(up_weight), my_half(down_weight)])
    attn_full = lax.all_gather(attn_half, ("fsdp", "ctx"), axis=0)
    ff_full = lax.all_gather(ff_half, ("fsdp", "ctx"), axis=0)

    sel_in = lax.dynamic_index_in_dim(attn_adapt_in, mine, 1, keepdims=False)
    sel_out = lax.dynamic_index_in_dim(attn_adapt_out, mine, 1, keepdims=False)
    part_in = lax.dynamic_slice_in_dim(sel_in, head_start, cols, 2)
    part_out = lax.dynamic_slice_in_dim(sel_out, head_start, cols, 2)
    up_in = lax.dynamic_index_in_dim(up_adapt_in, mine, 0, keepdims=False)
    up_out = lax.dynamic_slice(up_adapt_out, (mine, 0, unit_start), (1, rank, units))[0]
    down_in = lax.dynamic_slice(down_adapt_in, (mine, 0, unit_start), (1, rank, units))[0]
    down_out = lax.dynamic_index_in_dim(down_adapt_out, mine, 0, keepdims=False)

    def weight_cols(slot):
        return attn_full, pl.BlockSpec((shards, 1, half_rows, cols), lambda i, *_: (0, slot(i), 0, 0))

    def weight_pair(slot):
        return attn_full, pl.BlockSpec((shards, 1, half_rows, PAIR), lambda p, *_: (0, slot, 0, p))

    def slot_of(table, slot):
        return table, pl.BlockSpec((1,) + table.shape[1:], lambda i, *_: (slot(i), 0, 0))

    def slot_pair(table, slot):
        return table, pl.BlockSpec((1, rank, PAIR), lambda p, *_: (slot, 0, p))

    def whole(array):
        return array, fixed(array)

    def out(dims, dtype):
        return shape(dims, dtype), fixed_out(*dims)

    def by_pair(count, dtype=BF):
        return shape((count, cols), dtype), pl.BlockSpec((count, PAIR), lambda p, *_: (0, p))

    def kv_pair(array):
        return array, pl.BlockSpec((2, array.shape[1], PAIR), lambda p, *_: (0, 0, p))

    def at(array, first=0):
        return array, pl.BlockSpec((1,) + array.shape[1:], lambda i, *_: (first + i, 0, 0))

    logsum_out = (
        shape((pairs, 2, rows), F32),
        pl.BlockSpec((1, 2, rows), lambda p, *_: (p, 0, 0)),
    )

    def logsum_in(array):
        return array, pl.BlockSpec((1, 2, rows), lambda p, *_: (p, 0, 0))

    def pair_in(array):
        return array, pl.BlockSpec((array.shape[0], PAIR), lambda p, *_: (0, p))

    wide_acc = pltpu.VMEM((rows, width), F32)
    rank_acc = pltpu.VMEM((rows, rank), F32)
    rank_keep = pltpu.VMEM((rows, rank), BF)

    n1, query, self_kv, self_low = call(
        qkv_kernel,
        3,
        [
            whole(hidden),
            whole(ln_gains),
            weight_cols(lambda i: i),
            slot_of(sel_in, lambda i: i),
            slot_of(part_out, lambda i: i),
        ],
        [
            out((rows, width), BF),
            out((rows, cols), BF),
            (
                shape((2, rows, cols), BF),
                pl.BlockSpec((1, rows, cols), lambda i: (jnp.maximum(i - 1, 0), 0, 0)),
            ),
            (shape((3, rows, rank), BF), pl.BlockSpec((1, rows, rank), lambda i: (i, 0, 0))),
        ],
        name="qkv",
    )
    self_kv_other = swap(self_kv, "ctx")
    cross_kv, frames_low = call(
        frames_kernel,
        2,
        [
            whole(encoder),
            weight_cols(lambda i: 4 + i),
            slot_of(sel_in, lambda i: 5 + i),
            slot_of(part_out, lambda i: 5 + i),
        ],
        [
            (
                shape((2, frames, cols), BF),
                pl.BlockSpec((1, frames, cols), lambda i: (i, 0, 0)),
            ),
            (
                shape((2, frames, rank), BF),
                pl.BlockSpec((1, frames, rank), lambda i: (i, 0, 0)),
            ),
        ],
        name="frames",
    )
    cross_kv_other = swap(cross_kv, "ctx")
    self_mixed, self_logsum, branch, self_o_low = call(
        self_kernel,
        pairs,
        [
            pair_in(query),
            kv_pair(self_kv),
            kv_pair(self_kv_other),
            weight_pair(6),
            slot_pair(part_in, 3),
            slot_of(sel_out, lambda i: 3),
        ],
        [by_pair(rows), logsum_out, out((rows, width), BF), out((rows, rank), BF)],
        [wide_acc, rank_acc],
        scalars,
        name="self_attention",
    )
    branch, branch_other = with_other(branch, "tp")
    first_mid, n2, cross_q, cross_q_low, cross_mixed, cross_logsum, branch, cross_o_low = call(
        cross_kernel,
        pairs,
        [
            whole(hidden),
            whole(branch),
            whole(branch_other),
            whole(ln_gains),
            weight_pair(3),
            slot_of(sel_in, lambda i: 4),
            slot_pair(part_out, 4),
            kv_pair(cross_kv),
            kv_pair(cross_kv_other),
            weight_pair(7),
            slot_pair(part_in, 7),
            slot_of(sel_out, lambda i: 7),
        ],
        [
            out((rows, width), F32),
            out((rows, width), BF),
            by_pair(rows),
            out((rows, rank), BF),
            by_pair(rows),
            logsum_out,
            out((rows, width), BF),
            out((rows, rank), BF),
        ],
        [wide_acc, rank_acc],
        name="cross_attention",
    )
    branch, branch_other = with_other(branch, "tp")
    chunk = min(units, 512)

    def unit_weight(slot):
        return ff_full, pl.BlockSpec((shards, 1, half_rows, chunk), lambda i: (0, slot, 0, i))

    def unit_cols(array):
        return array, pl.BlockSpec((rank, chunk), lambda i: (0, i))

    second_mid, branch, grad_n3, up_in_t, up_out_t, down_in_t, down_out_t = call(
        units_kernel,
        units // chunk,
        [
            whole(first_mid),
            whole(branch),
            whole(branch_other),
            whole(ln_gains),
            whole(cotangent),
            unit_weight(0),
            unit_weight(1),
            whole(up_in),
            unit_cols(up_out),
            unit_cols(down_in),
            whole(down_out),
        ],
        [
            out((rows, width), F32),
            out((rows, width), BF),
            out((rows, width), BF),
            out((rank, width), F32),
            unit_cols(shape((rank, units), F32)),
            unit_cols(shape((rank, units), F32)),
            out((rank, width), F32),
        ],
        [
            pltpu.VMEM((rows, width), BF),
            rank_keep,
            rank_keep,
            wide_acc,
            wide_acc,
            rank_acc,
            rank_acc,
        ],
        name="units",
    )
    grad_n3, grad_n3_other = with_other(grad_n3, "tp")
    branch, branch_other = with_other(branch, "tp")
    layer_out = (
        second_mid + (branch.astype(F32) + branch_other.astype(F32))
    ).astype(BF)

    def back_call(
        kernel, scalar, carried, middle, grad, grad_other, slots, queries, mixed, kv, kv_other,
        logsum, normed, query_low, low, kind, name,
    ):
        weight_slot, low_slot, query_slot, query_low_slot = slots
        count = kv.shape[1]
        kv_out = (
            shape((2, count, cols), BF),
            pl.BlockSpec((2, count, PAIR), lambda p, *_: (0, 0, p)),
        )
        return call(
            kernel,
            pairs,
            [
                whole(carried),
                whole(middle),
                whole(ln_gains),
                whole(grad),
                whole(grad_other),
                weight_pair(weight_slot),
                slot_pair(part_in, low_slot),
                slot_of(sel_out, lambda i: low_slot),
                weight_pair(query_slot),
                slot_of(sel_in, lambda i: query_low_slot),
                slot_pair(part_out, query_low_slot),
                pair_in(queries),
                pair_in(mixed),
                kv_pair(kv),
                kv_pair(kv_other),
                logsum_in(logsum),
                whole(normed),
                whole(query_low),
                whole(low),
            ],
            [
                out((rows, width), F32),
                out((rows, width), kind),
                kv_out,
                kv_out,
                by_pair(rank, F32),
                out((rank, width), F32),
                out((rank, width), F32),
                by_pair(rank, F32),
            ],
            [pltpu.VMEM((rows, width), BF), rank_keep, wide_acc, rank_acc],
            scalar,
            name=name,
        )

    grad_second, grad_n2, grad_ckv, grad_ckv_send, co_in_t, co_out_t, cq_in_t, cq_out_t = back_call(
        cross_back_kernel, None, cotangent, second_mid, grad_n3, grad_n3_other, (7, 7, 3, 4),
        cross_q, cross_mixed, cross_kv, cross_kv_other, cross_logsum, n2, cross_q_low,
        cross_o_low, BF, "cross_back",
    )
    grad_n2, grad_n2_other = with_other(grad_n2, "tp")
    grad_ckv_other = swap(grad_ckv_send, "ctx")
    grad_frames, ckv_in_t, ckv_out_t = call(
        frames_back_kernel,
        2,
        [
            at(grad_ckv),
            at(grad_ckv_other),
            weight_cols(lambda i: 4 + i),
            slot_of(sel_in, lambda i: 5 + i),
            slot_of(part_out, lambda i: 5 + i),
            whole(encoder),
            at(frames_low),
        ],
        [
            out((frames, width), BF),
            at(shape((2, rank, width), F32)),
            at(shape((2, rank, cols), F32)),
        ],
        [pltpu.VMEM((frames, width), F32)],
        name="frames_back",
    )
    grad_frames, grad_frames_other = with_other(grad_frames, "tp")
    grad_encoder = grad_frames.astype(F32) + grad_frames_other.astype(F32)
    grad_first, grad_n1_start, grad_skv, grad_skv_send, so_in_t, so_out_t, q_in_t, q_out_t = back_call(
        self_back_kernel, scalars, grad_second, first_mid, grad_n2, grad_n2_other, (6, 3, 0, 0),
        query, self_mixed, self_kv, self_kv_other, self_logsum, n1, self_low[0],
        self_o_low, F32, "self_back",
    )
    grad_skv_other = swap(grad_skv_send, "ctx")
    grad_n1, kv_in_t, kv_out_t = call(
        pair_project_kernel,
        2,
        [
            at(grad_skv),
            at(grad_skv_other),
            weight_cols(lambda i: 1 + i),
            slot_of(sel_in, lambda i: 1 + i),
            slot_of(part_out, lambda i: 1 + i),
            whole(n1),
            at(self_low, 1),
            whole(grad_n1_start),
        ],
        [
            out((rows, width), BF),
            at(shape((2, rank, width), F32)),
            at(shape((2, rank, cols), F32)),
        ],
        [wide_acc],
        name="self_project_back",
    )
    grad_n1, grad_n1_other = with_other(grad_n1, "tp")
    grad_hidden = grad_first + normalize_back(
        hidden.astype(F32), ln_gains[0], grad_n1.astype(F32) + grad_n1_other.astype(F32)
    )

    early_full = [cq_in_t, ckv_in_t[0], ckv_in_t[1], co_out_t, up_in_t, down_out_t]
    early_part = [co_in_t, cq_out_t, ckv_out_t[0], ckv_out_t[1]]
    late_full = [q_in_t, kv_in_t[0], kv_in_t[1], so_out_t]
    late_part = [so_in_t, q_out_t, kv_out_t[0], kv_out_t[1]]
    broad = [up_out_t, down_in_t]
    regular = (
        ctx_size == 2 and tp_size == 2 and rank == 16
        and width == LANE * fsdp_size and wide == 4 * LANE * fsdp_size
    )
    if regular:

        def exchange(full, part, wides, order, tagged, name):
            per_group = (len(order) + 3) // 4
            count = 16 * (per_group + len(wides) + tagged)
            dims = (fsdp_size, 2, count, LANE)

            def kernel(*refs):
                pack_kernel(len(full), len(part), len(wides), order, tagged, *refs)

            keep, send = call(
                kernel,
                1,
                [whole(a) for a in full + part + wides],
                [out(dims, F32), out(dims, F32)],
                scalars=scalars,
                name=name,
            )
            recv = swap(send, "ctx")

            def pick(i):
                return lax.dynamic_index_in_dim(keep, i, 1, keepdims=False) + (
                    lax.dynamic_index_in_dim(recv, i, 1, keepdims=False)
                )

            away = swap(pick(1 - tensor_index).astype(BF), "tp")
            total = (pick(tensor_index) + away.astype(F32)).astype(BF)
            return lax.all_to_all(total, "fsdp", 0, 0, tiled=True)

        early = exchange(
            early_full, early_part, broad, (0, 1, 2, 6, 7, 8, 9, 3, 4, 5), 1, "pack_early"
        )
        late = exchange(late_full, late_part, [], (0, 1, 2, 4, 5, 6, 7, 3), 0, "pack_late")
        narrow_out = (attn_adapt_in.shape[0], adapters, rank, PIECE)
        tables = call(
            unpack_kernel,
            1,
            [whole(early), whole(late)],
            [
                out(narrow_out, F32),
                out(narrow_out, F32),
                out((adapters, rank, PIECE), F32),
                out((adapters, rank, LANE), F32),
                out((adapters, rank, LANE), F32),
                out((adapters, rank, PIECE), F32),
            ],
            name="unpack",
        )
    else:
        chosen = (mine == jnp.arange(adapters, dtype=jnp.int32)).astype(F32)

        def summed(parts, start, full):
            def spread_out(part):
                if part.shape[1] == full:
                    return part
                blank = jnp.zeros((part.shape[0], full), F32)
                return lax.dynamic_update_slice_in_dim(blank, part, start, axis=1)

            stacked = jnp.stack([spread_out(p) for p in parts])
            table = chosen[None, :, None, None] * stacked[:, None]
            return lax.psum_scatter(
                table, ("fsdp", "ctx", "tp"), scatter_dimension=3, tiled=True
            )

        attn_in_t = summed(
            late_full[:3] + [so_in_t] + early_full[:3] + [co_in_t], head_start, width
        )
        attn_out_t = summed(
            late_part[1:] + [so_out_t] + early_part[1:] + [co_out_t], head_start, width
        )
        small = summed([up_in_t, down_out_t], head_start, width)
        large = summed(broad, unit_start, wide)
        tables = (attn_in_t, attn_out_t, small[0], large[0], large[1], small[1])
    return (
        layer_out[None],
        grad_hidden[None],
        grad_encoder[None],
        *tables,
    )
def solution(mesh):
    in_specs = (
        P("fsdp", "ctx", None),
        P("fsdp", "ctx", None),
        P("fsdp", "ctx", None),
        P("fsdp"),
        P(),
        P(None, "fsdp", "tp"),
        P(None, "fsdp", "tp"),
        P("fsdp", "tp"),
        P("fsdp", "tp"),
        P(),
        P(),
        P(),
        P(),
        P(),
        P(),
    )
    out_specs = (
        P("fsdp", "ctx", None),
        P("fsdp", "ctx", None),
        P("fsdp", "ctx", None),
        P(None, None, None, ("fsdp", "ctx", "tp")),
        P(None, None, None, ("fsdp", "ctx", "tp")),
        P(None, None, ("fsdp", "ctx", "tp")),
        P(None, None, ("fsdp", "ctx", "tp")),
        P(None, None, ("fsdp", "ctx", "tp")),
        P(None, None, ("fsdp", "ctx", "tp")),
    )
    return jax.shard_map(
        on_device, mesh=mesh, in_specs=in_specs, out_specs=out_specs, check_vma=False
    )
```

profile of v0, /device:TPU:0, one launch (start us, length us, event | category | flops | bytes accessed | tf_op | source)
XLA Modules:
  0.0 350.9 jit_solution(15105424648898031814)
XLA Ops:
  11.9 1.7 dynamic-slice_bitcast_fusion.5.low_out.query_out.refs_10_
  14.3 73.5 %all-gather.5.cloned.1.call-done = bf16[128,64,512]{2,1,0:T(8,128)(2,1)} async-done(((bf16[8,64,512]{2,1,0:T(8,128)(2,1)}), bf16[128,64,512]{2,1,0:T(8,128)(2,1)}) %all-gather.5.cloned.1.call-update) | async-done | bytes 8388624 | tf_op jit(solution)/shard_map/all_gather | solution.py:533
  87.8 7.1 %frames.1 = (bf16[2,750,512]{2,1,0:T(8,128)(2,1)}, bf16[2,750,16]{2,1,0:T(8,128)(2,1)}) custom-call(bf16[750,1024]{1,0:T(8,128)(2,1)} %bitcast.87, bf16[16,8,64,512]{3,2,1,0:T(8,128)(2,1)} %bitcast.72, bf16[8,16,1024]{2,1,0:T(8,128)(2,1)} %dynamic-slice_bitcast_fusion.3.low_in.query_in.refs_9_, ...), custom_call_target="tpu_custom_call" | custom-call | tf_op jit(solution)/shard_map/frames/pallas_call | solution.py:482
  94.9 4.2 %copy.31 = bf16[2,750,512]{2,0,1:T(2,128)(2,1)} copy(bf16[2,750,512]{2,1,0:T(8,128)(2,1)} %get-tuple-element.69.mine.refs_13_) | data formatting | bytes 3072000 | tf_op jit(solution)/shard_map/frames/pallas_call | solution.py:482
  99.4 5.7 %qkv.1 = (bf16[224,1024]{1,0:T(8,128)(2,1)}, bf16[224,512]{1,0:T(8,128)(2,1)}, bf16[2,224,512]{2,1,0:T(8,128)(2,1)}, bf16[3,224,16]{2,1,0:T(8,128)(2,1)}) custom-call(bf16[224,1024]{1,0:T(8,128)(2,1)} %bitcast.85, f32[3,1024]{1,0:T(4,128)} %refs_2_.3, bf16[16,8,64,512]{3,2,1,0:T(8,128)(2,1)} %bitcast.73, ...), custom_call_target="tpu_custom_call" | custom-call | tf_op jit(solution)/shard_map/qkv/pallas_call | solution.py:482
  106.7 1.7 dynamic-slice_bitcast_fusion.2.low_out.refs_7_
  109.1 7.3 %self_attention.1 = (bf16[224,512]{1,0:T(8,128)(2,1)}, f32[4,2,224]{2,1,0:T(2,128)}, bf16[224,1024]{1,0:T(8,128)(2,1)}, bf16[224,16]{1,0:T(8,128)(2,1)}) custom-call(s32[3]{0:T(128)} %pad_add_fusion.where.refs_0_, bf16[224,512]{1,0:T(8,128)(2,1)} %get-tuple-element.66.query.refs_11_, bf16[2,224,512]{2,1,0:T(8,128)(2,1)} %get-tuple-element.67.mine.refs_13_, ...), custom_call_target="tpu_custom_call" | custom-call | tf_op jit(solution)/shard_map/self_attention/pallas_call | solution.py:482
  118.0 2.8 copy.32.other.refs_14_
  120.8 8.6 %collective-permute-done.1.branch_other = bf16[224,1024]{1,0:T(8,128)(2,1)S(1)} collective-permute-done((bf16[224,1024]{1,0:T(8,128)(2,1)}, bf16[224,1024]{1,0:T(8,128)(2,1)S(1)}, u32[]{:S(2)}, u32[]{:S(2)}) %collective-permute-start.1) | collective-permute-done | bytes 458784 | tf_op jit(solution)/shard_map/ppermute | solution.py:49
  130.2 13.5 %cross_attention.1 = (f32[224,1024]{1,0:T(8,128)}, bf16[224,1024]{1,0:T(8,128)(2,1)}, bf16[224,512]{1,0:T(8,128)(2,1)}, bf16[224,16]{1,0:T(8,128)(2,1)}, bf16[22...) custom-call(bf16[224,1024]{1,0:T(8,128)(2,1)} %bitcast.86, ...), custom_call_target="tpu_custom_call" | custom-call | tf_op jit(solution)/shard_map/cross_attention/pallas_call | solution.py:482
  148.1 15.3 %all-gather.7.cloned.1.call-done = bf16[32,64,2048]{2,1,0:T(8,128)(2,1)} async-done(((bf16[2,64,2048]{2,1,0:T(8,128)(2,1)}), bf16[32,64,2048]{2,1,0:T(8,128)(2,1)}) %all-gather.7.cloned.1.call-update) | async-done | bytes 8388624 | tf_op jit(solution)/shard_map/all_gather | solution.py:534
  164.2 11.5 %units.1 = (f32[224,1024]{1,0:T(8,128)}, bf16[224,1024]{1,0:T(8,128)(2,1)}, bf16[224,1024]{1,0:T(8,128)(2,1)}, f32[16,1024]{1,0:T(8,128)}, f32[16,2048]{1,0:T(8,...) custom-call(f32[224,1024]{1,0:T(8,128)} %get-tuple-element.70.middle.refs_1_, ...), custom_call_target="tpu_custom_call" | custom-call | tf_op jit(solution)/shard_map/units/pallas_call | solution.py:482
  177.3 11.4 %collective-permute-done.5.refs_4_ = bf16[224,1024]{1,0:T(8,128)(2,1)S(1)} collective-permute-done((bf16[224,1024]{1,0:T(8,128)(2,1)}, bf16[224,1024]{1,0:T(8,128)(2,1)S(1)}, u32[]{:S(2)}, u32[]{:S(2)}) %collective-permute-start.5) | collective-permute-done | bytes 458784 | tf_op jit(solution)/shard_map/ppermute | solution.py:49
  189.5 18.1 %cross_back.1 = (f32[224,1024]{1,0:T(8,128)}, bf16[224,1024]{1,0:T(8,128)(2,1)}, bf16[2,750,512]{2,1,0:T(8,128)(2,1)}, bf16[2,750,512]{2,1,0:T(8,128)(2,1)}, f32...) custom-call(bf16[224,1024]{1,0:T(8,128)(2,1)} %bitcast.90, ...), custom_call_target="tpu_custom_call" | custom-call | tf_op jit(solution)/shard_map/cross_back/pallas_call | solution.py:482
  207.6 3.1 copy.34
  213.9 9.8 %collective-permute-done.6.refs_4_ = bf16[224,1024]{1,0:T(8,128)(2,1)S(1)} collective-permute-done((bf16[224,1024]{1,0:T(8,128)(2,1)S(1)}, bf16[224,1024]{1,0:T(8,128)(2,1)S(1)}, u32[]{:S(2)}, u32[]{:S(2)}) %collective-permute-start.6) | collective-permute-done | bytes 458784 | tf_op jit(solution)/shard_map/ppermute | solution.py:49
  224.4 12.0 %self_back.1 = (f32[224,1024]{1,0:T(8,128)}, f32[224,1024]{1,0:T(8,128)}, bf16[2,224,512]{2,1,0:T(8,128)(2,1)}, bf16[2,224,512]{2,1,0:T(8,128)(2,1)}, f32[16,512...) custom-call(s32[3]{0:T(128)} %pad_add_fusion.where.refs_0_, ...), custom_call_target="tpu_custom_call" | custom-call | tf_op jit(solution)/shard_map/self_back/pallas_call | solution.py:482
  239.8 4.6 %self_project_back.1 = (bf16[224,1024]{1,0:T(8,128)(2,1)}, f32[2,16,1024]{2,1,0:T(8,128)}, f32[2,16,512]{2,1,0:T(8,128)}) custom-call(bf16[2,224,512]{2,1,0:T(8,128)(2,1)} %get-tuple-element.89.grad_mine, bf16[2,224,512]{2,1,0:T(8,128)(2,1)} %copy-done.10, bf16[16,8,64,512]{3,2,1,0:T(8,128)(2,1)} %bitcast.81, ...), custom_call_target="tpu_custom_call" | custom-call | tf_op jit(solution)/shard_map/self_project_back/pallas_call | solution.py:482
  247.3 5.0 %pack_late.1 = (f32[8,2,32,128]{3,2,1,0:T(8,128)}, f32[8,2,32,128]{3,2,1,0:T(8,128)}) custom-call(s32[3]{0:T(128)} %pad_add_fusion.where.refs_0_, f32[16,1024]{1,0:T(8,128)} %get-tuple-element.109.refs_1_, f32[16,1024]{1,0:T(8,128)} %get-tuple-element.144.refs_2_, f32[16,1024]{1,0:T(8,128)} %get-tuple-element.143.refs_3_, ...), custom_call_target="tpu_custom_call" | custom-call | tf_op jit(solution)/shard_map/pack_late/pallas_call | solution.py:482
  254.4 2.8 copy.35.grad_other
  257.2 8.6 %frames_back.1 = (bf16[750,1024]{1,0:T(8,128)(2,1)}, f32[2,16,1024]{2,1,0:T(8,128)}, f32[2,16,512]{2,1,0:T(8,128)}) custom-call(bf16[2,750,512]{2,1,0:T(8,128)(2,1)} %get-tuple-element.93.grad_mine, bf16[2,750,512]{2,1,0:T(8,128)(2,1)} %copy.35.grad_other, bf16[16,8,64,512]{3,2,1,0:T(8,128)(2,1)} %bitcast.82, ...), custom_call_target="tpu_custom_call" | custom-call | tf_op jit(solution)/shard_map/frames_back/pallas_call | solution.py:482
  268.8 5.7 %pack_early.1 = (f32[8,2,96,128]{3,2,1,0:T(8,128)}, f32[8,2,96,128]{3,2,1,0:T(8,128)}) custom-call(s32[3]{0:T(128)} %pad_add_fusion.where.refs_0_, f32[16,1024]{1,0:T(8,128)} %get-tuple-element.97.refs_1_, f32[16,1024]{1,0:T(8,128)} %get-tuple-element.146.refs_2_, f32[16,1024]{1,0:T(8,128)} %get-tuple-element.145.refs_3_, ...), custom_call_target="tpu_custom_call" | custom-call | tf_op jit(solution)/shard_map/pack_early/pallas_call | solution.py:482
  274.5 2.1 copy.37
  278.6 2.1 fusion.11
  282.6 3.4 all-to-all-start.1
  288.8 32.2 %collective-permute-done.12 = bf16[8,96,128]{2,1,0:T(8,128)(2,1)S(1)} collective-permute-done((bf16[8,96,128]{2,1,0:T(8,128)(2,1)S(1)}, bf16[8,96,128]{2,1,0:T(8,128)(2,1)S(1)}, u32[]{:S(2)}, u32[]{:S(2)}) %collective-permute-start.12) | collective-permute-done | bytes 196640 | tf_op jit(solution)/shard_map/ppermute | solution.py:49
  321.0 1.7 fusion.12
  322.7 3.4 all-to-all-start
  327.5 6.4 %all-to-all-done.early = bf16[8,96,128]{2,1,0:T(8,128)(2,1)S(1)} async-done(((bf16[8,96,128]{2,1,0:T(8,128)(2,1)}), bf16[8,96,128]{2,1,0:T(8,128)(2,1)S(1)}, u32[]{:S(2)}, u32[]{:S(2)}) %all-to-all-start) | async-done | bytes 196640 | tf_op jit(solution)/shard_map/all_to_all | solution.py:875
  334.5 2.3 unpack.1
  336.8 2.5 add_bitcast_fusion
  339.3 4.8 %copy.42 = f32[1,750,1024]{2,0,1:T(1,128)} copy(f32[1,750,1024]{2,1,0:T(8,128)S(1)} %add_bitcast_fusion) | data formatting | bytes 6144000
  (101 shorter events, 41.3 us)
Async XLA Ops:
  7.2 6.4 %copy-start = (bf16[8,8,16,1024]{3,2,1,0:T(8,128)(2,1)S(1)}, bf16[8,8,16,1024]{3,2,1,0:T(8,128)(2,1)}, u32[]{:S(2)}) copy-start(bf16[8,8,16,1024]{3,2,1,0:T(8,128)(2,1)} %param.24) | copy-start | bytes 6291460
  7.2 3.1 copy-start.20
  7.2 3.1 copy-start.19
  7.2 80.6 %all-gather.5.cloned.1.call-start = ((), (), s32[]{:S(2)}) async-start(), calls=%async_computation.2 | async-start | bytes 8912896 | tf_op jit(solution)/shard_map/all_gather | solution.py:533
  10.2 153.2 %all-gather.7.cloned.1.call-start = ((), (), s32[]{:S(2)}) async-start(), calls=%async_computation.3 | async-start | bytes 8912896 | tf_op jit(solution)/shard_map/all_gather | solution.py:534
  99.1 18.8 %collective-permute-start.2 = (bf16[2,750,512]{2,0,1:T(2,128)(2,1)}, bf16[2,750,512]{2,0,1:T(2,128)(2,1)}, u32[]{:S(2)}, u32[]{:S(2)}) collective-permute-start(bf16[2,750,512]{2,0,1:T(2,128)(2,1)} %copy.31), channel_id=1, source_target_pairs={{0,2},{2,0},{1,3},{3,1},{4,6},{6,4},{5,7},{7,5},{8,10},{10,8},{9,1... | collective-permute-start | bytes 4608008 | tf_op jit(solution)/shard_map/ppermute | solution.py:49
  105.0 3.3 collective-permute-start
  116.5 12.9 %collective-permute-start.1 = (bf16[224,1024]{1,0:T(8,128)(2,1)}, bf16[224,1024]{1,0:T(8,128)(2,1)S(1)}, u32[]{:S(2)}, u32[]{:S(2)}) collective-permute-start(bf16[224,1024]{1,0:T(8,128)(2,1)} %get-tuple-element.68.branch_mine), channel_id=1, source_target_pairs={{0,1},{1,0},{2,3},{3,2},{4,5},{5,4},{6,7},{7,6},{8,9},{9,8},{10,11... | collective-permute-start | bytes 1376264 | tf_op jit(solution)/shard_map/ppermute | solution.py:49
  143.7 19.8 %collective-permute-start.3 = (bf16[224,1024]{1,0:T(8,128)(2,1)}, bf16[224,1024]{1,0:T(8,128)(2,1)S(1)}, u32[]{:S(2)}, u32[]{:S(2)}) collective-permute-start(bf16[224,1024]{1,0:T(8,128)(2,1)} %get-tuple-element.71.branch_mine), channel_id=1, source_target_pairs={{0,1},{1,0},{2,3},{3,2},{4,5},{5,4},{6,7},{7,6},{8,9},{9,8},{10,11... | collective-permute-start | bytes 1376264 | tf_op jit(solution)/shard_map/ppermute | solution.py:49
  175.7 13.0 %collective-permute-start.5 = (bf16[224,1024]{1,0:T(8,128)(2,1)}, bf16[224,1024]{1,0:T(8,128)(2,1)S(1)}, u32[]{:S(2)}, u32[]{:S(2)}) collective-permute-start(bf16[224,1024]{1,0:T(8,128)(2,1)} %get-tuple-element.74.refs_3_), channel_id=1, source_target_pairs={{0,1},{1,0},{2,3},{3,2},{4,5},{5,4},{6,7},{7,6},{8,9},{9,8},{10,11... | collective-permute-start | bytes 1376264 | tf_op jit(solution)/shard_map/ppermute | solution.py:49
  207.6 3.2 copy-start.9
  207.6 4.7 %copy-start.2 = (bf16[1,224,1024]{2,1,0:T(8,128)(2,1)S(1)}, bf16[1,224,1024]{2,1,0:T(8,128)(2,1)}, u32[]{:S(2)}) copy-start(bf16[1,224,1024]{2,1,0:T(8,128)(2,1)} %param.15) | copy-start | bytes 1376260
  210.7 43.8 %collective-permute-start.9 = (bf16[2,750,512]{2,0,1:T(2,128)(2,1)S(1)}, bf16[2,750,512]{2,0,1:T(2,128)(2,1)}, u32[]{:S(2)}, u32[]{:S(2)}) collective-permute-start(bf16[2,750,512]{2,0,1:T(2,128)(2,1)S(1)} %copy.34), channel_id=1, source_target_pairs={{0,2},{2,0},{1,3},{3,1},{4,6},{6,4},{5,7},{7,5},{8,10},{10,8},{9,1... | collective-permute-start | bytes 4608008 | tf_op jit(solution)/shard_map/ppermute | solution.py:49
  210.7 12.9 %collective-permute-start.6 = (bf16[224,1024]{1,0:T(8,128)(2,1)S(1)}, bf16[224,1024]{1,0:T(8,128)(2,1)S(1)}, u32[]{:S(2)}, u32[]{:S(2)}) collective-permute-start(bf16[224,1024]{1,0:T(8,128)(2,1)S(1)} %copy-done.9), channel_id=1, source_target_pairs={{0,1},{1,0},{2,3},{3,2},{4,5},{5,4},{6,7},{7,6},{8,9},{9,8},{10,11... | collective-permute-start | bytes 1376264 | tf_op jit(solution)/shard_map/ppermute | solution.py:49
  236.4 2.6 collective-permute-start.7
  237.5 41.1 %collective-permute-start.4 = (bf16[224,1024]{1,0:T(8,128)(2,1)}, bf16[224,1024]{1,0:T(8,128)(2,1)}, u32[]{:S(2)}, u32[]{:S(2)}) collective-permute-start(bf16[224,1024]{1,0:T(8,128)(2,1)} %get-tuple-element.73), channel_id=1, source_target_pairs={{0,1},{1,0},{2,3},{3,2},{4,5},{5,4},{6,7},{7,6},{8,9},{9,8},{10,11... | collective-permute-start | bytes 1376264 | tf_op jit(solution)/shard_map/ppermute | solution.py:49
  253.3 23.4 %collective-permute-start.13 = (f32[8,2,32,128]{3,2,0,1:T(8,128)S(1)}, f32[8,2,32,128]{3,2,0,1:T(8,128)S(1)}, u32[]{:S(2)}, u32[]{:S(2)}) collective-permute-start(f32[8,2,32,128]{3,2,0,1:T(8,128)S(1)} %copy.40), channel_id=1, source_target_pairs={{0,2},{2,0},{1,3},{3,1},{4,6},{6,4},{5,7},{7,5},{8,10},{10,8},{9,1... | collective-permute-start | bytes 786440 | tf_op jit(solution)/shard_map/ppermute | solution.py:49
  253.5 32.4 %collective-permute-start.8 = (bf16[224,1024]{1,0:T(8,128)(2,1)}, bf16[224,1024]{1,0:T(8,128)(2,1)S(1)}, u32[]{:S(2)}, u32[]{:S(2)}) collective-permute-start(bf16[224,1024]{1,0:T(8,128)(2,1)} %get-tuple-element.92), channel_id=1, source_target_pairs={{0,1},{1,0},{2,3},{3,2},{4,5},{5,4},{6,7},{7,6},{8,9},{9,8},{10,11... | collective-permute-start | bytes 1376264 | tf_op jit(solution)/shard_map/ppermute | solution.py:49
  265.8 11.7 %copy-start.15 = (f32[8,2,32,128]{3,2,1,0:T(8,128)S(1)}, f32[8,2,32,128]{3,2,1,0:T(8,128)}, u32[]{:S(2)}) copy-start(f32[8,2,32,128]{3,2,1,0:T(8,128)} %get-tuple-element.115) | copy-start | bytes 786436
  265.8 12.9 %copy-start.3 = (f32[224,1024]{1,0:T(8,128)S(1)}, f32[224,1024]{1,0:T(8,128)}, u32[]{:S(2)}) copy-start(f32[224,1024]{1,0:T(8,128)} %get-tuple-element.72.refs_1_) | copy-start | bytes 2752516
  276.6 9.8 %collective-permute-start.11 = (f32[8,2,96,128]{3,2,0,1:T(8,128)}, f32[8,2,96,128]{3,2,0,1:T(8,128)}, u32[]{:S(2)}, u32[]{:S(2)}) collective-permute-start(f32[8,2,96,128]{3,2,0,1:T(8,128)} %copy.37), channel_id=1, source_target_pairs={{0,2},{2,0},{1,3},{3,1},{4,6},{6,4},{5,7},{7,5},{8,10},{10,8},{9,1... | collective-permute-start | bytes 2359304 | tf_op jit(solution)/shard_map/ppermute | solution.py:49
  277.4 8.6 %copy-start.4 = (bf16[224,1024]{1,0:T(8,128)(2,1)S(1)}, bf16[224,1024]{1,0:T(8,128)(2,1)}, u32[]{:S(2)}) copy-start(bf16[224,1024]{1,0:T(8,128)(2,1)} %get-tuple-element.92) | copy-start | bytes 1376260
  277.4 4.5 %copy-start.17 = (f32[8,2,32,128]{3,2,0,1:T(8,128)S(1)}, f32[8,2,32,128]{3,2,0,1:T(8,128)}, u32[]{:S(2)}) copy-start(f32[8,2,32,128]{3,2,0,1:T(8,128)} %copy-done.16) | copy-start | bytes 786436
  277.5 8.9 %copy-start.7 = (f32[8,2,96,128]{3,2,1,0:T(8,128)S(1)}, f32[8,2,96,128]{3,2,1,0:T(8,128)}, u32[]{:S(2)}) copy-start(f32[8,2,96,128]{3,2,1,0:T(8,128)} %get-tuple-element.107) | copy-start | bytes 2359300
  277.5 4.5 %collective-permute-start.14 = (bf16[8,32,128]{2,1,0:T(8,128)(2,1)S(1)}, bf16[8,32,128]{2,1,0:T(8,128)(2,1)S(1)}, u32[]{:S(2)}, u32[]{:S(2)}) collective-permute-start(bf16[8,32,128]{2,1,0:T(8,128)(2,1)S(1)} %fusion.15), channel_id=1, source_target_pairs={{0,1},{1,0},{2,3},{3,2},{4,5},{5,4},{6,7},{7,6},{8,9},{9,8},{10,11... | collective-permute-start | bytes 196616 | tf_op jit(solution)/shard_map/ppermute | solution.py:49
  280.8 56.0 %collective-permute-start.10 = (bf16[750,1024]{1,0:T(8,128)(2,1)}, bf16[750,1024]{1,0:T(8,128)(2,1)}, u32[]{:S(2)}, u32[]{:S(2)}) collective-permute-start(bf16[750,1024]{1,0:T(8,128)(2,1)} %get-tuple-element.96), channel_id=1, source_target_pairs={{0,1},{1,0},{2,3},{3,2},{4,5},{5,4},{6,7},{7,6},{8,9},{9,8},{10,11... | collective-permute-start | bytes 4608008 | tf_op jit(solution)/shard_map/ppermute | solution.py:49
  282.6 40.1 %all-to-all-start.1 = ((bf16[8,32,128]{2,1,0:T(8,128)(2,1)}), bf16[8,32,128]{2,1,0:T(8,128)(2,1)S(1)}, u32[]{:S(2)}, u32[]{:S(2)}) async-start(bf16[8,32,128]{2,1,0:T(8,128)(2,1)} %fusion.14), calls=%async_computation.1 | async-start | bytes 131072 | tf_op jit(solution)/shard_map/all_to_all | solution.py:875
  286.4 39.8 %copy-start.6 = (f32[224,1024]{1,0:T(8,128)S(1)}, f32[224,1024]{1,0:T(8,128)}, u32[]{:S(2)}) copy-start(f32[224,1024]{1,0:T(8,128)} %get-tuple-element.88) | copy-start | bytes 2752516
  287.5 33.5 %collective-permute-start.12 = (bf16[8,96,128]{2,1,0:T(8,128)(2,1)S(1)}, bf16[8,96,128]{2,1,0:T(8,128)(2,1)S(1)}, u32[]{:S(2)}, u32[]{:S(2)}) collective-permute-start(bf16[8,96,128]{2,1,0:T(8,128)(2,1)S(1)} %fusion.13), channel_id=1, source_target_pairs={{0,1},{1,0},{2,3},{3,2},{4,5},{5,4},{6,7},{7,6},{8,9},{9,8},{10,11... | collective-permute-start | bytes 589832 | tf_op jit(solution)/shard_map/ppermute | solution.py:49
  322.7 4.8 %copy-start.18 = (bf16[8,32,128]{2,1,0:T(8,128)(2,1)}, bf16[8,32,128]{2,1,0:T(8,128)(2,1)S(1)}, u32[]{:S(2)}) copy-start(bf16[8,32,128]{2,1,0:T(8,128)(2,1)S(1)} %all-to-all-done.1.late) | copy-start | bytes 196612
  322.7 11.1 %all-to-all-start = ((bf16[8,96,128]{2,1,0:T(8,128)(2,1)}), bf16[8,96,128]{2,1,0:T(8,128)(2,1)S(1)}, u32[]{:S(2)}, u32[]{:S(2)}) async-start(bf16[8,96,128]{2,1,0:T(8,128)(2,1)} %fusion.12), calls=%async_computation | async-start | bytes 393216 | tf_op jit(solution)/shard_map/all_to_all | solution.py:875
  339.3 4.8 %copy-start.1 = (bf16[8,8,16,1024]{3,2,1,0:T(8,128)(2,1)S(1)}, bf16[8,8,16,1024]{3,2,1,0:T(8,128)(2,1)}, u32[]{:S(2)}) copy-start(bf16[8,8,16,1024]{3,2,1,0:T(8,128)(2,1)} %param.24) | copy-start | bytes 6291460
  (8 other events, 6.0 us)
Sparse Core Ops, SparseCore 0:
  10.8 77.0 all-gather.4
  90.5 72.8 all-gather.6
where the time goes:
time: 352 us; the launch traced here: 351 us
  waiting for transfers between devices  158 us (45%)
  Pallas kernels  101 us (29%)
  local copies, waits for them, and re-layouts  44.8 us (13%)
  starting transfers between devices  19.7 us (6%)
  between operations  15 us (4%)
  other arithmetic  12.6 us (4%)
    pallas_call x12, Pallas kernels, call(): return run(*arrays) if scalars is None else run(scalars, *arrays)  101 us
    all_gather x1, waiting for transfers between devices, on_device(): attn_full = lax.all_gather(attn_half, ('fsdp', 'ctx'), axis=0)  73.5 us
    ppermute x15, waiting for transfers between devices, swap(): return lax.ppermute(value, axis, [(0, 1), (1, 0)])  62.3 us
    all_gather x1, waiting for transfers between devices, on_device(): ff_full = lax.all_gather(ff_half, ('fsdp', 'ctx'), axis=0)  15.3 us
    ppermute x15, starting transfers between devices, swap(): return lax.ppermute(value, axis, [(0, 1), (1, 0)])  12.9 us
    unnamed x43, local copies, waits for them, and re-layouts  10.9 us
    pallas_call x4, local copies, waits for them, and re-layouts, call(): return run(*arrays) if scalars is None else run(scalars, *arrays)  10.3 us
  transfers between devices with their start and end apart: 19, of which 8 were waited for; matrix products, arithmetic and copies ran while one was open for 11% of the time, Pallas kernels for 20%

commit v1 on v0

--- a/solution.py
+++ b/solution.py
@@ -1,3 +1,5 @@
+from functools import partial
+
 import jax
 import jax.numpy as jnp
 from jax import lax
@@ -163,7 +165,11 @@
     rows = frames[...]
     rank_rows = mm_nt(rows, low_in[0]).astype(BF)
     low[0] = rank_rows
-    key_value[0] = (mm(rows, matrix(weight)) + mm(rank_rows, low_out[0])).astype(BF)
+    count = rows.shape[0]
+    key_value[0, :count] = (mm(rows, matrix(weight)) + mm(rank_rows, low_out[0])).astype(BF)
+    spare = key_value.shape[1] - count
+    if spare:
+        key_value[0, count:] = jnp.zeros((spare, key_value.shape[2]), BF)
 
 
 def self_kernel(
@@ -192,6 +198,7 @@
 
 
 def cross_kernel(
+    count,
     hidden, branch_mine, branch_other, gains, query_weight, query_in, query_out, mine, other,
     weight, low_in, low_out,
     middle, normed, query, query_low, mixed, logsum, branch, low, acc, low_acc,
@@ -212,7 +219,12 @@
         mm(normed[...], matrix(query_weight)) + mm(query_low[...], query_out[0])
     ).astype(BF)
     query[...] = queries
-    out, logs = pair_forward(queries, (mine[0], other[0]), (mine[1], other[1]), no_limit)
+    out, logs = pair_forward(
+        queries,
+        (mine[0, :count], other[0, :count]),
+        (mine[1, :count], other[1, :count]),
+        no_limit,
+    )
     out = out.astype(BF)
     mixed[...] = out
     logsum[0, 0:1, :] = logs[0]
@@ -271,7 +283,7 @@
 
 
 def attention_back(
-    limit, slot, carried, rows, gains, grad_mine, grad_other, weight, low_in, low_out,
+    limit, slot, count, carried, rows, gains, grad_mine, grad_other, weight, low_in, low_out,
     query_weight, query_in, query_out, query, mixed, mine, other, logsum, normed, query_low, low,
     carry, grad_normed, grad_kv, grad_kv_other,
     table_in, table_out, table_query_in, table_query_out,
@@ -296,16 +308,21 @@
     grad_query, grad_keys, grad_values = pair_backward(
         grad,
         query[...],
-        (mine[0], other[0]),
-        (mine[1], other[1]),
+        (mine[0, :count], other[0, :count]),
+        (mine[1, :count], other[1, :count]),
         (logsum[0, 0:1, :], logsum[0, 1:2, :]),
         limit,
     )
-    grad_kv[0], grad_kv_other[0] = grad_keys
-    grad_kv[1], grad_kv_other[1] = grad_values
+    for which, (first, second) in enumerate((grad_keys, grad_values)):
+        grad_kv[which, :count] = first
+        grad_kv_other[which, :count] = second
+        spare = grad_kv.shape[1] - count
+        if spare:
+            grad_kv[which, count:] = jnp.zeros((spare, PAIR), BF)
+            grad_kv_other[which, count:] = jnp.zeros((spare, PAIR), BF)
     acc[...] += mm_nt(grad_query, matrix(query_weight))
     query_back[...] += mm_nt(grad_query, query_out[0])
-    table_query_out[...] = mm_tn(query_low[...], grad_query)
+    table_query_out[...] = mm_tn(query_low[0], grad_query)
 
     @at_last()
     def _():
@@ -315,12 +332,8 @@
         table_query_in[...] = mm_tn(rank_rows, normed[...])
 
 
-def cross_back_kernel(*refs):
-    attention_back(no_limit, 2, *refs)
-
-
-def self_back_kernel(where, *refs):
-    attention_back(causal_limit(where[0]), 1, *refs)
+def self_back_kernel(count, where, *refs):
+    attention_back(causal_limit(where[0]), 1, count, *refs)
 
 
 def pair_project_kernel(
@@ -332,35 +345,50 @@
         acc[...] = start[...]
 
     pair_project_step(
-        grad_mine, grad_other, weight, low_in, low_out, rows, low, total, table_in, table_out, acc
-    )
+        grad_mine, grad_other, weight, low_in, low_out, rows, low, table_in, table_out, acc
+    )
+
+    @at_last()
+    def _():
+        total[...] = acc[...].astype(BF)
+
+
+def add_rows_kernel(top, top_other, low, low_other, total):
+    count = top.shape[0]
+    first = top[...].astype(F32) + top_other[...].astype(F32)
+    second = low[...].astype(F32) + low_other[...].astype(F32)
+    total[:count] = first[:, None, :]
+    total[count:] = second[:, None, :]
 
 
 def frames_back_kernel(
-    grad_mine, grad_other, weight, low_in, low_out, rows, low, total, table_in, table_out, acc
+    grad_mine, grad_other, weight, low_in, low_out, rows, low, top, rest, table_in, table_out, acc
 ):
     @at_first()
     def _():
         acc[...] = jnp.zeros_like(acc)
 
     pair_project_step(
-        grad_mine, grad_other, weight, low_in, low_out, rows, low, total, table_in, table_out, acc
-    )
+        grad_mine, grad_other, weight, low_in, low_out, rows, low, table_in, table_out, acc
+    )
+
+    @at_last()
+    def _():
+        count = top.shape[0]
+        top[...] = acc[:count].astype(BF)
+        rest[...] = acc[count:].astype(BF)
 
 
 def pair_project_step(
-    grad_mine, grad_other, weight, low_in, low_out, rows, low, total, table_in, table_out, acc
+    grad_mine, grad_other, weight, low_in, low_out, rows, low, table_in, table_out, acc
 ):
-    grad = (grad_mine[0].astype(F32) + grad_other[0].astype(F32)).astype(BF)
+    count = rows.shape[0]
+    grad = (grad_mine[0, :count].astype(F32) + grad_other[0, :count].astype(F32)).astype(BF)
     rank_rows = mm_nt(grad, low_out[0]).astype(BF)
     acc[...] += mm_nt(grad, matrix(weight)) + mm(rank_rows, low_in[0])
     table_in[0] = mm_tn(rank_rows, rows[...])
     table_out[0] = mm_tn(low[0], grad)
 
-    @at_last()
-    def _():
-        total[...] = acc[...].astype(BF)
-
 
 LANE = 128
 PIECE = 32
@@ -368,11 +396,13 @@
 
 def pack_kernel(fulls, shares, wides, order, tagged, *refs):
     where = refs[0]
-    tables = refs[1 : 1 + fulls + shares]
-    broad = refs[1 + fulls + shares : 1 + fulls + shares + wides]
-    keep, send = refs[1 + fulls + shares + wides :]
+    keep, send = refs[-2:]
+    flat = []
+    for ref in refs[1:-2]:
+        flat += [ref] if len(ref.shape) == 2 else [ref.at[i] for i in range(ref.shape[0])]
+    tables, broad = flat[: fulls + shares], flat[fulls + shares :]
     context, tensor = where[0], where[1]
-    blocks = keep.shape[0]
+    blocks = keep.shape[1]
     per_group = (len(order) + 3) // 4
     rows = per_group * 16
     lane = lax.broadcasted_iota(jnp.int32, (rows, LANE), 1) // PIECE
@@ -411,11 +441,11 @@
 
             @pl.when(context == p // 2)
             def _(whole=whole, f=f, p=p):
-                keep[f, p % 2] = whole
+                keep[p % 2, f] = whole
 
             @pl.when(context != p // 2)
             def _(whole=whole, f=f, p=p):
-                send[f, p % 2] = whole
+                send[p % 2, f] = whole
 
 
 def unpack_kernel(early, late, attn_in, attn_out, up_in, up_out, down_in, down_out):
@@ -463,7 +493,7 @@
     return pl.BlockSpec(dims, lambda *_: zeros)
 
 
-def call(kernel, steps, ins, outs, scratch=(), scalars=None, name=None):
+def call(kernel, steps, ins, outs, scratch=(), scalars=None, name=None, cost=5):
     arrays = [a for a, _ in ins]
     spec = pltpu.PrefetchScalarGridSpec(
         num_scalar_prefetch=0 if scalars is None else 1,
@@ -477,6 +507,9 @@
         grid_spec=spec,
         out_shape=[o for o, _ in outs],
         compiler_params=pltpu.CompilerParams(dimension_semantics=("arbitrary",)),
+        cost_estimate=pl.CostEstimate(
+            flops=cost * 1_000_000_000, transcendentals=0, bytes_accessed=cost * 3_690_000
+        ),
         name=name,
     )
     return run(*arrays) if scalars is None else run(scalars, *arrays)
@@ -507,6 +540,7 @@
     hidden, encoder, cotangent = hidden[0], encoder[0], cotangent[0]
     rows, width = hidden.shape
     frames = encoder.shape[0]
+    padded = -(-frames // 16) * 16
     wide = up_adapt_out.shape[2]
     cols = attn_in_weight.shape[2]
     units = up_weight.shape[1]
@@ -569,6 +603,9 @@
     def at(array, first=0):
         return array, pl.BlockSpec((1,) + array.shape[1:], lambda i, *_: (first + i, 0, 0))
 
+    def at_slot(array):
+        return array, pl.BlockSpec((1,) + array.shape[1:], lambda i, *_: (0, 0, 0))
+
     logsum_out = (
         shape((pairs, 2, rows), F32),
         pl.BlockSpec((1, 2, rows), lambda p, *_: (p, 0, 0)),
@@ -617,8 +654,8 @@
         ],
         [
             (
-                shape((2, frames, cols), BF),
-                pl.BlockSpec((1, frames, cols), lambda i: (i, 0, 0)),
+                shape((2, padded, cols), BF),
+                pl.BlockSpec((1, padded, cols), lambda i: (i, 0, 0)),
             ),
             (
                 shape((2, frames, rank), BF),
@@ -626,6 +663,7 @@
             ),
         ],
         name="frames",
+        cost=7,
     )
     cross_kv_other = swap(cross_kv, "ctx")
     self_mixed, self_logsum, branch, self_o_low = call(
@@ -643,10 +681,11 @@
         [wide_acc, rank_acc],
         scalars,
         name="self_attention",
+        cost=7,
     )
     branch, branch_other = with_other(branch, "tp")
     first_mid, n2, cross_q, cross_q_low, cross_mixed, cross_logsum, branch, cross_o_low = call(
-        cross_kernel,
+        partial(cross_kernel, frames),
         pairs,
         [
             whole(hidden),
@@ -674,6 +713,7 @@
         ],
         [wide_acc, rank_acc],
         name="cross_attention",
+        cost=13,
     )
     branch, branch_other = with_other(branch, "tp")
     chunk = min(units, 512)
@@ -719,16 +759,14 @@
             rank_acc,
         ],
         name="units",
+        cost=11,
     )
     grad_n3, grad_n3_other = with_other(grad_n3, "tp")
     branch, branch_other = with_other(branch, "tp")
-    layer_out = (
-        second_mid + (branch.astype(F32) + branch_other.astype(F32))
-    ).astype(BF)
 
     def back_call(
         kernel, scalar, carried, middle, grad, grad_other, slots, queries, mixed, kv, kv_other,
-        logsum, normed, query_low, low, kind, name,
+        logsum, normed, query_low, low, kind, name, cost,
     ):
         weight_slot, low_slot, query_slot, query_low_slot = slots
         count = kv.shape[1]
@@ -757,7 +795,7 @@
                 kv_pair(kv_other),
                 logsum_in(logsum),
                 whole(normed),
-                whole(query_low),
+                at_slot(query_low),
                 whole(low),
             ],
             [
@@ -773,16 +811,22 @@
             [pltpu.VMEM((rows, width), BF), rank_keep, wide_acc, rank_acc],
             scalar,
             name=name,
+            cost=cost,
         )
 
     grad_second, grad_n2, grad_ckv, grad_ckv_send, co_in_t, co_out_t, cq_in_t, cq_out_t = back_call(
-        cross_back_kernel, None, cotangent, second_mid, grad_n3, grad_n3_other, (7, 7, 3, 4),
-        cross_q, cross_mixed, cross_kv, cross_kv_other, cross_logsum, n2, cross_q_low,
-        cross_o_low, BF, "cross_back",
+        partial(attention_back, no_limit, 2, frames), None, cotangent, second_mid, grad_n3, grad_n3_other, (7, 7, 3, 4),
+        cross_q, cross_mixed, cross_kv, cross_kv_other, cross_logsum, n2, cross_q_low[None],
+        cross_o_low, BF, "cross_back", 18,
     )
     grad_n2, grad_n2_other = with_other(grad_n2, "tp")
     grad_ckv_other = swap(grad_ckv_send, "ctx")
-    grad_frames, ckv_in_t, ckv_out_t = call(
+    grad_ckv_other, branch_other = lax.optimization_barrier((grad_ckv_other, branch_other))
+    layer_out = (
+        second_mid + (branch.astype(F32) + branch_other.astype(F32))
+    ).astype(BF)
+    first_half = padded // 2
+    grad_top, grad_low, ckv_in_t, ckv_out_t = call(
         frames_back_kernel,
         2,
         [
@@ -795,21 +839,27 @@
             at(frames_low),
         ],
         [
-            out((frames, width), BF),
+            out((first_half, width), BF),
+            out((frames - first_half, width), BF),
             at(shape((2, rank, width), F32)),
             at(shape((2, rank, cols), F32)),
         ],
         [pltpu.VMEM((frames, width), F32)],
         name="frames_back",
-    )
-    grad_frames, grad_frames_other = with_other(grad_frames, "tp")
-    grad_encoder = grad_frames.astype(F32) + grad_frames_other.astype(F32)
+        cost=9,
+    )
+    grad_top, grad_low, grad_n2_other = lax.optimization_barrier(
+        (grad_top, grad_low, grad_n2_other)
+    )
+    grad_top, grad_top_other = with_other(grad_top, "tp")
+    grad_low, grad_low_other = with_other(grad_low, "tp")
     grad_first, grad_n1_start, grad_skv, grad_skv_send, so_in_t, so_out_t, q_in_t, q_out_t = back_call(
-        self_back_kernel, scalars, grad_second, first_mid, grad_n2, grad_n2_other, (6, 3, 0, 0),
-        query, self_mixed, self_kv, self_kv_other, self_logsum, n1, self_low[0],
-        self_o_low, F32, "self_back",
+        partial(self_back_kernel, rows), scalars, grad_second, first_mid, grad_n2, grad_n2_other, (6, 3, 0, 0),
+        query, self_mixed, self_kv, self_kv_other, self_logsum, n1, self_low,
+        self_o_low, F32, "self_back", 12,
     )
     grad_skv_other = swap(grad_skv_send, "ctx")
+    grad_skv_other, grad_top_other = lax.optimization_barrier((grad_skv_other, grad_top_other))
     grad_n1, kv_in_t, kv_out_t = call(
         pair_project_kernel,
         2,
@@ -832,14 +882,21 @@
         name="self_project_back",
     )
     grad_n1, grad_n1_other = with_other(grad_n1, "tp")
+    grad_encoder = call(
+        add_rows_kernel,
+        1,
+        [whole(grad_top), whole(grad_top_other), whole(grad_low), whole(grad_low_other)],
+        [out((frames, 1, width), F32)],
+        name="encoder_total",
+    )[0].reshape(frames, width)
     grad_hidden = grad_first + normalize_back(
         hidden.astype(F32), ln_gains[0], grad_n1.astype(F32) + grad_n1_other.astype(F32)
     )
 
-    early_full = [cq_in_t, ckv_in_t[0], ckv_in_t[1], co_out_t, up_in_t, down_out_t]
-    early_part = [co_in_t, cq_out_t, ckv_out_t[0], ckv_out_t[1]]
-    late_full = [q_in_t, kv_in_t[0], kv_in_t[1], so_out_t]
-    late_part = [so_in_t, q_out_t, kv_out_t[0], kv_out_t[1]]
+    early_full = [cq_in_t, ckv_in_t, co_out_t, up_in_t, down_out_t]
+    early_part = [co_in_t, cq_out_t, ckv_out_t]
+    late_full = [q_in_t, kv_in_t, so_out_t]
+    late_part = [so_in_t, q_out_t, kv_out_t]
     broad = [up_out_t, down_in_t]
     regular = (
         ctx_size == 2 and tp_size == 2 and rank == 16
@@ -850,10 +907,13 @@
         def exchange(full, part, wides, order, tagged, name):
             per_group = (len(order) + 3) // 4
             count = 16 * (per_group + len(wides) + tagged)
-            dims = (fsdp_size, 2, count, LANE)
+            dims = (2, fsdp_size, count, LANE)
+
+            def number(arrays):
+                return sum(1 if a.ndim == 2 else a.shape[0] for a in arrays)
 
             def kernel(*refs):
-                pack_kernel(len(full), len(part), len(wides), order, tagged, *refs)
+                pack_kernel(number(full), number(part), len(wides), order, tagged, *refs)
 
             keep, send = call(
                 kernel,
@@ -866,8 +926,8 @@
             recv = swap(send, "ctx")
 
             def pick(i):
-                return lax.dynamic_index_in_dim(keep, i, 1, keepdims=False) + (
-                    lax.dynamic_index_in_dim(recv, i, 1, keepdims=False)
+                return lax.dynamic_index_in_dim(keep, i, 0, keepdims=False) + (
+                    lax.dynamic_index_in_dim(recv, i, 0, keepdims=False)
                 )
 
             away = swap(pick(1 - tensor_index).astype(BF), "tp")
@@ -897,6 +957,8 @@
         chosen = (mine == jnp.arange(adapters, dtype=jnp.int32)).astype(F32)
 
         def summed(parts, start, full):
+            parts = [t for p in parts for t in ([p] if p.ndim == 2 else [p[0], p[1]])]
+
             def spread_out(part):
                 if part.shape[1] == full:
                     return part
@@ -910,7 +972,7 @@
             )
 
         attn_in_t = summed(
-            late_full[:3] + [so_in_t] + early_full[:3] + [co_in_t], head_start, width
+            late_full[:2] + [so_in_t] + early_full[:2] + [co_in_t], head_start, width
         )
         attn_out_t = summed(
             late_part[1:] + [so_out_t] + early_part[1:] + [co_out_t], head_start, width

time: 352 us -> 321 us (0.912)
  local copies, waits for them, and re-layouts: 44.8 us -> 16.4 us
  Pallas kernels: 101 us -> 106 us
  waiting for transfers between devices: 158 us -> 153 us
    ppermute x15 -> x16, waiting for transfers between devices: 62.3 us -> 46.7 us  [swap(): return lax.ppermute(value, axis, [(0, 1), (1, 0)])]
    pallas_call x4 -> x0, local copies, waits for them, and re-layouts: 10.3 us -> none  [call(): return run(*arrays) if scalars is None else run(scalars, *arrays)]
    squeeze x5 -> x0, local copies, waits for them, and re-layouts: 7.4 us -> none  [the longest x1 1.53 us: on_device(): ckv_in_t[1]]
    all_to_all x2, waiting for transfers between devices: 6.37 us -> 12.8 us  [exchange(): return lax.all_to_all(total, 'fsdp', 0, 0, tiled=True)]
    ppermute x2 -> x0, local copies, waits for them, and re-layouts: 5.57 us -> none  [swap(): return lax.ppermute(value, axis, [(0, 1), (1, 0)])]
    unnamed x43 -> x42, local copies, waits for them, and re-layouts: 10.9 us -> 5.72 us
    pallas_call x12 -> x13, Pallas kernels: 101 us -> 106 us  [call(): return run(*arrays) if scalars is None else run(scalars, *arrays)]
    all_gather x1, waiting for transfers between devices: 15.3 us -> 19.6 us  [on_device(): ff_full = lax.all_gather(ff_half, ('fsdp', 'ctx'), axis=0)]
  transfers between devices with their start and end apart: 19 -> 20, of which waited for: 8 -> 9; matrix products, arithmetic and copies ran while one was open for 11% -> 5% of each run, Pallas kernels for 20% -> 23%
where the time goes in v1:
time: 321 us; the launch traced here: 320 us
  waiting for transfers between devices  153 us (48%)
  Pallas kernels  106 us (33%)
  starting transfers between devices  19.9 us (6%)
  local copies, waits for them, and re-layouts  16.4 us (5%)
  between operations  15 us (5%)
  other arithmetic  9.84 us (3%)
    pallas_call x13, Pallas kernels, call(): return run(*arrays) if scalars is None else run(scalars, *arrays)  106 us
    all_gather x1, waiting for transfers between devices, on_device(): attn_full = lax.all_gather(attn_half, ('fsdp', 'ctx'), axis=0)  73.5 us
    ppermute x16, waiting for transfers between devices, swap(): return lax.ppermute(value, axis, [(0, 1), (1, 0)])  46.7 us
    all_gather x1, waiting for transfers between devices, on_device(): ff_full = lax.all_gather(ff_half, ('fsdp', 'ctx'), axis=0)  19.6 us
    ppermute x16, starting transfers between devices, swap(): return lax.ppermute(value, axis, [(0, 1), (1, 0)])  13.1 us
    all_to_all x2, waiting for transfers between devices, exchange(): return lax.all_to_all(total, 'fsdp', 0, 0, tiled=True)  12.8 us
    all_to_all x2, starting transfers between devices, exchange(): return lax.all_to_all(total, 'fsdp', 0, 0, tiled=True)  6.74 us
  transfers between devices with their start and end apart: 20, of which 9 were waited for; matrix products, arithmetic and copies ran while one was open for 5% of the time, Pallas kernels for 23%

profile of v1, /device:TPU:0, one launch (start us, length us, event | category | flops | bytes accessed | tf_op | source)
XLA Modules:
  0.0 319.7 jit_solution(8829610687230260049)
XLA Ops:
  11.9 1.7 dynamic-slice_bitcast_fusion.5.low_out.query_out.refs_10_
  14.3 73.5 %all-gather.5.cloned.1.call-done = bf16[128,64,512]{2,1,0:T(8,128)(2,1)} async-done(((bf16[8,64,512]{2,1,0:T(8,128)(2,1)}), bf16[128,64,512]{2,1,0:T(8,128)(2,1)}) %all-gather.5.cloned.1.call-update) | async-done | bytes 8388624 | tf_op jit(solution)/shard_map/all_gather | solution.py:567
  87.8 5.7 %qkv.1 = (bf16[224,1024]{1,0:T(8,128)(2,1)}, bf16[224,512]{1,0:T(8,128)(2,1)}, bf16[2,224,512]{2,1,0:T(8,128)(2,1)}, bf16[3,224,16]{2,1,0:T(8,128)(2,1)}) custom-call(bf16[224,1024]{1,0:T(8,128)(2,1)} %bitcast.54, f32[3,1024]{1,0:T(4,128)} %refs_2_.1, bf16[16,8,64,512]{3,2,1,0:T(8,128)(2,1)} %bitcast.58, ...), custom_call_target="tpu_custom_call" | custom-call | flops 5000000000 | bytes 18450000 | tf_op jit(solution)/shard_map/qkv/pallas_call | solution.py:515
  93.7 7.1 %frames.1 = (bf16[2,752,512]{2,1,0:T(8,128)(2,1)}, bf16[2,750,16]{2,1,0:T(8,128)(2,1)}) custom-call(bf16[750,1024]{1,0:T(8,128)(2,1)} %bitcast.71, bf16[16,8,64,512]{3,2,1,0:T(8,128)(2,1)} %bitcast.59, bf16[8,16,1024]{2,1,0:T(8,128)(2,1)} %dynamic-slice_bitcast_fusion.3.low_in.query_in.refs_9_, ...), custom_call_target="tpu_custom_call" | custom-call | flops 7000000000 | bytes 25830000 | tf_op jit(solution)/shard_map/frames/pallas_call | solution.py:515
  102.5 1.7 dynamic-slice_bitcast_fusion.2.low_out.refs_7_
  104.9 7.3 %self_attention.1 = (bf16[224,512]{1,0:T(8,128)(2,1)}, f32[4,2,224]{2,1,0:T(2,128)}, bf16[224,1024]{1,0:T(8,128)(2,1)}, bf16[224,16]{1,0:T(8,128)(2,1)}) custom-call(s32[3]{0:T(128)} %pad_add_fusion.where.refs_0_, bf16[224,512]{1,0:T(8,128)(2,1)} %get-tuple-element.74.query.refs_11_, bf16[2,224,512]{2,1,0:T(8,128)(2,1)} %get-tuple-element.75.mine.refs_13_, ...), custom_call_target="tpu_custom_call" | custom-call | flops 7000000000 | bytes 25830000 | tf_op jit(solution)/shard_map/self_attention/pallas_call | solution.py:515
  112.2 1.5 collective-permute-start.1
  113.8 11.4 %collective-permute-done.1.branch_other = bf16[224,1024]{1,0:T(8,128)(2,1)S(1)} collective-permute-done((bf16[224,1024]{1,0:T(8,128)(2,1)}, bf16[224,1024]{1,0:T(8,128)(2,1)S(1)}, u32[]{:S(2)}, u32[]{:S(2)}) %collective-permute-start.1) | collective-permute-done | bytes 458784 | tf_op jit(solution)/shard_map/ppermute | solution.py:51
  126.0 13.4 %cross_attention.1 = (f32[224,1024]{1,0:T(8,128)}, bf16[224,1024]{1,0:T(8,128)(2,1)}, bf16[224,512]{1,0:T(8,128)(2,1)}, bf16[224,16]{1,0:T(8,128)(2,1)}, bf16[22...) custom-call(bf16[224,1024]{1,0:T(8,128)(2,1)} %bitcast.55, ...), custom_call_target="tpu_custom_call" | custom-call | flops 12999999488 | bytes 47970000 | tf_op jit(solution)/shard_map/cross_attention/pallas_call | solution.py:515
  139.4 1.5 collective-permute-start.3
  142.4 1.5 dynamic-slice_bitcast_fusion.6
  143.9 19.6 %all-gather.7.cloned.1.call-done = bf16[32,64,2048]{2,1,0:T(8,128)(2,1)} async-done(((bf16[2,64,2048]{2,1,0:T(8,128)(2,1)}), bf16[32,64,2048]{2,1,0:T(8,128)(2,1)}) %all-gather.7.cloned.1.call-update) | async-done | bytes 8388624 | tf_op jit(solution)/shard_map/all_gather | solution.py:568
  164.2 11.5 %units.1 = (f32[224,1024]{1,0:T(8,128)}, bf16[224,1024]{1,0:T(8,128)(2,1)}, bf16[224,1024]{1,0:T(8,128)(2,1)}, f32[16,1024]{1,0:T(8,128)}, f32[16,2048]{1,0:T(8,...) custom-call(f32[224,1024]{1,0:T(8,128)} %get-tuple-element.78.middle.refs_1_, ...), custom_call_target="tpu_custom_call" | custom-call | flops 11000000512 | bytes 40590000 | tf_op jit(solution)/shard_map/units/pallas_call | solution.py:515
  175.8 1.6 collective-permute-start.4
  177.3 11.4 %collective-permute-done.4.grad_other = bf16[224,1024]{1,0:T(8,128)(2,1)S(1)} collective-permute-done((bf16[224,1024]{1,0:T(8,128)(2,1)}, bf16[224,1024]{1,0:T(8,128)(2,1)S(1)}, u32[]{:S(2)}, u32[]{:S(2)}) %collective-permute-start.4) | collective-permute-done | bytes 458784 | tf_op jit(solution)/shard_map/ppermute | solution.py:51
  189.5 18.2 %cross_back.1 = (f32[224,1024]{1,0:T(8,128)}, bf16[224,1024]{1,0:T(8,128)(2,1)}, bf16[2,752,512]{2,1,0:T(8,128)(2,1)}, bf16[2,752,512]{2,1,0:T(8,128)(2,1)}, f32...) custom-call(bf16[224,1024]{1,0:T(8,128)(2,1)} %bitcast.74, ...), custom_call_target="tpu_custom_call" | custom-call | flops 17999998976 | bytes 66420000 | tf_op jit(solution)/shard_map/cross_back/pallas_call | solution.py:515
  211.1 10.3 %collective-permute-done.6 = bf16[224,1024]{1,0:T(8,128)(2,1)S(1)} collective-permute-done((bf16[224,1024]{1,0:T(8,128)(2,1)S(1)}, bf16[224,1024]{1,0:T(8,128)(2,1)S(1)}, u32[]{:S(2)}, u32[]{:S(2)}) %collective-permute-start.6) | collective-permute-done | bytes 458784 | tf_op jit(solution)/shard_map/ppermute | solution.py:51
  222.5 8.4 %frames_back.1 = (bf16[376,1024]{1,0:T(8,128)(2,1)}, bf16[374,1024]{1,0:T(8,128)(2,1)}, f32[2,16,1024]{2,1,0:T(8,128)}, f32[2,16,512]{2,1,0:T(8,128)}) custom-call(bf16[2,752,512]{2,1,0:T(8,128)(2,1)} %get-tuple-element.93.grad_mine, bf16[2,752,512]{2,1,0:T(8,128)(2,1)} %copy-done.14, bf16[16,8,64,512]{3,2,1,0:T(8,128)(2,1)} %bitcast.65, ...), custom_call_target="tpu_custom_call" | custom-call | flops 8999999488 | bytes 33210000 | tf_op jit(solution)/shard_map/frames_back/pallas_call | solution.py:515
  232.5 12.0 %self_back.1 = (f32[224,1024]{1,0:T(8,128)}, f32[224,1024]{1,0:T(8,128)}, bf16[2,224,512]{2,1,0:T(8,128)(2,1)}, bf16[2,224,512]{2,1,0:T(8,128)(2,1)}, f32[16,512...) custom-call(s32[3]{0:T(128)} %pad_add_fusion.where.refs_0_, ...), custom_call_target="tpu_custom_call" | custom-call | flops 12000000000 | bytes 44280000 | tf_op jit(solution)/shard_map/self_back/pallas_call | solution.py:515
  244.5 5.9 %pack_early.1 = (f32[2,8,96,128]{3,2,1,0:T(8,128)}, f32[2,8,96,128]{3,2,1,0:T(8,128)}) custom-call(s32[3]{0:T(128)} %pad_add_fusion.where.refs_0_, f32[16,1024]{1,0:T(8,128)} %get-tuple-element.113.refs_1_, f32[2,16,1024]{2,1,0:T(8,128)} %get-tuple-element.114.refs_2_, f32[16,1024]{1,0:T(8,128)} %get-tuple-element.115.refs_3_, ...), custom_call_target="tpu_custom_call" | custom-call | flops 5000000000 | bytes 18450000 | tf_op jit(solution)/shard_map/pack_early/pallas_call | solution.py:515
  253.3 4.7 %self_project_back.1 = (bf16[224,1024]{1,0:T(8,128)(2,1)}, f32[2,16,1024]{2,1,0:T(8,128)}, f32[2,16,512]{2,1,0:T(8,128)}) custom-call(bf16[2,224,512]{2,1,0:T(8,128)(2,1)} %get-tuple-element.105.grad_mine, bf16[2,224,512]{2,1,0:T(8,128)(2,1)} %copy-done.16, bf16[16,8,64,512]{3,2,1,0:T(8,128)(2,1)} %bitcast.68, ...), custom_call_target="tpu_custom_call" | custom-call | flops 5000000000 | bytes 18450000 | tf_op jit(solution)/shard_map/self_project_back/pallas_call | solution.py:515
  258.0 5.3 %pack_late.1 = (f32[2,8,32,128]{3,2,1,0:T(8,128)}, f32[2,8,32,128]{3,2,1,0:T(8,128)}) custom-call(s32[3]{0:T(128)} %pad_add_fusion.where.refs_0_, f32[16,1024]{1,0:T(8,128)} %get-tuple-element.125.refs_1_, f32[2,16,1024]{2,1,0:T(8,128)} %get-tuple-element.126.refs_2_, f32[16,1024]{1,0:T(8,128)} %get-tuple-element.127.refs_3_, ...), custom_call_target="tpu_custom_call" | custom-call | flops 5000000000 | bytes 18450000 | tf_op jit(solution)/shard_map/pack_late/pallas_call | solution.py:515
  265.6 5.7 %collective-permute-done.11.low_other = bf16[374,1024]{1,0:T(8,128)(2,1)} collective-permute-done((bf16[374,1024]{1,0:T(8,128)(2,1)}, bf16[374,1024]{1,0:T(8,128)(2,1)}, u32[]{:S(2)}, u32[]{:S(2)}) %collective-permute-start.11) | collective-permute-done | bytes 765984 | tf_op jit(solution)/shard_map/ppermute | solution.py:51
  271.3 4.3 %encoder_total.1 = f32[750,1,1024]{2,1,0:T(1,128)} custom-call(bf16[376,1024]{1,0:T(8,128)(2,1)} %get-tuple-element.107.top, bf16[376,1024]{1,0:T(8,128)(2,1)} %collective-permute-done.9.top_other, bf16[374,1024]{1,0:T(8,128)(2,1)} %get-tuple-element.112.low, bf16[374,1024]{1,0:T(8,128)(2,1)} %collective-permute-done.11.low_other), custom_call_target="tpu_custom_call" | custom-call | flops 5000000000 | bytes 18450000 | tf_op jit(solution)/shard_map/encoder_total/pallas_call | solution.py:515
  277.3 7.8 %collective-permute-done.13 = bf16[8,96,128]{2,1,0:T(8,128)(2,1)} collective-permute-done((bf16[8,96,128]{2,1,0:T(8,128)(2,1)S(1)}, bf16[8,96,128]{2,1,0:T(8,128)(2,1)}, u32[]{:S(2)}, u32[]{:S(2)}) %collective-permute-start.13) | collective-permute-done | bytes 196640 | tf_op jit(solution)/shard_map/ppermute | solution.py:51
  285.1 1.8 fusion.12
  286.9 1.6 fusion.14
  288.5 3.4 %all-to-all-start.1 = ((bf16[8,32,128]{2,1,0:T(8,128)(2,1)}), bf16[8,32,128]{2,1,0:T(8,128)(2,1)S(1)}, u32[]{:S(2)}, u32[]{:S(2)}) async-start(bf16[8,32,128]{2,1,0:T(8,128)(2,1)} %fusion.14), calls=%async_computation.1 | async-start | bytes 131072 | tf_op jit(solution)/shard_map/all_to_all | solution.py:935
  292.3 6.4 %all-to-all-done.1.late = bf16[8,32,128]{2,1,0:T(8,128)(2,1)S(1)} async-done(((bf16[8,32,128]{2,1,0:T(8,128)(2,1)}), bf16[8,32,128]{2,1,0:T(8,128)(2,1)S(1)}, u32[]{:S(2)}, u32[]{:S(2)}) %all-to-all-start.1) | async-done | bytes 65568 | tf_op jit(solution)/shard_map/all_to_all | solution.py:935
  298.7 3.4 %all-to-all-start = ((bf16[8,96,128]{2,1,0:T(8,128)(2,1)}), bf16[8,96,128]{2,1,0:T(8,128)(2,1)S(1)}, u32[]{:S(2)}, u32[]{:S(2)}) async-start(bf16[8,96,128]{2,1,0:T(8,128)(2,1)} %fusion.12), calls=%async_computation | async-start | bytes 393216 | tf_op jit(solution)/shard_map/all_to_all | solution.py:935
  303.4 6.4 %all-to-all-done.early = bf16[8,96,128]{2,1,0:T(8,128)(2,1)S(1)} async-done(((bf16[8,96,128]{2,1,0:T(8,128)(2,1)}), bf16[8,96,128]{2,1,0:T(8,128)(2,1)S(1)}, u32[]{:S(2)}, u32[]{:S(2)}) %all-to-all-start) | async-done | bytes 196640 | tf_op jit(solution)/shard_map/all_to_all | solution.py:935
  310.5 2.4 unpack.1
  (91 shorter events, 26.5 us)
Async XLA Ops:
  7.2 6.4 %copy-start = (bf16[8,8,16,1024]{3,2,1,0:T(8,128)(2,1)S(1)}, bf16[8,8,16,1024]{3,2,1,0:T(8,128)(2,1)}, u32[]{:S(2)}) copy-start(bf16[8,8,16,1024]{3,2,1,0:T(8,128)(2,1)} %param.24) | copy-start | bytes 6291460
  7.2 3.1 copy-start.12
  7.2 3.1 copy-start.11
  7.2 80.6 %all-gather.5.cloned.1.call-start = ((), (), s32[]{:S(2)}) async-start(), calls=%async_computation.2 | async-start | bytes 8912896 | tf_op jit(solution)/shard_map/all_gather | solution.py:567
  10.2 153.2 %all-gather.7.cloned.1.call-start = ((), (), s32[]{:S(2)}) async-start(), calls=%async_computation.3 | async-start | bytes 8912896 | tf_op jit(solution)/shard_map/all_gather | solution.py:568
  93.5 10.7 %collective-permute-start = (bf16[2,224,512]{2,1,0:T(8,128)(2,1)}, bf16[2,224,512]{2,1,0:T(8,128)(2,1)S(1)}, u32[]{:S(2)}, u32[]{:S(2)}) collective-permute-start(bf16[2,224,512]{2,1,0:T(8,128)(2,1)} %get-tuple-element.75.mine.refs_13_), channel_id=1, source_target_pairs={{0,2},{2,0},{1,3},{3,1},{4,6},{6,4},{5,7},{7,5},{8,10},{10,8},{9,1... | collective-permute-start | bytes 1376264 | tf_op jit(solution)/shard_map/ppermute | solution.py:51
  100.9 24.3 %collective-permute-start.2 = (bf16[2,752,512]{2,1,0:T(8,128)(2,1)}, bf16[2,752,512]{2,1,0:T(8,128)(2,1)}, u32[]{:S(2)}, u32[]{:S(2)}) collective-permute-start(bf16[2,752,512]{2,1,0:T(8,128)(2,1)} %get-tuple-element.77.mine), channel_id=1, source_target_pairs={{0,2},{2,0},{1,3},{3,1},{4,6},{6,4},{5,7},{7,5},{8,10},{10,8},{9,1... | collective-permute-start | bytes 4620296 | tf_op jit(solution)/shard_map/ppermute | solution.py:51
  112.2 13.0 %collective-permute-start.1 = (bf16[224,1024]{1,0:T(8,128)(2,1)}, bf16[224,1024]{1,0:T(8,128)(2,1)S(1)}, u32[]{:S(2)}, u32[]{:S(2)}) collective-permute-start(bf16[224,1024]{1,0:T(8,128)(2,1)} %get-tuple-element.76.branch_mine), channel_id=1, source_target_pairs={{0,1},{1,0},{2,3},{3,2},{4,5},{5,4},{6,7},{7,6},{8,9},{9,8},{10,11... | collective-permute-start | bytes 1376264 | tf_op jit(solution)/shard_map/ppermute | solution.py:51
  139.4 24.0 %collective-permute-start.3 = (bf16[224,1024]{1,0:T(8,128)(2,1)}, bf16[224,1024]{1,0:T(8,128)(2,1)S(1)}, u32[]{:S(2)}, u32[]{:S(2)}) collective-permute-start(bf16[224,1024]{1,0:T(8,128)(2,1)} %get-tuple-element.79.branch_mine), channel_id=1, source_target_pairs={{0,1},{1,0},{2,3},{3,2},{4,5},{5,4},{6,7},{7,6},{8,9},{9,8},{10,11... | collective-permute-start | bytes 1376264 | tf_op jit(solution)/shard_map/ppermute | solution.py:51
  175.8 13.0 %collective-permute-start.4 = (bf16[224,1024]{1,0:T(8,128)(2,1)}, bf16[224,1024]{1,0:T(8,128)(2,1)S(1)}, u32[]{:S(2)}, u32[]{:S(2)}) collective-permute-start(bf16[224,1024]{1,0:T(8,128)(2,1)} %get-tuple-element.82.grad_mine), channel_id=1, source_target_pairs={{0,1},{1,0},{2,3},{3,2},{4,5},{5,4},{6,7},{7,6},{8,9},{9,8},{10,11... | collective-permute-start | bytes 1376264 | tf_op jit(solution)/shard_map/ppermute | solution.py:51
  189.5 18.3 %copy-start.2 = (bf16[1,224,1024]{2,1,0:T(8,128)(2,1)S(1)}, bf16[1,224,1024]{2,1,0:T(8,128)(2,1)}, u32[]{:S(2)}) copy-start(bf16[1,224,1024]{2,1,0:T(8,128)(2,1)} %param.15) | copy-start | bytes 1376260
  189.5 18.4 %copy-start.8 = (bf16[224,1024]{1,0:T(8,128)(2,1)S(1)}, bf16[224,1024]{1,0:T(8,128)(2,1)}, u32[]{:S(2)}) copy-start(bf16[224,1024]{1,0:T(8,128)(2,1)} %get-tuple-element.81) | copy-start | bytes 1376260
  207.7 13.7 %collective-permute-start.5 = (bf16[2,752,512]{2,1,0:T(8,128)(2,1)}, bf16[2,752,512]{2,1,0:T(8,128)(2,1)S(1)}, u32[]{:S(2)}, u32[]{:S(2)}) collective-permute-start(bf16[2,752,512]{2,1,0:T(8,128)(2,1)} %get-tuple-element.89), channel_id=1, source_target_pairs={{0,2},{2,0},{1,3},{3,1},{4,6},{6,4},{5,7},{7,5},{8,10},{10,8},{9,1... | collective-permute-start | bytes 4620296 | tf_op jit(solution)/shard_map/ppermute | solution.py:51
  207.9 13.5 %collective-permute-start.6 = (bf16[224,1024]{1,0:T(8,128)(2,1)S(1)}, bf16[224,1024]{1,0:T(8,128)(2,1)S(1)}, u32[]{:S(2)}, u32[]{:S(2)}) collective-permute-start(bf16[224,1024]{1,0:T(8,128)(2,1)S(1)} %copy-done.8), channel_id=1, source_target_pairs={{0,1},{1,0},{2,3},{3,2},{4,5},{5,4},{6,7},{7,6},{8,9},{9,8},{10,11... | collective-permute-start | bytes 1376264 | tf_op jit(solution)/shard_map/ppermute | solution.py:51
  210.5 20.5 %collective-permute-start.7 = (bf16[224,1024]{1,0:T(8,128)(2,1)}, bf16[224,1024]{1,0:T(8,128)(2,1)S(1)}, u32[]{:S(2)}, u32[]{:S(2)}) collective-permute-start(bf16[224,1024]{1,0:T(8,128)(2,1)} %get-tuple-element.92.refs_3_), channel_id=1, source_target_pairs={{0,1},{1,0},{2,3},{3,2},{4,5},{5,4},{6,7},{7,6},{8,9},{9,8},{10,11... | collective-permute-start | bytes 1376264 | tf_op jit(solution)/shard_map/ppermute | solution.py:51
  231.0 21.6 %collective-permute-start.9 = (bf16[376,1024]{1,0:T(8,128)(2,1)}, bf16[376,1024]{1,0:T(8,128)(2,1)}, u32[]{:S(2)}, u32[]{:S(2)}) collective-permute-start(bf16[376,1024]{1,0:T(8,128)(2,1)} %get-tuple-element.107.top), channel_id=1, source_target_pairs={{0,1},{1,0},{2,3},{3,2},{4,5},{5,4},{6,7},{7,6},{8,9},{9,8},{10,11... | collective-permute-start | bytes 2310152 | tf_op jit(solution)/shard_map/ppermute | solution.py:51
  244.5 8.1 %collective-permute-start.8 = (bf16[2,224,512]{2,1,0:T(8,128)(2,1)}, bf16[2,224,512]{2,1,0:T(8,128)(2,1)S(1)}, u32[]{:S(2)}, u32[]{:S(2)}) collective-permute-start(bf16[2,224,512]{2,1,0:T(8,128)(2,1)} %get-tuple-element.106), channel_id=1, source_target_pairs={{0,2},{2,0},{1,3},{3,1},{4,6},{6,4},{5,7},{7,5},{8,10},{10,8},{9,1... | collective-permute-start | bytes 1376264 | tf_op jit(solution)/shard_map/ppermute | solution.py:51
  244.5 7.1 %copy-start.4 = (f32[224,1024]{1,0:T(8,128)S(1)}, f32[224,1024]{1,0:T(8,128)}, u32[]{:S(2)}) copy-start(f32[224,1024]{1,0:T(8,128)} %get-tuple-element.80.rows) | copy-start | bytes 2752516
  250.4 14.3 %collective-permute-start.12 = (f32[2,8,96,128]{3,2,1,0:T(8,128)}, f32[2,8,96,128]{3,2,1,0:T(8,128)S(1)}, u32[]{:S(2)}, u32[]{:S(2)}) collective-permute-start(f32[2,8,96,128]{3,2,1,0:T(8,128)} %get-tuple-element.124), channel_id=1, source_target_pairs={{0,2},{2,0},{1,3},{3,1},{4,6},{6,4},{5,7},{7,5},{8,10},{10,8},{9,1... | collective-permute-start | bytes 2359304 | tf_op jit(solution)/shard_map/ppermute | solution.py:51
  250.9 20.4 %collective-permute-start.11 = (bf16[374,1024]{1,0:T(8,128)(2,1)}, bf16[374,1024]{1,0:T(8,128)(2,1)}, u32[]{:S(2)}, u32[]{:S(2)}) collective-permute-start(bf16[374,1024]{1,0:T(8,128)(2,1)} %get-tuple-element.112.low), channel_id=1, source_target_pairs={{0,1},{1,0},{2,3},{3,2},{4,5},{5,4},{6,7},{7,6},{8,9},{9,8},{10,11... | collective-permute-start | bytes 2297864 | tf_op jit(solution)/shard_map/ppermute | solution.py:51
  258.0 5.3 %copy-start.3 = (bf16[224,1024]{1,0:T(8,128)(2,1)S(1)}, bf16[224,1024]{1,0:T(8,128)(2,1)}, u32[]{:S(2)}) copy-start(bf16[224,1024]{1,0:T(8,128)(2,1)} %get-tuple-element.110) | copy-start | bytes 1376260
  258.0 6.7 %copy-start.6 = (f32[2,8,96,128]{3,2,1,0:T(8,128)S(1)}, f32[2,8,96,128]{3,2,1,0:T(8,128)}, u32[]{:S(2)}) copy-start(f32[2,8,96,128]{3,2,1,0:T(8,128)} %get-tuple-element.123) | copy-start | bytes 2359300
  263.3 12.2 %collective-permute-start.14 = (f32[2,8,32,128]{3,2,1,0:T(8,128)}, f32[2,8,32,128]{3,2,1,0:T(8,128)}, u32[]{:S(2)}, u32[]{:S(2)}) collective-permute-start(f32[2,8,32,128]{3,2,1,0:T(8,128)} %get-tuple-element.132), channel_id=1, source_target_pairs={{0,2},{2,0},{1,3},{3,1},{4,6},{6,4},{5,7},{7,5},{8,10},{10,8},{9,1... | collective-permute-start | bytes 786440 | tf_op jit(solution)/shard_map/ppermute | solution.py:51
  263.3 28.5 %collective-permute-start.10 = (bf16[224,1024]{1,0:T(8,128)(2,1)S(1)}, bf16[224,1024]{1,0:T(8,128)(2,1)S(1)}, u32[]{:S(2)}, u32[]{:S(2)}) collective-permute-start(bf16[224,1024]{1,0:T(8,128)(2,1)S(1)} %copy-done.3), channel_id=1, source_target_pairs={{0,1},{1,0},{2,3},{3,2},{4,5},{5,4},{6,7},{7,6},{8,9},{9,8},{10,11... | collective-permute-start | bytes 1376264 | tf_op jit(solution)/shard_map/ppermute | solution.py:51
  264.7 6.6 %copy-start.7 = (f32[2,8,96,128]{3,2,1,0:T(8,128)}, f32[2,8,96,128]{3,2,1,0:T(8,128)S(1)}, u32[]{:S(2)}) copy-start(f32[2,8,96,128]{3,2,1,0:T(8,128)S(1)} %collective-permute-done.12) | copy-start | bytes 2359300
  264.8 10.8 %copy-start.9 = (f32[2,8,32,128]{3,2,1,0:T(8,128)S(1)}, f32[2,8,32,128]{3,2,1,0:T(8,128)}, u32[]{:S(2)}) copy-start(f32[2,8,32,128]{3,2,1,0:T(8,128)} %get-tuple-element.131) | copy-start | bytes 786436
  264.8 20.3 %collective-permute-start.13 = (bf16[8,96,128]{2,1,0:T(8,128)(2,1)S(1)}, bf16[8,96,128]{2,1,0:T(8,128)(2,1)}, u32[]{:S(2)}, u32[]{:S(2)}) collective-permute-start(bf16[8,96,128]{2,1,0:T(8,128)(2,1)S(1)} %fusion.13), channel_id=1, source_target_pairs={{0,1},{1,0},{2,3},{3,2},{4,5},{5,4},{6,7},{7,6},{8,9},{9,8},{10,11... | collective-permute-start | bytes 589832 | tf_op jit(solution)/shard_map/ppermute | solution.py:51
  275.5 26.6 %copy-start.5 = (f32[224,1024]{1,0:T(8,128)S(1)}, f32[224,1024]{1,0:T(8,128)}, u32[]{:S(2)}) copy-start(f32[224,1024]{1,0:T(8,128)} %get-tuple-element.104) | copy-start | bytes 2752516
  276.6 10.4 %collective-permute-start.15 = (bf16[8,32,128]{2,1,0:T(8,128)(2,1)S(1)}, bf16[8,32,128]{2,1,0:T(8,128)(2,1)S(1)}, u32[]{:S(2)}, u32[]{:S(2)}) collective-permute-start(bf16[8,32,128]{2,1,0:T(8,128)(2,1)S(1)} %fusion.15), channel_id=1, source_target_pairs={{0,1},{1,0},{2,3},{3,2},{4,5},{5,4},{6,7},{7,6},{8,9},{9,8},{10,11... | collective-permute-start | bytes 196616 | tf_op jit(solution)/shard_map/ppermute | solution.py:51
  288.5 10.2 %all-to-all-start.1 = ((bf16[8,32,128]{2,1,0:T(8,128)(2,1)}), bf16[8,32,128]{2,1,0:T(8,128)(2,1)S(1)}, u32[]{:S(2)}, u32[]{:S(2)}) async-start(bf16[8,32,128]{2,1,0:T(8,128)(2,1)} %fusion.14), calls=%async_computation.1 | async-start | bytes 131072 | tf_op jit(solution)/shard_map/all_to_all | solution.py:935
  298.7 11.1 %copy-start.13 = (bf16[8,32,128]{2,1,0:T(8,128)(2,1)}, bf16[8,32,128]{2,1,0:T(8,128)(2,1)S(1)}, u32[]{:S(2)}) copy-start(bf16[8,32,128]{2,1,0:T(8,128)(2,1)S(1)} %all-to-all-done.1.late) | copy-start | bytes 196612
  298.7 11.1 %all-to-all-start = ((bf16[8,96,128]{2,1,0:T(8,128)(2,1)}), bf16[8,96,128]{2,1,0:T(8,128)(2,1)S(1)}, u32[]{:S(2)}, u32[]{:S(2)}) async-start(bf16[8,96,128]{2,1,0:T(8,128)(2,1)} %fusion.12), calls=%async_computation | async-start | bytes 393216 | tf_op jit(solution)/shard_map/all_to_all | solution.py:935
  (9 other events, 9.6 us)
Sparse Core Ops, SparseCore 0:
  10.8 77.0 all-gather.4
  90.5 72.8 all-gather.6

commit v2 on v1

--- a/solution.py
+++ b/solution.py
@@ -76,45 +76,52 @@
     return jnp.where(row < HEAD_DIM, first, second).T
 
 
-def pair_forward(queries, keys, values, limit):
+def pair_forward(queries, keys, values, limit, saved=None):
     mixed, logsums = [], []
-    for keep in half_masks(queries.shape[0]):
-        mine = pick_half(queries, keep)
-        scores = [limit(i, mm_nt(k, mine) * SCALE) for i, k in enumerate(keys)]
+    turned = [v.T for v in values]
+    for half, keep in enumerate(half_masks(queries.shape[0])):
+        mine = pick_half(queries, keep) * BF(SCALE)
+        scores = [limit(i, mm_nt(k, mine)) for i, k in enumerate(keys)]
         top = jnp.max(scores[0], axis=0, keepdims=True)
         for s in scores[1:]:
             top = jnp.maximum(top, jnp.max(s, axis=0, keepdims=True))
         powers = [jnp.exp(s - top) for s in scores]
         total = sum(jnp.sum(e, axis=0, keepdims=True) for e in powers)
         share = 1.0 / total
-        out = sum(mm_tn(v, (e * share).astype(BF)) for v, e in zip(values, powers))
-        mixed.append(out)
+        weights = [(e * share).astype(BF) for e in powers]
+        if saved is not None:
+            for i, w in enumerate(weights):
+                saved[0, half, i, : w.shape[0]] = w
+        mixed.append(sum(mm(v, w) for v, w in zip(turned, weights)))
         logsums.append(top + jnp.log(total))
     return join_halves(*mixed), logsums
 
 
-def pair_backward(grad, queries, keys, values, logsums, limit):
+def pair_backward(grad, mixed, queries, keys, values, logsums, limit, saved=None):
     grad_query, grad_keys, grad_values = [], [0.0] * len(keys), [0.0] * len(keys)
-    for keep, logsum in zip(half_masks(queries.shape[0]), logsums):
-        mine = pick_half(queries, keep)
+    inners = (grad.astype(F32) * mixed.astype(F32)).T
+    turned = [k.T for k in keys]
+    for half, (keep, logsum) in enumerate(zip(half_masks(queries.shape[0]), logsums)):
+        mine = pick_half(queries, keep) * BF(SCALE)
         grad_mine = pick_half(grad, keep)
-        weights = [
-            jnp.exp(limit(i, mm_nt(k, mine) * SCALE) - logsum) for i, k in enumerate(keys)
-        ]
-        grad_weights = [mm_nt(v, grad_mine) for v in values]
-        inner = sum(
-            jnp.sum(g * w, axis=0, keepdims=True) for g, w in zip(grad_weights, weights)
-        )
+        at = HEAD_DIM * half
+        inner = jnp.sum(inners[at : at + HEAD_DIM], axis=0, keepdims=True)
         part = 0.0
-        for i, key in enumerate(keys):
-            grad_scores = (weights[i] * (grad_weights[i] - inner)).astype(BF)
-            part = part + mm_tn(key, grad_scores)
+        for i, (key, value) in enumerate(zip(keys, values)):
+            if saved is None:
+                weights = jnp.exp(limit(i, mm_nt(key, mine)) - logsum)
+                rounded = weights.astype(BF)
+            else:
+                rounded = saved[0, half, i, : key.shape[0]]
+                weights = rounded.astype(F32)
+            grad_scores = (weights * (mm_nt(value, grad_mine) - inner)).astype(BF)
+            part = part + mm(turned[i], grad_scores)
             grad_keys[i] = grad_keys[i] + mm(grad_scores, mine)
-            grad_values[i] = grad_values[i] + mm(weights[i].astype(BF), grad_mine)
+            grad_values[i] = grad_values[i] + mm(rounded, grad_mine)
         grad_query.append(part)
     return (
         (join_halves(*grad_query) * SCALE).astype(BF),
-        [(g * SCALE).astype(BF) for g in grad_keys],
+        [g.astype(BF) for g in grad_keys],
         [g.astype(BF) for g in grad_values],
     )
 
@@ -201,7 +208,7 @@
     count,
     hidden, branch_mine, branch_other, gains, query_weight, query_in, query_out, mine, other,
     weight, low_in, low_out,
-    middle, normed, query, query_low, mixed, logsum, branch, low, acc, low_acc,
+    middle, normed, query, query_low, mixed, saved, branch, low, acc, low_acc,
 ):
     @at_first()
     def _():
@@ -219,16 +226,15 @@
         mm(normed[...], matrix(query_weight)) + mm(query_low[...], query_out[0])
     ).astype(BF)
     query[...] = queries
-    out, logs = pair_forward(
+    out, _ = pair_forward(
         queries,
         (mine[0, :count], other[0, :count]),
         (mine[1, :count], other[1, :count]),
         no_limit,
+        saved,
     )
     out = out.astype(BF)
     mixed[...] = out
-    logsum[0, 0:1, :] = logs[0]
-    logsum[0, 1:2, :] = logs[1]
     acc[...] += mm_nt(out, matrix(weight))
     low_acc[...] += mm_nt(out, low_in[0])
 
@@ -283,7 +289,7 @@
 
 
 def attention_back(
-    limit, slot, count, carried, rows, gains, grad_mine, grad_other, weight, low_in, low_out,
+    limit, slot, count, stored, carried, rows, gains, grad_mine, grad_other, weight, low_in, low_out,
     query_weight, query_in, query_out, query, mixed, mine, other, logsum, normed, query_low, low,
     carry, grad_normed, grad_kv, grad_kv_other,
     table_in, table_out, table_query_in, table_query_out,
@@ -307,11 +313,13 @@
     table_in[...] = mm_tn(back_low[...], mixed[...])
     grad_query, grad_keys, grad_values = pair_backward(
         grad,
+        mixed[...],
         query[...],
         (mine[0, :count], other[0, :count]),
         (mine[1, :count], other[1, :count]),
-        (logsum[0, 0:1, :], logsum[0, 1:2, :]),
+        (None, None) if stored else (logsum[0, 0:1, :], logsum[0, 1:2, :]),
         limit,
+        logsum if stored else None,
     )
     for which, (first, second) in enumerate((grad_keys, grad_values)):
         grad_kv[which, :count] = first
@@ -333,7 +341,7 @@
 
 
 def self_back_kernel(count, where, *refs):
-    attention_back(causal_limit(where[0]), 1, count, *refs)
+    attention_back(causal_limit(where[0]), 1, count, False, *refs)
 
 
 def pair_project_kernel(
@@ -353,12 +361,18 @@
         total[...] = acc[...].astype(BF)
 
 
-def add_rows_kernel(top, top_other, low, low_other, total):
-    count = top.shape[0]
-    first = top[...].astype(F32) + top_other[...].astype(F32)
-    second = low[...].astype(F32) + low_other[...].astype(F32)
-    total[:count] = first[:, None, :]
-    total[count:] = second[:, None, :]
+def close_kernel(hidden, gains, carried, grad_mine, grad_other, total):
+    total[...] = carried[...] + normalize_back(
+        hidden[...].astype(F32),
+        gains[0:1, :],
+        grad_mine[...].astype(F32) + grad_other[...].astype(F32),
+    )
+
+
+def add_rows_kernel(mine, other, *refs):
+    total = refs[-1]
+    value = mine[...].astype(F32) + other[...].astype(F32)
+    total[...] = value[:, None, :]
 
 
 def frames_back_kernel(
@@ -394,7 +408,7 @@
 PIECE = 32
 
 
-def pack_kernel(fulls, shares, wides, order, tagged, *refs):
+def pack_kernel(fulls, shares, order, tagged, *refs):
     where = refs[0]
     keep, send = refs[-2:]
     flat = []
@@ -406,77 +420,76 @@
     per_group = (len(order) + 3) // 4
     rows = per_group * 16
     lane = lax.broadcasted_iota(jnp.int32, (rows, LANE), 1) // PIECE
-    for f in range(blocks):
-        shard = f * 2 // blocks
-        local = f % (blocks // 2)
+    padded = list(order) + [None] * (4 * per_group - len(order))
+
+    def one_block(f, carry):
+        shard = f // (blocks // 2)
+        local = f - shard * (blocks // 2)
+        owned = tensor == shard
 
         def table_of(k):
             if k is None:
                 return jnp.zeros((16, LANE), F32)
             if k < fulls:
-                return tables[k][:, f * LANE : (f + 1) * LANE]
-            part = tables[k][:, local * LANE : (local + 1) * LANE]
-            return jnp.where(tensor == shard, part, 0.0)
-
-        padded = list(order) + [None] * (4 * per_group - len(order))
+                return tables[k][:, pl.ds(pl.multiple_of(f * LANE, LANE), LANE)]
+            part = tables[k][:, pl.ds(pl.multiple_of(local * LANE, LANE), LANE)]
+            return jnp.where(owned, part, 0.0)
+
         groups = [
             jnp.concatenate(
                 [table_of(k) for k in padded[g * per_group : (g + 1) * per_group]], axis=0
             )
             for g in range(4)
         ]
-        for p in range(4):
-            value = jnp.zeros((rows, LANE), F32)
-            for g in range(4):
-                turned = pltpu.roll(groups[g], (PIECE * (g - p)) % LANE, 1)
-                value = jnp.where(lane == g, turned, value)
-            pieces = [value]
-            for w in broad:
-                at = local * 4 * LANE + p * LANE
-                pieces.append(jnp.where(tensor == shard, w[:, at : at + LANE], 0.0))
-            if tagged:
-                tag = where[2].astype(F32) * 0.25
-                pieces.append(jnp.full((16, LANE), 1.0, F32) * tag)
-            whole = jnp.concatenate(pieces, axis=0)
-
-            @pl.when(context == p // 2)
-            def _(whole=whole, f=f, p=p):
-                keep[p % 2, f] = whole
-
-            @pl.when(context != p // 2)
-            def _(whole=whole, f=f, p=p):
-                send[p % 2, f] = whole
-
-
-def unpack_kernel(early, late, attn_in, attn_out, up_in, up_out, down_in, down_out):
-    clips = early.shape[0]
-    adapters = attn_in.shape[1]
-    tag_row = early.shape[1] - 16
-    tags = [early[c, tag_row : tag_row + 1, :].astype(F32) for c in range(clips)]
-    early_rows = [early[c].astype(F32) for c in range(clips)]
-    late_rows = [late[c].astype(F32) for c in range(clips)]
-    for a in range(adapters):
-        first = jnp.zeros(early_rows[0].shape, F32)
-        second = jnp.zeros(late_rows[0].shape, F32)
+        for target, side in ((keep, context), (send, 1 - context)):
+            for t in range(2):
+                p = 2 * side + t
+                value = jnp.zeros((rows, LANE), F32)
+                for g in range(4):
+                    turned = pltpu.roll(groups[g], (PIECE * (g + 4 - p)) % LANE, 1)
+                    value = jnp.where(lane == g, turned, value)
+                target[t, f, :rows] = value
+                row = rows
+                for w in broad:
+                    at = pl.multiple_of(local * 4 * LANE + p * LANE, LANE)
+                    target[t, f, row : row + 16] = jnp.where(owned, w[:, pl.ds(at, LANE)], 0.0)
+                    row += 16
+                if tagged:
+                    tag = where[2].astype(F32) * 0.25
+                    target[t, f, row : row + 16] = jnp.full((16, LANE), 1.0, F32) * tag
+        return carry
+
+    lax.fori_loop(0, blocks, one_block, 0)
+
+
+def unpack_kernel(parts, attn_in, attn_out, up_in, up_out, down_in, down_out):
+    projections, adapters = attn_in.shape[:2]
+    clips, rows = parts.shape[:2]
+    per_group = (2 * projections + 2 + 3) // 4
+    narrow = 16 * per_group
+
+    def one(a, carry):
+        adapter = a.astype(F32)
+        block = jnp.zeros((rows - 16, LANE), F32)
         for c in range(clips):
-            same = (tags[c] > a - 0.5) & (tags[c] < a + 0.5)
-            weight = jnp.where(same, 1.0, 0.0)
-            first = first + early_rows[c] * weight
-            second = second + late_rows[c] * weight
-
-        def piece(block, k, per_group):
+            tag = parts[c, rows - 16 : rows - 15, :].astype(F32)
+            same = (tag > adapter - 0.5) & (tag < adapter + 0.5)
+            block = block + jnp.where(same, parts[c, : rows - 16].astype(F32), 0.0)
+
+        def piece(k):
             g, at = k // per_group, 16 * (k % per_group)
             return block[at : at + 16, PIECE * g : PIECE * (g + 1)]
 
-        for j in range(4):
-            attn_in[j, a] = piece(second, j, 2)
-            attn_out[j, a] = piece(second, 4 + j, 2)
-            attn_in[4 + j, a] = piece(first, j, 3)
-            attn_out[4 + j, a] = piece(first, 4 + j, 3)
-        up_in[a] = piece(first, 8, 3)
-        down_out[a] = piece(first, 9, 3)
-        up_out[a] = first[48:64]
-        down_in[a] = first[64:80]
+        for j in range(projections):
+            attn_in[j, a] = piece(j)
+            attn_out[j, a] = piece(projections + j)
+        up_in[a] = piece(2 * projections)
+        down_out[a] = piece(2 * projections + 1)
+        up_out[a] = block[narrow : narrow + 16]
+        down_in[a] = block[narrow + 16 : narrow + 32]
+        return carry
+
+    lax.fori_loop(0, adapters, one, 0)
 
 
 def shape(dims, dtype):
@@ -493,7 +506,7 @@
     return pl.BlockSpec(dims, lambda *_: zeros)
 
 
-def call(kernel, steps, ins, outs, scratch=(), scalars=None, name=None, cost=5):
+def call(kernel, steps, ins, outs, scratch=(), scalars=None, name=None, cost=5, aliases=None):
     arrays = [a for a, _ in ins]
     spec = pltpu.PrefetchScalarGridSpec(
         num_scalar_prefetch=0 if scalars is None else 1,
@@ -508,8 +521,9 @@
         out_shape=[o for o, _ in outs],
         compiler_params=pltpu.CompilerParams(dimension_semantics=("arbitrary",)),
         cost_estimate=pl.CostEstimate(
-            flops=cost * 1_000_000_000, transcendentals=0, bytes_accessed=cost * 3_690_000
+            flops=cost * 10_000_000, transcendentals=0, bytes_accessed=cost * 36_900
         ),
+        input_output_aliases=aliases or {},
         name=name,
     )
     return run(*arrays) if scalars is None else run(scalars, *arrays)
@@ -612,10 +626,48 @@
     )
 
     def logsum_in(array):
-        return array, pl.BlockSpec((1, 2, rows), lambda p, *_: (p, 0, 0))
+        rest = (0,) * (array.ndim - 1)
+        return array, pl.BlockSpec((1,) + array.shape[1:], lambda p, *_: (p, *rest))
+
+    saved_shape = shape((pairs, 2, 2, padded, rows), BF)
 
     def pair_in(array):
         return array, pl.BlockSpec((array.shape[0], PAIR), lambda p, *_: (0, p))
+
+    regular = (
+        ctx_size == 2 and tp_size == 2 and rank == 16
+        and width == LANE * fsdp_size and wide == 4 * LANE * fsdp_size
+    )
+
+    def ordered(first, *others):
+        return lax.optimization_barrier((first, *others))
+
+    def pack(full, part, wides, order, tagged, name):
+        count = 16 * ((len(order) + 3) // 4 + len(wides) + tagged)
+        dims = (2, fsdp_size, count, LANE)
+
+        def number(arrays):
+            return sum(1 if a.ndim == 2 else a.shape[0] for a in arrays)
+
+        keep, send = call(
+            partial(pack_kernel, number(full), number(part), order, tagged),
+            1,
+            [whole(a) for a in full + part + wides],
+            [out(dims, F32), out(dims, F32)],
+            scalars=scalars,
+            name=name,
+        )
+        recv = swap(send, "ctx")
+
+        def pick(i):
+            return lax.dynamic_index_in_dim(keep, i, 0, keepdims=False) + (
+                lax.dynamic_index_in_dim(recv, i, 0, keepdims=False)
+            )
+
+        return pick(tensor_index), pick(1 - tensor_index).astype(BF)
+
+    def finish(kept, away):
+        return lax.all_to_all((kept + away.astype(F32)).astype(BF), "fsdp", 0, 0, tiled=True)
 
     wide_acc = pltpu.VMEM((rows, width), F32)
     rank_acc = pltpu.VMEM((rows, rank), F32)
@@ -707,7 +759,7 @@
             by_pair(rows),
             out((rows, rank), BF),
             by_pair(rows),
-            logsum_out,
+            logsum_in(saved_shape),
             out((rows, width), BF),
             out((rows, rank), BF),
         ],
@@ -762,6 +814,7 @@
         cost=11,
     )
     grad_n3, grad_n3_other = with_other(grad_n3, "tp")
+    branch, grad_n3_other = ordered(branch, grad_n3_other)
     branch, branch_other = with_other(branch, "tp")
 
     def back_call(
@@ -815,17 +868,18 @@
         )
 
     grad_second, grad_n2, grad_ckv, grad_ckv_send, co_in_t, co_out_t, cq_in_t, cq_out_t = back_call(
-        partial(attention_back, no_limit, 2, frames), None, cotangent, second_mid, grad_n3, grad_n3_other, (7, 7, 3, 4),
+        partial(attention_back, no_limit, 2, frames, True), None, cotangent, second_mid, grad_n3, grad_n3_other, (7, 7, 3, 4),
         cross_q, cross_mixed, cross_kv, cross_kv_other, cross_logsum, n2, cross_q_low[None],
         cross_o_low, BF, "cross_back", 18,
     )
+    grad_n2, grad_ckv_send, branch_other = ordered(grad_n2, grad_ckv_send, branch_other)
     grad_n2, grad_n2_other = with_other(grad_n2, "tp")
     grad_ckv_other = swap(grad_ckv_send, "ctx")
-    grad_ckv_other, branch_other = lax.optimization_barrier((grad_ckv_other, branch_other))
     layer_out = (
         second_mid + (branch.astype(F32) + branch_other.astype(F32))
     ).astype(BF)
-    first_half = padded // 2
+    block_rows = 128
+    first_rows = (frames * 3 // 4) // block_rows * block_rows
     grad_top, grad_low, ckv_in_t, ckv_out_t = call(
         frames_back_kernel,
         2,
@@ -839,8 +893,8 @@
             at(frames_low),
         ],
         [
-            out((first_half, width), BF),
-            out((frames - first_half, width), BF),
+            out((first_rows, width), BF),
+            out((frames - first_rows, width), BF),
             at(shape((2, rank, width), F32)),
             at(shape((2, rank, cols), F32)),
         ],
@@ -852,14 +906,12 @@
         (grad_top, grad_low, grad_n2_other)
     )
     grad_top, grad_top_other = with_other(grad_top, "tp")
-    grad_low, grad_low_other = with_other(grad_low, "tp")
     grad_first, grad_n1_start, grad_skv, grad_skv_send, so_in_t, so_out_t, q_in_t, q_out_t = back_call(
         partial(self_back_kernel, rows), scalars, grad_second, first_mid, grad_n2, grad_n2_other, (6, 3, 0, 0),
         query, self_mixed, self_kv, self_kv_other, self_logsum, n1, self_low,
         self_o_low, F32, "self_back", 12,
     )
     grad_skv_other = swap(grad_skv_send, "ctx")
-    grad_skv_other, grad_top_other = lax.optimization_barrier((grad_skv_other, grad_top_other))
     grad_n1, kv_in_t, kv_out_t = call(
         pair_project_kernel,
         2,
@@ -882,67 +934,19 @@
         name="self_project_back",
     )
     grad_n1, grad_n1_other = with_other(grad_n1, "tp")
-    grad_encoder = call(
-        add_rows_kernel,
-        1,
-        [whole(grad_top), whole(grad_top_other), whole(grad_low), whole(grad_low_other)],
-        [out((frames, 1, width), F32)],
-        name="encoder_total",
-    )[0].reshape(frames, width)
-    grad_hidden = grad_first + normalize_back(
-        hidden.astype(F32), ln_gains[0], grad_n1.astype(F32) + grad_n1_other.astype(F32)
-    )
-
-    early_full = [cq_in_t, ckv_in_t, co_out_t, up_in_t, down_out_t]
-    early_part = [co_in_t, cq_out_t, ckv_out_t]
-    late_full = [q_in_t, kv_in_t, so_out_t]
-    late_part = [so_in_t, q_out_t, kv_out_t]
-    broad = [up_out_t, down_in_t]
-    regular = (
-        ctx_size == 2 and tp_size == 2 and rank == 16
-        and width == LANE * fsdp_size and wide == 4 * LANE * fsdp_size
-    )
+    full = [q_in_t, kv_in_t, cq_in_t, ckv_in_t, so_out_t, co_out_t, up_in_t, down_out_t]
+    part = [so_in_t, co_in_t, q_out_t, kv_out_t, cq_out_t, ckv_out_t]
     if regular:
-
-        def exchange(full, part, wides, order, tagged, name):
-            per_group = (len(order) + 3) // 4
-            count = 16 * (per_group + len(wides) + tagged)
-            dims = (2, fsdp_size, count, LANE)
-
-            def number(arrays):
-                return sum(1 if a.ndim == 2 else a.shape[0] for a in arrays)
-
-            def kernel(*refs):
-                pack_kernel(number(full), number(part), len(wides), order, tagged, *refs)
-
-            keep, send = call(
-                kernel,
-                1,
-                [whole(a) for a in full + part + wides],
-                [out(dims, F32), out(dims, F32)],
-                scalars=scalars,
-                name=name,
-            )
-            recv = swap(send, "ctx")
-
-            def pick(i):
-                return lax.dynamic_index_in_dim(keep, i, 0, keepdims=False) + (
-                    lax.dynamic_index_in_dim(recv, i, 0, keepdims=False)
-                )
-
-            away = swap(pick(1 - tensor_index).astype(BF), "tp")
-            total = (pick(tensor_index) + away.astype(F32)).astype(BF)
-            return lax.all_to_all(total, "fsdp", 0, 0, tiled=True)
-
-        early = exchange(
-            early_full, early_part, broad, (0, 1, 2, 6, 7, 8, 9, 3, 4, 5), 1, "pack_early"
-        )
-        late = exchange(late_full, late_part, [], (0, 1, 2, 4, 5, 6, 7, 3), 0, "pack_late")
+        order = (0, 1, 2, 10, 3, 4, 5, 11, 12, 13, 14, 6, 15, 16, 17, 7, 8, 9)
+        full[0], layer_out, grad_top_other = ordered(q_in_t, layer_out, grad_top_other)
+        kept, away = pack(full, part, [up_out_t, down_in_t], order, 1, "pack")
+        away, grad_low = ordered(swap(away, "tp"), grad_low)
+        parts = finish(kept, away)
         narrow_out = (attn_adapt_in.shape[0], adapters, rank, PIECE)
         tables = call(
             unpack_kernel,
             1,
-            [whole(early), whole(late)],
+            [whole(parts)],
             [
                 out(narrow_out, F32),
                 out(narrow_out, F32),
@@ -972,14 +976,49 @@
             )
 
         attn_in_t = summed(
-            late_full[:2] + [so_in_t] + early_full[:2] + [co_in_t], head_start, width
+            [q_in_t, kv_in_t, so_in_t, cq_in_t, ckv_in_t, co_in_t], head_start, width
         )
         attn_out_t = summed(
-            late_part[1:] + [so_out_t] + early_part[1:] + [co_out_t], head_start, width
+            [q_out_t, kv_out_t, so_out_t, cq_out_t, ckv_out_t, co_out_t], head_start, width
         )
         small = summed([up_in_t, down_out_t], head_start, width)
-        large = summed(broad, unit_start, wide)
+        large = summed([up_out_t, down_in_t], unit_start, wide)
         tables = (attn_in_t, attn_out_t, small[0], large[0], large[1], small[1])
+    grad_low, grad_low_other = with_other(grad_low, "tp")
+    def row_blocks(array, first=0):
+        block = (block_rows,) + array.shape[1:]
+        rest = (0,) * (array.ndim - 1)
+        return array, pl.BlockSpec(block, lambda i: (first + i, *rest))
+
+    total_shape = shape((frames, 1, width), F32)
+    steps = first_rows // block_rows
+    (grad_encoder,) = call(
+        add_rows_kernel,
+        steps,
+        [row_blocks(grad_top), row_blocks(grad_top_other)],
+        [row_blocks(total_shape)],
+        name="encoder_top",
+    )
+    (grad_encoder,) = call(
+        add_rows_kernel,
+        -(-(frames - first_rows) // block_rows),
+        [
+            row_blocks(grad_low),
+            row_blocks(grad_low_other),
+            (grad_encoder, pl.BlockSpec(memory_space=pl.ANY)),
+        ],
+        [row_blocks(total_shape, steps)],
+        aliases={2: 0},
+        name="encoder_low",
+    )
+    grad_encoder = grad_encoder.reshape(frames, width)
+    (grad_hidden,) = call(
+        close_kernel,
+        1,
+        [whole(a) for a in (hidden, ln_gains, grad_first, grad_n1, grad_n1_other)],
+        [out((rows, width), F32)],
+        name="hidden_total",
+    )
     return (
         layer_out[None],
         grad_hidden[None],

time: 321 us -> 294 us (0.916)
  waiting for transfers between devices: 153 us -> 137 us
  starting transfers between devices: 19.9 us -> 14.9 us
  other arithmetic: 9.84 us -> 6.31 us
    all_to_all x2 -> x1, waiting for transfers between devices: 12.8 us -> 0.01 us  [finish(): lax.all_to_all((kept + away.astype(F32)).astype(BF), 'fsdp', 0, 0, tiled=...]
    all_to_all x2 -> x1, starting transfers between devices: 6.74 us -> 3.41 us  [finish(): lax.all_to_all((kept + away.astype(F32)).astype(BF), 'fsdp', 0, 0, tiled=...]
    pallas_call x13 -> x14, Pallas kernels: 106 us -> 104 us  [call(): return run(*arrays) if scalars is None else run(scalars, *arrays)]
    ppermute x16 -> x14, starting transfers between devices: 13.1 us -> 11.4 us  [swap(): return lax.ppermute(value, axis, [(0, 1), (1, 0)])]
    ppermute x16 -> x14, waiting for transfers between devices: 46.7 us -> 45.2 us  [swap(): return lax.ppermute(value, axis, [(0, 1), (1, 0)])]
  transfers between devices with their start and end apart: 20 -> 17, of which waited for: 9 -> 10; matrix products, arithmetic and copies ran while one was open for 5% -> 4% of each run, Pallas kernels for 23% -> 29%
where the time goes in v2:
time: 294 us; the launch traced here: 293 us
  waiting for transfers between devices  137 us (47%)
  Pallas kernels  104 us (35%)
  local copies, waits for them, and re-layouts  15.6 us (5%)
  starting transfers between devices  14.9 us (5%)
  between operations  14.9 us (5%)
  other arithmetic  6.31 us (2%)
    pallas_call x14, Pallas kernels, call(): return run(*arrays) if scalars is None else run(scalars, *arrays)  104 us
    all_gather x1, waiting for transfers between devices, on_device(): attn_full = lax.all_gather(attn_half, ('fsdp', 'ctx'), axis=0)  73.5 us
    ppermute x14, waiting for transfers between devices, swap(): return lax.ppermute(value, axis, [(0, 1), (1, 0)])  45.2 us
    all_gather x1, waiting for transfers between devices, on_device(): ff_full = lax.all_gather(ff_half, ('fsdp', 'ctx'), axis=0)  18.7 us
    ppermute x14, starting transfers between devices, swap(): return lax.ppermute(value, axis, [(0, 1), (1, 0)])  11.4 us
  transfers between devices with their start and end apart: 17, of which 10 were waited for; matrix products, arithmetic and copies ran while one was open for 4% of the time, Pallas kernels for 29%

profile of v2, /device:TPU:0, one launch (start us, length us, event | category | flops | bytes accessed | tf_op | source)
XLA Modules:
  0.0 293.0 jit_solution(15749943226039962119)
XLA Ops:
  11.9 1.7 dynamic-slice_bitcast_fusion.5.low_out.query_out.refs_10_
  14.3 73.5 %all-gather.5.cloned.1.call-done = bf16[128,64,512]{2,1,0:T(8,128)(2,1)} async-done(((bf16[8,64,512]{2,1,0:T(8,128)(2,1)}), bf16[128,64,512]{2,1,0:T(8,128)(2,1)}) %all-gather.5.cloned.1.call-update) | async-done | bytes 8388624 | tf_op jit(solution)/shard_map/all_gather | solution.py:581
  87.8 7.1 %frames.1 = (bf16[2,752,512]{2,1,0:T(8,128)(2,1)}, bf16[2,750,16]{2,1,0:T(8,128)(2,1)}) custom-call(bf16[750,1024]{1,0:T(8,128)(2,1)} %bitcast.55, bf16[16,8,64,512]{3,2,1,0:T(8,128)(2,1)} %bitcast.41, bf16[8,16,1024]{2,1,0:T(8,128)(2,1)} %dynamic-slice_bitcast_fusion.3.low_in.query_in.refs_9_, ...), custom_call_target="tpu_custom_call" | custom-call | flops 70000000 | bytes 258300 | tf_op jit(solution)/shard_map/frames/pallas_call | solution.py:529
  95.2 5.8 %qkv.1 = (bf16[224,1024]{1,0:T(8,128)(2,1)}, bf16[224,512]{1,0:T(8,128)(2,1)}, bf16[2,224,512]{2,1,0:T(8,128)(2,1)}, bf16[3,224,16]{2,1,0:T(8,128)(2,1)}) custom-call(bf16[224,1024]{1,0:T(8,128)(2,1)} %bitcast.57, f32[3,1024]{1,0:T(4,128)} %gains.9, bf16[16,8,64,512]{3,2,1,0:T(8,128)(2,1)} %bitcast.42, ...), custom_call_target="tpu_custom_call" | custom-call | flops 50000000 | bytes 184500 | tf_op jit(solution)/shard_map/qkv/pallas_call | solution.py:529
  102.7 1.7 dynamic-slice_bitcast_fusion.2.low_out.refs_7_
  105.2 7.2 %self_attention.1 = (bf16[224,512]{1,0:T(8,128)(2,1)}, f32[4,2,224]{2,1,0:T(2,128)}, bf16[224,1024]{1,0:T(8,128)(2,1)}, bf16[224,16]{1,0:T(8,128)(2,1)}) custom-call(s32[3]{0:T(128)} %pad_add_fusion.where.refs_0_, bf16[224,512]{1,0:T(8,128)(2,1)} %get-tuple-element.78.query.refs_11_, bf16[2,224,512]{2,1,0:T(8,128)(2,1)} %get-tuple-element.79.mine.refs_13_, ...), custom_call_target="tpu_custom_call" | custom-call | flops 70000000 | bytes 258300 | tf_op jit(solution)/shard_map/self_attention/pallas_call | solution.py:529
  112.4 1.6 collective-permute-start.1
  114.0 11.3 %collective-permute-done.1.branch_other = bf16[224,1024]{1,0:T(8,128)(2,1)S(1)} collective-permute-done((bf16[224,1024]{1,0:T(8,128)(2,1)}, bf16[224,1024]{1,0:T(8,128)(2,1)S(1)}, u32[]{:S(2)}, u32[]{:S(2)}) %collective-permute-start.1) | collective-permute-done | bytes 458784 | tf_op jit(solution)/shard_map/ppermute | solution.py:51
  126.1 14.1 %cross_attention.1 = (f32[224,1024]{1,0:T(8,128)}, bf16[224,1024]{1,0:T(8,128)(2,1)}, bf16[224,512]{1,0:T(8,128)(2,1)}, bf16[224,16]{1,0:T(8,128)(2,1)}, bf16[22...) custom-call(bf16[224,1024]{1,0:T(8,128)(2,1)} %bitcast.58, ...), custom_call_target="tpu_custom_call" | custom-call | flops 130000000 | bytes 479700 | tf_op jit(solution)/shard_map/cross_attention/pallas_call | solution.py:529
  140.2 1.6 collective-permute-start.3
  143.2 1.5 dynamic-slice_bitcast_fusion.6
  144.7 18.7 %all-gather.7.cloned.1.call-done = bf16[32,64,2048]{2,1,0:T(8,128)(2,1)} async-done(((bf16[2,64,2048]{2,1,0:T(8,128)(2,1)}), bf16[32,64,2048]{2,1,0:T(8,128)(2,1)}) %all-gather.7.cloned.1.call-update) | async-done | bytes 8388624 | tf_op jit(solution)/shard_map/all_gather | solution.py:582
  164.2 11.6 %units.1 = (f32[224,1024]{1,0:T(8,128)}, bf16[224,1024]{1,0:T(8,128)(2,1)}, bf16[224,1024]{1,0:T(8,128)(2,1)}, f32[16,1024]{1,0:T(8,128)}, f32[16,2048]{1,0:T(8,...) custom-call(f32[224,1024]{1,0:T(8,128)} %get-tuple-element.82.middle.refs_1_, ...), custom_call_target="tpu_custom_call" | custom-call | flops 110000000 | bytes 405900 | tf_op jit(solution)/shard_map/units/pallas_call | solution.py:529
  175.8 1.6 collective-permute-start.4
  177.4 11.4 %collective-permute-done.4.grad_other = bf16[224,1024]{1,0:T(8,128)(2,1)S(1)} collective-permute-done((bf16[224,1024]{1,0:T(8,128)(2,1)}, bf16[224,1024]{1,0:T(8,128)(2,1)S(1)}, u32[]{:S(2)}, u32[]{:S(2)}) %collective-permute-start.4) | collective-permute-done | bytes 458784 | tf_op jit(solution)/shard_map/ppermute | solution.py:51
  188.8 1.5 collective-permute-start.5
  190.2 15.0 %cross_back.1 = (f32[224,1024]{1,0:T(8,128)}, bf16[224,1024]{1,0:T(8,128)(2,1)}, bf16[2,752,512]{2,1,0:T(8,128)(2,1)}, bf16[2,752,512]{2,1,0:T(8,128)(2,1)}, f32...) custom-call(bf16[224,1024]{1,0:T(8,128)(2,1)} %bitcast.61, ...), custom_call_target="tpu_custom_call" | custom-call | flops 180000000 | bytes 664200 | tf_op jit(solution)/shard_map/cross_back/pallas_call | solution.py:529
  206.1 2.8 collective-permute-done.6.grad_other
  210.0 8.4 %frames_back.1 = (bf16[512,1024]{1,0:T(8,128)(2,1)}, bf16[238,1024]{1,0:T(8,128)(2,1)}, f32[2,16,1024]{2,1,0:T(8,128)}, f32[2,16,512]{2,1,0:T(8,128)}) custom-call(bf16[2,752,512]{2,1,0:T(8,128)(2,1)} %get-tuple-element.99.grad_mine, bf16[2,752,512]{2,1,0:T(8,128)(2,1)} %copy-done.4, bf16[16,8,64,512]{3,2,1,0:T(8,128)(2,1)} %bitcast.48, ...), custom_call_target="tpu_custom_call" | custom-call | flops 90000000 | bytes 332100 | tf_op jit(solution)/shard_map/frames_back/pallas_call | solution.py:529
  219.3 12.2 %self_back.1 = (f32[224,1024]{1,0:T(8,128)}, f32[224,1024]{1,0:T(8,128)}, bf16[2,224,512]{2,1,0:T(8,128)(2,1)}, bf16[2,224,512]{2,1,0:T(8,128)(2,1)}, f32[16,512...) custom-call(s32[3]{0:T(128)} %pad_add_fusion.where.refs_0_, ...), custom_call_target="tpu_custom_call" | custom-call | flops 120000000 | bytes 442800 | tf_op jit(solution)/shard_map/self_back/pallas_call | solution.py:529
  234.4 4.6 %self_project_back.1 = (bf16[224,1024]{1,0:T(8,128)(2,1)}, f32[2,16,1024]{2,1,0:T(8,128)}, f32[2,16,512]{2,1,0:T(8,128)}) custom-call(bf16[2,224,512]{2,1,0:T(8,128)(2,1)} %get-tuple-element.115.grad_mine, bf16[2,224,512]{2,1,0:T(8,128)(2,1)} %copy-done.13, bf16[16,8,64,512]{3,2,1,0:T(8,128)(2,1)} %bitcast.51, ...), custom_call_target="tpu_custom_call" | custom-call | flops 50000000 | bytes 184500 | tf_op jit(solution)/shard_map/self_project_back/pallas_call | solution.py:529
  239.0 5.0 %collective-permute-done.8.other = bf16[512,1024]{1,0:T(8,128)(2,1)S(1)} collective-permute-done((bf16[512,1024]{1,0:T(8,128)(2,1)}, bf16[512,1024]{1,0:T(8,128)(2,1)S(1)}, u32[]{:S(2)}, u32[]{:S(2)}) %collective-permute-start.8) | collective-permute-done | bytes 1048608 | tf_op jit(solution)/shard_map/ppermute | solution.py:51
  244.0 5.2 %pack.1 = (f32[2,8,128,128]{3,2,1,0:T(8,128)}, f32[2,8,128,128]{3,2,1,0:T(8,128)}) custom-call(s32[3]{0:T(128)} %pad_add_fusion.where.refs_0_, f32[16,1024]{1,0:T(8,128)} %get-tuple-element.119.refs_1_, f32[2,16,1024]{2,1,0:T(8,128)} %get-tuple-element.120.refs_2_, f32[16,1024]{1,0:T(8,128)} %get-tuple-element.121.refs_3_, ...), custom_call_target="tpu_custom_call" | custom-call | flops 50000000 | bytes 184500 | tf_op jit(solution)/shard_map/pack/pallas_call | solution.py:529
  249.1 2.9 collective-permute-done.11
  255.2 7.3 %collective-permute-done.12 = bf16[8,128,128]{2,1,0:T(8,128)(2,1)} collective-permute-done((bf16[8,128,128]{2,1,0:T(8,128)(2,1)S(1)}, bf16[8,128,128]{2,1,0:T(8,128)(2,1)}, u32[]{:S(2)}, u32[]{:S(2)}) %collective-permute-start.12) | collective-permute-done | bytes 262176 | tf_op jit(solution)/shard_map/ppermute | solution.py:51
  263.2 1.9 fusion
  265.1 3.4 %all-to-all-start = ((bf16[8,128,128]{2,1,0:T(8,128)(2,1)}), bf16[8,128,128]{2,1,0:T(8,128)(2,1)S(1)}, u32[]{:S(2)}, u32[]{:S(2)}) async-start(bf16[8,128,128]{2,1,0:T(8,128)(2,1)} %fusion), calls=%async_computation | async-start | bytes 524288 | tf_op jit(solution)/shard_map/all_to_all | solution.py:670
  268.5 3.7 %collective-permute-done.10.grad_other = bf16[224,1024]{1,0:T(8,128)(2,1)S(1)} collective-permute-done((bf16[224,1024]{1,0:T(8,128)(2,1)S(1)}, bf16[224,1024]{1,0:T(8,128)(2,1)S(1)}, u32[]{:S(2)}, u32[]{:S(2)}) %collective-permute-start.10) | collective-permute-done | bytes 458784 | tf_op jit(solution)/shard_map/ppermute | solution.py:51
  272.9 3.2 %hidden_total.1 = f32[224,1024]{1,0:T(8,128)} custom-call(bf16[224,1024]{1,0:T(8,128)(2,1)} %bitcast.59, f32[3,1024]{1,0:T(4,128)} %gains.9, f32[224,1024]{1,0:T(8,128)} %get-tuple-element.114.carried, bf16[224,1024]{1,0:T(8,128)(2,1)} %get-tuple-element.118.grad_mine, bf16[224,1024]{1,0:T(8,128)(2,1)} %copy-done.9), custom_call_target="tpu_custom_call" | custom-call | flops 50000000 | bytes 184500 | tf_op jit(solution)/shard_map/hidden_total/pallas_call | solution.py:529
  276.1 4.0 %encoder_top.1.refs_0_ = f32[750,1,1024]{2,1,0:T(1,128)} custom-call(bf16[512,1024]{1,0:T(8,128)(2,1)} %get-tuple-element.112.mine, bf16[512,1024]{1,0:T(8,128)(2,1)} %copy-done.5), custom_call_target="tpu_custom_call" | custom-call | flops 50000000 | bytes 184500 | tf_op jit(solution)/shard_map/encoder_top/pallas_call | solution.py:529
  280.8 3.2 %unpack.1 = (f32[8,8,16,32]{3,2,1,0:T(8,128)}, f32[8,8,16,32]{3,2,1,0:T(8,128)}, f32[8,16,32]{2,1,0:T(8,128)}, f32[8,16,128]{2,1,0:T(8,128)}, f32[8,16,128]{2,1,0:T(8,128)}, /*index=5*/f32[8,16,32]{2,1,0:T(8,128)}) custom-call(bf16[8,128,128]{2,1,0:T(8,128)(2,1)} %copy-done.6), custom_call_target="tpu_custom_call" | custom-call | flops 50000000 | bytes 184500 | tf_op jit(solution)/shard_map/unpack/pallas_call | solution.py:529
  284.0 2.1 encoder_low.1
  (67 shorter events, 21.5 us)
Async XLA Ops:
  7.2 6.4 %copy-start = (bf16[8,8,16,1024]{3,2,1,0:T(8,128)(2,1)S(1)}, bf16[8,8,16,1024]{3,2,1,0:T(8,128)(2,1)}, u32[]{:S(2)}) copy-start(bf16[8,8,16,1024]{3,2,1,0:T(8,128)(2,1)} %param.24) | copy-start | bytes 6291460
  7.2 3.1 %copy-start.16 = (bf16[128,2048]{1,0:T(8,128)(2,1)S(1)}, bf16[128,2048]{1,0:T(8,128)(2,1)}, u32[]{:S(2)}) copy-start(bf16[128,2048]{1,0:T(8,128)(2,1)} %param.22) | copy-start | bytes 1572868
  7.2 3.1 %copy-start.15 = (bf16[128,2048]{1,0:T(8,128)(2,1)S(1)}, bf16[128,2048]{1,0:T(8,128)(2,1)}, u32[]{:S(2)}) copy-start(bf16[128,2048]{1,0:T(8,128)(2,1)} %param.23) | copy-start | bytes 1572868
  7.2 80.6 %all-gather.5.cloned.1.call-start = ((), (), s32[]{:S(2)}) async-start(), calls=%async_computation.1 | async-start | bytes 8912896 | tf_op jit(solution)/shard_map/all_gather | solution.py:581
  10.2 153.2 %all-gather.7.cloned.1.call-start = ((), (), s32[]{:S(2)}) async-start(), calls=%async_computation.2 | async-start | bytes 8912896 | tf_op jit(solution)/shard_map/all_gather | solution.py:582
  94.9 30.4 %collective-permute-start.2 = (bf16[2,752,512]{2,1,0:T(8,128)(2,1)}, bf16[2,752,512]{2,1,0:T(8,128)(2,1)}, u32[]{:S(2)}, u32[]{:S(2)}) collective-permute-start(bf16[2,752,512]{2,1,0:T(8,128)(2,1)} %get-tuple-element.81.mine), channel_id=1, source_target_pairs={{0,2},{2,0},{1,3},{3,1},{4,6},{6,4},{5,7},{7,5},{8,10},{10,8},{9,1... | collective-permute-start | bytes 4620296 | tf_op jit(solution)/shard_map/ppermute | solution.py:51
  101.0 3.4 %collective-permute-start = (bf16[2,224,512]{2,1,0:T(8,128)(2,1)}, bf16[2,224,512]{2,1,0:T(8,128)(2,1)S(1)}, u32[]{:S(2)}, u32[]{:S(2)}) collective-permute-start(bf16[2,224,512]{2,1,0:T(8,128)(2,1)} %get-tuple-element.79.mine.refs_13_), channel_id=1, source_target_pairs={{0,2},{2,0},{1,3},{3,1},{4,6},{6,4},{5,7},{7,5},{8,10},{10,8},{9,1... | collective-permute-start | bytes 1376264 | tf_op jit(solution)/shard_map/ppermute | solution.py:51
  104.4 0.8 copy-start.3
  112.4 12.9 %collective-permute-start.1 = (bf16[224,1024]{1,0:T(8,128)(2,1)}, bf16[224,1024]{1,0:T(8,128)(2,1)S(1)}, u32[]{:S(2)}, u32[]{:S(2)}) collective-permute-start(bf16[224,1024]{1,0:T(8,128)(2,1)} %get-tuple-element.80.branch_mine), channel_id=1, source_target_pairs={{0,1},{1,0},{2,3},{3,2},{4,5},{5,4},{6,7},{7,6},{8,9},{9,8},{10,11... | collective-permute-start | bytes 1376264 | tf_op jit(solution)/shard_map/ppermute | solution.py:51
  125.3 0.8 copy-start.14
  140.2 23.2 %collective-permute-start.3 = (bf16[224,1024]{1,0:T(8,128)(2,1)}, bf16[224,1024]{1,0:T(8,128)(2,1)S(1)}, u32[]{:S(2)}, u32[]{:S(2)}) collective-permute-start(bf16[224,1024]{1,0:T(8,128)(2,1)} %get-tuple-element.83.branch_mine), channel_id=1, source_target_pairs={{0,1},{1,0},{2,3},{3,2},{4,5},{5,4},{6,7},{7,6},{8,9},{9,8},{10,11... | collective-permute-start | bytes 1376264 | tf_op jit(solution)/shard_map/ppermute | solution.py:51
  163.5 0.8 copy-start.12
  175.8 13.0 %collective-permute-start.4 = (bf16[224,1024]{1,0:T(8,128)(2,1)}, bf16[224,1024]{1,0:T(8,128)(2,1)S(1)}, u32[]{:S(2)}, u32[]{:S(2)}) collective-permute-start(bf16[224,1024]{1,0:T(8,128)(2,1)} %get-tuple-element.85.grad_mine), channel_id=1, source_target_pairs={{0,1},{1,0},{2,3},{3,2},{4,5},{5,4},{6,7},{7,6},{8,9},{9,8},{10,11... | collective-permute-start | bytes 1376264 | tf_op jit(solution)/shard_map/ppermute | solution.py:51
  188.8 1.5 copy-start.7
  188.8 16.5 %collective-permute-start.5 = (bf16[224,1024]{1,0:T(8,128)(2,1)}, bf16[224,1024]{1,0:T(8,128)(2,1)S(1)}, u32[]{:S(2)}, u32[]{:S(2)}) collective-permute-start(bf16[224,1024]{1,0:T(8,128)(2,1)} %get-tuple-element.97), channel_id=1, source_target_pairs={{0,1},{1,0},{2,3},{3,2},{4,5},{5,4},{6,7},{7,6},{8,9},{9,8},{10,11... | collective-permute-start | bytes 1376264 | tf_op jit(solution)/shard_map/ppermute | solution.py:51
  205.3 3.6 %collective-permute-start.6 = (bf16[2,752,512]{2,1,0:T(8,128)(2,1)}, bf16[2,752,512]{2,1,0:T(8,128)(2,1)S(1)}, u32[]{:S(2)}, u32[]{:S(2)}) collective-permute-start(bf16[2,752,512]{2,1,0:T(8,128)(2,1)} %get-tuple-element.100), channel_id=1, source_target_pairs={{0,2},{2,0},{1,3},{3,1},{4,6},{6,4},{5,7},{7,5},{8,10},{10,8},{9,1... | collective-permute-start | bytes 4620296 | tf_op jit(solution)/shard_map/ppermute | solution.py:51
  205.3 13.1 %collective-permute-start.7 = (bf16[224,1024]{1,0:T(8,128)(2,1)}, bf16[224,1024]{1,0:T(8,128)(2,1)S(1)}, u32[]{:S(2)}, u32[]{:S(2)}) collective-permute-start(bf16[224,1024]{1,0:T(8,128)(2,1)} %get-tuple-element.98.refs_3_), channel_id=1, source_target_pairs={{0,1},{1,0},{2,3},{3,2},{4,5},{5,4},{6,7},{7,6},{8,9},{9,8},{10,11... | collective-permute-start | bytes 1376264 | tf_op jit(solution)/shard_map/ppermute | solution.py:51
  208.9 1.1 copy-start.4
  218.5 0.8 copy-start.11
  218.5 25.5 %collective-permute-start.8 = (bf16[512,1024]{1,0:T(8,128)(2,1)}, bf16[512,1024]{1,0:T(8,128)(2,1)S(1)}, u32[]{:S(2)}, u32[]{:S(2)}) collective-permute-start(bf16[512,1024]{1,0:T(8,128)(2,1)} %get-tuple-element.112.mine), channel_id=1, source_target_pairs={{0,1},{1,0},{2,3},{3,2},{4,5},{5,4},{6,7},{7,6},{8,9},{9,8},{10,11... | collective-permute-start | bytes 3145736 | tf_op jit(solution)/shard_map/ppermute | solution.py:51
  219.3 12.4 %copy-start.2 = (f32[224,1024]{1,0:T(8,128)S(1)}, f32[224,1024]{1,0:T(8,128)}, u32[]{:S(2)}) copy-start(f32[224,1024]{1,0:T(8,128)} %get-tuple-element.84.rows) | copy-start | bytes 2752516
  219.3 12.4 %copy-start.10 = (bf16[224,1024]{1,0:T(8,128)(2,1)S(1)}, bf16[224,1024]{1,0:T(8,128)(2,1)}, u32[]{:S(2)}) copy-start(bf16[224,1024]{1,0:T(8,128)(2,1)} %get-tuple-element.97) | copy-start | bytes 1376260
  231.5 2.1 collective-permute-start.9
  239.0 14.9 %copy-start.8 = (bf16[224,1024]{1,0:T(8,128)(2,1)S(1)}, bf16[224,1024]{1,0:T(8,128)(2,1)}, u32[]{:S(2)}) copy-start(bf16[224,1024]{1,0:T(8,128)(2,1)} %get-tuple-element.118.grad_mine) | copy-start | bytes 1376260
  244.0 21.1 %copy-start.5 = (bf16[512,1024]{1,0:T(8,128)(2,1)}, bf16[512,1024]{1,0:T(8,128)(2,1)S(1)}, u32[]{:S(2)}) copy-start(bf16[512,1024]{1,0:T(8,128)(2,1)S(1)} %collective-permute-done.8.other) | copy-start | bytes 3145732
  249.1 2.9 collective-permute-start.11
  253.1 9.3 %collective-permute-start.12 = (bf16[8,128,128]{2,1,0:T(8,128)(2,1)S(1)}, bf16[8,128,128]{2,1,0:T(8,128)(2,1)}, u32[]{:S(2)}, u32[]{:S(2)}) collective-permute-start(bf16[8,128,128]{2,1,0:T(8,128)(2,1)S(1)} %fusion.1), channel_id=1, source_target_pairs={{0,1},{1,0},{2,3},{3,2},{4,5},{5,4},{6,7},{7,6},{8,9},{9,8},{10,11... | collective-permute-start | bytes 786440 | tf_op jit(solution)/shard_map/ppermute | solution.py:51
  253.9 18.3 %collective-permute-start.10 = (bf16[224,1024]{1,0:T(8,128)(2,1)S(1)}, bf16[224,1024]{1,0:T(8,128)(2,1)S(1)}, u32[]{:S(2)}, u32[]{:S(2)}) collective-permute-start(bf16[224,1024]{1,0:T(8,128)(2,1)S(1)} %copy-done.8), channel_id=1, source_target_pairs={{0,1},{1,0},{2,3},{3,2},{4,5},{5,4},{6,7},{7,6},{8,9},{9,8},{10,11... | collective-permute-start | bytes 1376264 | tf_op jit(solution)/shard_map/ppermute | solution.py:51
  262.5 21.6 %collective-permute-start.13 = (bf16[238,1024]{1,0:T(8,128)(2,1)}, bf16[238,1024]{1,0:T(8,128)(2,1)}, u32[]{:S(2)}, u32[]{:S(2)}) collective-permute-start(bf16[238,1024]{1,0:T(8,128)(2,1)} %get-tuple-element.138.mine), channel_id=1, source_target_pairs={{0,1},{1,0},{2,3},{3,2},{4,5},{5,4},{6,7},{7,6},{8,9},{9,8},{10,11... | collective-permute-start | bytes 1462280 | tf_op jit(solution)/shard_map/ppermute | solution.py:51
  265.1 15.0 %all-to-all-start = ((bf16[8,128,128]{2,1,0:T(8,128)(2,1)}), bf16[8,128,128]{2,1,0:T(8,128)(2,1)S(1)}, u32[]{:S(2)}, u32[]{:S(2)}) async-start(bf16[8,128,128]{2,1,0:T(8,128)(2,1)} %fusion), calls=%async_computation | async-start | bytes 524288 | tf_op jit(solution)/shard_map/all_to_all | solution.py:670
  272.2 0.8 copy-start.9
  280.8 5.4 %copy-start.1 = (bf16[8,8,16,1024]{3,2,1,0:T(8,128)(2,1)S(1)}, bf16[8,8,16,1024]{3,2,1,0:T(8,128)(2,1)}, u32[]{:S(2)}) copy-start(bf16[8,8,16,1024]{3,2,1,0:T(8,128)(2,1)} %param.24) | copy-start | bytes 6291460
  (2 other events, 1.5 us)
Sparse Core Ops, SparseCore 0:
  10.8 77.0 all-gather.4
  90.5 72.8 all-gather.6

commit v3 on v2

--- a/solution.py
+++ b/solution.py
@@ -245,20 +245,25 @@
         branch[...] = (acc[...] + mm(rank_rows, low_out[0])).astype(BF)
 
 
+def third_norm_kernel(
+    middle, branch_mine, branch_other, gains, cotangent, up_in, down_out,
+    second, normed, up_low, down_back,
+):
+    total = middle[...] + (branch_mine[...].astype(F32) + branch_other[...].astype(F32))
+    second[...] = total
+    rows = normalize(total, gains[2:3, :]).astype(BF)
+    normed[...] = rows
+    up_low[...] = mm_nt(rows, up_in[...]).astype(BF)
+    down_back[...] = mm_nt(cotangent[...], down_out[...]).astype(BF)
+
+
 def units_kernel(
-    middle, branch_mine, branch_other, gains, cotangent, up, down, up_in, up_out, down_in,
-    down_out,
-    second, branch, grad_normed, table_up_in, table_up_out, table_down_in, table_down_out,
-    normed, up_low, down_back, acc, back, low_acc, back_low,
+    normed, up_low, down_back, cotangent, up, down, up_in, up_out, down_in, down_out,
+    branch, grad_normed, table_up_in, table_up_out, table_down_in, table_down_out,
+    acc, back, low_acc, back_low,
 ):
     @at_first()
     def _():
-        total = middle[...] + (branch_mine[...].astype(F32) + branch_other[...].astype(F32))
-        second[...] = total
-        rows = normalize(total, gains[2:3, :]).astype(BF)
-        normed[...] = rows
-        up_low[...] = mm_nt(rows, up_in[...]).astype(BF)
-        down_back[...] = mm_nt(cotangent[...], down_out[...]).astype(BF)
         acc[...] = jnp.zeros_like(acc)
         back[...] = jnp.zeros_like(back)
         low_acc[...] = jnp.zeros_like(low_acc)
@@ -376,7 +381,7 @@
 
 
 def frames_back_kernel(
-    grad_mine, grad_other, weight, low_in, low_out, rows, low, top, rest, table_in, table_out, acc
+    grad_mine, grad_other, weight, low_in, low_out, rows, low, total, table_in, table_out, acc
 ):
     @at_first()
     def _():
@@ -388,9 +393,7 @@
 
     @at_last()
     def _():
-        count = top.shape[0]
-        top[...] = acc[:count].astype(BF)
-        rest[...] = acc[count:].astype(BF)
+        total[...] = acc[...].astype(BF)
 
 
 def pair_project_step(
@@ -642,7 +645,7 @@
     def ordered(first, *others):
         return lax.optimization_barrier((first, *others))
 
-    def pack(full, part, wides, order, tagged, name):
+    def pack(full, part, wides, order, tagged, name, after):
         count = 16 * ((len(order) + 3) // 4 + len(wides) + tagged)
         dims = (2, fsdp_size, count, LANE)
 
@@ -657,14 +660,14 @@
             scalars=scalars,
             name=name,
         )
-        recv = swap(send, "ctx")
+        recv, after = ordered(swap(send, "ctx"), after)
 
         def pick(i):
             return lax.dynamic_index_in_dim(keep, i, 0, keepdims=False) + (
                 lax.dynamic_index_in_dim(recv, i, 0, keepdims=False)
             )
 
-        return pick(tensor_index), pick(1 - tensor_index).astype(BF)
+        return pick(tensor_index), pick(1 - tensor_index).astype(BF), after
 
     def finish(kept, away):
         return lax.all_to_all((kept + away.astype(F32)).astype(BF), "fsdp", 0, 0, tiled=True)
@@ -776,14 +779,30 @@
     def unit_cols(array):
         return array, pl.BlockSpec((rank, chunk), lambda i: (0, i))
 
-    second_mid, branch, grad_n3, up_in_t, up_out_t, down_in_t, down_out_t = call(
+    second_mid, n3, up_low, down_back = call(
+        third_norm_kernel,
+        1,
+        [
+            whole(a)
+            for a in (
+                first_mid, branch, branch_other, ln_gains, cotangent, up_in, down_out
+            )
+        ],
+        [
+            out((rows, width), F32),
+            out((rows, width), BF),
+            out((rows, rank), BF),
+            out((rows, rank), BF),
+        ],
+        name="third_norm",
+    )
+    branch, grad_n3, up_in_t, up_out_t, down_in_t, down_out_t = call(
         units_kernel,
         units // chunk,
         [
-            whole(first_mid),
-            whole(branch),
-            whole(branch_other),
-            whole(ln_gains),
+            whole(n3),
+            whole(up_low),
+            whole(down_back),
             whole(cotangent),
             unit_weight(0),
             unit_weight(1),
@@ -793,7 +812,6 @@
             whole(down_out),
         ],
         [
-            out((rows, width), F32),
             out((rows, width), BF),
             out((rows, width), BF),
             out((rank, width), F32),
@@ -801,15 +819,7 @@
             unit_cols(shape((rank, units), F32)),
             out((rank, width), F32),
         ],
-        [
-            pltpu.VMEM((rows, width), BF),
-            rank_keep,
-            rank_keep,
-            wide_acc,
-            wide_acc,
-            rank_acc,
-            rank_acc,
-        ],
+        [wide_acc, wide_acc, rank_acc, rank_acc],
         name="units",
         cost=11,
     )
@@ -879,8 +889,7 @@
         second_mid + (branch.astype(F32) + branch_other.astype(F32))
     ).astype(BF)
     block_rows = 128
-    first_rows = (frames * 3 // 4) // block_rows * block_rows
-    grad_top, grad_low, ckv_in_t, ckv_out_t = call(
+    grad_frames, ckv_in_t, ckv_out_t = call(
         frames_back_kernel,
         2,
         [
@@ -893,8 +902,7 @@
             at(frames_low),
         ],
         [
-            out((first_rows, width), BF),
-            out((frames - first_rows, width), BF),
+            out((frames, width), BF),
             at(shape((2, rank, width), F32)),
             at(shape((2, rank, cols), F32)),
         ],
@@ -902,10 +910,8 @@
         name="frames_back",
         cost=9,
     )
-    grad_top, grad_low, grad_n2_other = lax.optimization_barrier(
-        (grad_top, grad_low, grad_n2_other)
-    )
-    grad_top, grad_top_other = with_other(grad_top, "tp")
+    grad_frames, grad_n2_other = ordered(grad_frames, grad_n2_other)
+    grad_frames, grad_frames_other = with_other(grad_frames, "tp")
     grad_first, grad_n1_start, grad_skv, grad_skv_send, so_in_t, so_out_t, q_in_t, q_out_t = back_call(
         partial(self_back_kernel, rows), scalars, grad_second, first_mid, grad_n2, grad_n2_other, (6, 3, 0, 0),
         query, self_mixed, self_kv, self_kv_other, self_logsum, n1, self_low,
@@ -934,13 +940,33 @@
         name="self_project_back",
     )
     grad_n1, grad_n1_other = with_other(grad_n1, "tp")
+    def row_blocks(array):
+        rest = (0,) * (array.ndim - 1)
+        return array, pl.BlockSpec((block_rows,) + array.shape[1:], lambda i: (i, *rest))
+
+    block_rows = 256
+    encoder_args = (
+        add_rows_kernel,
+        -(-frames // block_rows),
+        [row_blocks(grad_frames)],
+        [row_blocks(shape((frames, 1, width), F32))],
+    )
+
+    def encoder_total(other):
+        kernel, steps, ins, outs = encoder_args
+        (total,) = call(kernel, steps, ins + [row_blocks(other)], outs, name="encoder_total")
+        return total
+
     full = [q_in_t, kv_in_t, cq_in_t, ckv_in_t, so_out_t, co_out_t, up_in_t, down_out_t]
     part = [so_in_t, co_in_t, q_out_t, kv_out_t, cq_out_t, ckv_out_t]
     if regular:
         order = (0, 1, 2, 10, 3, 4, 5, 11, 12, 13, 14, 6, 15, 16, 17, 7, 8, 9)
-        full[0], layer_out, grad_top_other = ordered(q_in_t, layer_out, grad_top_other)
-        kept, away = pack(full, part, [up_out_t, down_in_t], order, 1, "pack")
-        away, grad_low = ordered(swap(away, "tp"), grad_low)
+        full[0], layer_out = ordered(q_in_t, layer_out)
+        kept, away, grad_frames_other = pack(
+            full, part, [up_out_t, down_in_t], order, 1, "pack", grad_frames_other
+        )
+        grad_encoder = encoder_total(grad_frames_other)
+        away, grad_encoder = ordered(swap(away, "tp"), grad_encoder)
         parts = finish(kept, away)
         narrow_out = (attn_adapt_in.shape[0], adapters, rank, PIECE)
         tables = call(
@@ -958,6 +984,7 @@
             name="unpack",
         )
     else:
+        grad_encoder = encoder_total(grad_frames_other)
         chosen = (mine == jnp.arange(adapters, dtype=jnp.int32)).astype(F32)
 
         def summed(parts, start, full):
@@ -984,33 +1011,6 @@
         small = summed([up_in_t, down_out_t], head_start, width)
         large = summed([up_out_t, down_in_t], unit_start, wide)
         tables = (attn_in_t, attn_out_t, small[0], large[0], large[1], small[1])
-    grad_low, grad_low_other = with_other(grad_low, "tp")
-    def row_blocks(array, first=0):
-        block = (block_rows,) + array.shape[1:]
-        rest = (0,) * (array.ndim - 1)
-        return array, pl.BlockSpec(block, lambda i: (first + i, *rest))
-
-    total_shape = shape((frames, 1, width), F32)
-    steps = first_rows // block_rows
-    (grad_encoder,) = call(
-        add_rows_kernel,
-        steps,
-        [row_blocks(grad_top), row_blocks(grad_top_other)],
-        [row_blocks(total_shape)],
-        name="encoder_top",
-    )
-    (grad_encoder,) = call(
-        add_rows_kernel,
-        -(-(frames - first_rows) // block_rows),
-        [
-            row_blocks(grad_low),
-            row_blocks(grad_low_other),
-            (grad_encoder, pl.BlockSpec(memory_space=pl.ANY)),
-        ],
-        [row_blocks(total_shape, steps)],
-        aliases={2: 0},
-        name="encoder_low",
-    )
     grad_encoder = grad_encoder.reshape(frames, width)
     (grad_hidden,) = call(
         close_kernel,

time: 294 us -> 288 us (0.980)
  waiting for transfers between devices: 137 us -> 133 us
    all_gather x1, waiting for transfers between devices: 18.7 us -> 7.31 us  [on_device(): ff_full = lax.all_gather(ff_half, ('fsdp', 'ctx'), axis=0)]
    ppermute x14 -> x13, waiting for transfers between devices: 45.2 us -> 49.8 us  [swap(): return lax.ppermute(value, axis, [(0, 1), (1, 0)])]
    ppermute x14 -> x13, starting transfers between devices: 11.4 us -> 10.7 us  [swap(): return lax.ppermute(value, axis, [(0, 1), (1, 0)])]
  transfers between devices with their start and end apart: 17 -> 16, of which waited for: 10 -> 13; matrix products, arithmetic and copies ran while one was open for 4% -> 4% of each run, Pallas kernels for 29% -> 32%
where the time goes in v3:
time: 288 us; the launch traced here: 287 us
  waiting for transfers between devices  133 us (46%)
  Pallas kernels  104 us (36%)
  local copies, waits for them, and re-layouts  14.9 us (5%)
  between operations  14.9 us (5%)
  starting transfers between devices  14.2 us (5%)
  other arithmetic  6.35 us (2%)
    pallas_call x14, Pallas kernels, call(): return run(*arrays) if scalars is None else run(scalars, *arrays)  104 us
    all_gather x1, waiting for transfers between devices, on_device(): attn_full = lax.all_gather(attn_half, ('fsdp', 'ctx'), axis=0)  73.5 us
    ppermute x13, waiting for transfers between devices, swap(): return lax.ppermute(value, axis, [(0, 1), (1, 0)])  49.8 us
    ppermute x13, starting transfers between devices, swap(): return lax.ppermute(value, axis, [(0, 1), (1, 0)])  10.7 us
    all_gather x1, waiting for transfers between devices, on_device(): ff_full = lax.all_gather(ff_half, ('fsdp', 'ctx'), axis=0)  7.31 us
  transfers between devices with their start and end apart: 16, of which 13 were waited for; matrix products, arithmetic and copies ran while one was open for 4% of the time, Pallas kernels for 32%

profile of v3, /device:TPU:0, one launch (start us, length us, event | category | flops | bytes accessed | tf_op | source)
XLA Modules:
  0.0 286.8 jit_solution(12182250393379754714)
XLA Ops:
  11.9 1.7 dynamic-slice_bitcast_fusion.5.low_out.query_out.refs_10_
  14.3 73.5 %all-gather.5.cloned.1.call-done = bf16[128,64,512]{2,1,0:T(8,128)(2,1)} async-done(((bf16[8,64,512]{2,1,0:T(8,128)(2,1)}), bf16[128,64,512]{2,1,0:T(8,128)(2,1)}) %all-gather.5.cloned.1.call-update) | async-done | bytes 8388624 | tf_op jit(solution)/shard_map/all_gather | solution.py:584
  87.8 7.1 %frames.1 = (bf16[2,752,512]{2,1,0:T(8,128)(2,1)}, bf16[2,750,16]{2,1,0:T(8,128)(2,1)}) custom-call(bf16[750,1024]{1,0:T(8,128)(2,1)} %bitcast.54, bf16[16,8,64,512]{3,2,1,0:T(8,128)(2,1)} %bitcast.41, bf16[8,16,1024]{2,1,0:T(8,128)(2,1)} %dynamic-slice_bitcast_fusion.3.low_in.query_in.refs_9_, ...), custom_call_target="tpu_custom_call" | custom-call | flops 70000000 | bytes 258300 | tf_op jit(solution)/shard_map/frames/pallas_call | solution.py:532
  95.2 5.8 %qkv.1 = (bf16[224,1024]{1,0:T(8,128)(2,1)}, bf16[224,512]{1,0:T(8,128)(2,1)}, bf16[2,224,512]{2,1,0:T(8,128)(2,1)}, bf16[3,224,16]{2,1,0:T(8,128)(2,1)}) custom-call(bf16[224,1024]{1,0:T(8,128)(2,1)} %bitcast.59, f32[3,1024]{1,0:T(4,128)} %gains.9, bf16[16,8,64,512]{3,2,1,0:T(8,128)(2,1)} %bitcast.42, ...), custom_call_target="tpu_custom_call" | custom-call | flops 50000000 | bytes 184500 | tf_op jit(solution)/shard_map/qkv/pallas_call | solution.py:532
  102.7 1.7 dynamic-slice_bitcast_fusion.2.low_out.refs_7_
  105.1 7.3 %self_attention.1 = (bf16[224,512]{1,0:T(8,128)(2,1)}, f32[4,2,224]{2,1,0:T(2,128)}, bf16[224,1024]{1,0:T(8,128)(2,1)}, bf16[224,16]{1,0:T(8,128)(2,1)}) custom-call(s32[3]{0:T(128)} %pad_add_fusion.where.refs_0_, bf16[224,512]{1,0:T(8,128)(2,1)} %get-tuple-element.80.query.refs_11_, bf16[2,224,512]{2,1,0:T(8,128)(2,1)} %get-tuple-element.81.mine.refs_13_, ...), custom_call_target="tpu_custom_call" | custom-call | flops 70000000 | bytes 258300 | tf_op jit(solution)/shard_map/self_attention/pallas_call | solution.py:532
  112.4 1.6 collective-permute-start.1
  114.0 11.4 %collective-permute-done.1.branch_other = bf16[224,1024]{1,0:T(8,128)(2,1)S(1)} collective-permute-done((bf16[224,1024]{1,0:T(8,128)(2,1)}, bf16[224,1024]{1,0:T(8,128)(2,1)S(1)}, u32[]{:S(2)}, u32[]{:S(2)}) %collective-permute-start.1) | collective-permute-done | bytes 458784 | tf_op jit(solution)/shard_map/ppermute | solution.py:51
  126.1 14.1 %cross_attention.1 = (f32[224,1024]{1,0:T(8,128)}, bf16[224,1024]{1,0:T(8,128)(2,1)}, bf16[224,512]{1,0:T(8,128)(2,1)}, bf16[224,16]{1,0:T(8,128)(2,1)}, bf16[22...) custom-call(bf16[224,1024]{1,0:T(8,128)(2,1)} %bitcast.60, ...), custom_call_target="tpu_custom_call" | custom-call | flops 130000000 | bytes 479700 | tf_op jit(solution)/shard_map/cross_attention/pallas_call | solution.py:532
  140.3 1.6 collective-permute-start.3
  144.8 7.6 %collective-permute-done.3.branch_other = bf16[224,1024]{1,0:T(8,128)(2,1)S(1)} collective-permute-done((bf16[224,1024]{1,0:T(8,128)(2,1)}, bf16[224,1024]{1,0:T(8,128)(2,1)S(1)}, u32[]{:S(2)}, u32[]{:S(2)}) %collective-permute-start.3) | collective-permute-done | bytes 458784 | tf_op jit(solution)/shard_map/ppermute | solution.py:51
  153.1 3.0 %third_norm.1 = (f32[224,1024]{1,0:T(8,128)}, bf16[224,1024]{1,0:T(8,128)(2,1)}, bf16[224,16]{1,0:T(8,128)(2,1)}, bf16[224,16]{1,0:T(8,128)(2,1)}) custom-call(f32[224,1024]{1,0:T(8,128)} %get-tuple-element.84.middle.refs_1_, bf16[224,1024]{1,0:T(8,128)(2,1)} %get-tuple-element.85.branch_mine, bf16[224,1024]{1,0:T(8,128)(2,1)} %copy-done.9, ...), custom_call_target="tpu_custom_call" | custom-call | flops 50000000 | bytes 184500 | tf_op jit(solution)/shard_map/third_norm/pallas_call | solution.py:532
  156.1 7.3 %all-gather.7.cloned.1.call-done = bf16[32,64,2048]{2,1,0:T(8,128)(2,1)} async-done(((bf16[2,64,2048]{2,1,0:T(8,128)(2,1)}), bf16[32,64,2048]{2,1,0:T(8,128)(2,1)}) %all-gather.7.cloned.1.call-update) | async-done | bytes 8388624 | tf_op jit(solution)/shard_map/all_gather | solution.py:585
  163.4 10.2 %units.1 = (bf16[224,1024]{1,0:T(8,128)(2,1)}, bf16[224,1024]{1,0:T(8,128)(2,1)}, f32[16,1024]{1,0:T(8,128)}, f32[16,2048]{1,0:T(8,128)}, f32[16,2048]{1,0:T(8,128)}, /*index=5*/f32[16,1024]{1,0:T(8,128)}) custom-call(bf16[224,1024]{1,0:T(8,128)(2,1)} %get-tuple-element.87.normed, bf16[224,16]{1,0:T(8,128)(2,1)} %get-tuple-element.88.up_low, ...), custom_call_target="tpu_custom_call" | custom-call | flops 110000000 | bytes 405900 | tf_op jit(solution)/shard_map/units/pallas_call | solution.py:532
  173.7 1.5 collective-permute-start.4
  175.2 11.4 %collective-permute-done.4.grad_other = bf16[224,1024]{1,0:T(8,128)(2,1)S(1)} collective-permute-done((bf16[224,1024]{1,0:T(8,128)(2,1)}, bf16[224,1024]{1,0:T(8,128)(2,1)S(1)}, u32[]{:S(2)}, u32[]{:S(2)}) %collective-permute-start.4) | collective-permute-done | bytes 458784 | tf_op jit(solution)/shard_map/ppermute | solution.py:51
  188.1 14.9 %cross_back.1 = (f32[224,1024]{1,0:T(8,128)}, bf16[224,1024]{1,0:T(8,128)(2,1)}, bf16[2,752,512]{2,1,0:T(8,128)(2,1)}, bf16[2,752,512]{2,1,0:T(8,128)(2,1)}, f32...) custom-call(bf16[224,1024]{1,0:T(8,128)(2,1)} %bitcast.58, ...), custom_call_target="tpu_custom_call" | custom-call | flops 180000000 | bytes 664200 | tf_op jit(solution)/shard_map/cross_back/pallas_call | solution.py:532
  203.9 2.7 collective-permute-done.6.grad_other
  207.8 8.4 %frames_back.1 = (bf16[750,1024]{1,0:T(8,128)(2,1)}, f32[2,16,1024]{2,1,0:T(8,128)}, f32[2,16,512]{2,1,0:T(8,128)}) custom-call(bf16[2,752,512]{2,1,0:T(8,128)(2,1)} %get-tuple-element.104.grad_mine, bf16[2,752,512]{2,1,0:T(8,128)(2,1)} %copy-done.4, bf16[16,8,64,512]{3,2,1,0:T(8,128)(2,1)} %bitcast.48, ...), custom_call_target="tpu_custom_call" | custom-call | flops 90000000 | bytes 332100 | tf_op jit(solution)/shard_map/frames_back/pallas_call | solution.py:532
  217.0 12.2 %self_back.1 = (f32[224,1024]{1,0:T(8,128)}, f32[224,1024]{1,0:T(8,128)}, bf16[2,224,512]{2,1,0:T(8,128)(2,1)}, bf16[2,224,512]{2,1,0:T(8,128)(2,1)}, f32[16,512...) custom-call(s32[3]{0:T(128)} %pad_add_fusion.where.refs_0_, ...), custom_call_target="tpu_custom_call" | custom-call | flops 120000000 | bytes 442800 | tf_op jit(solution)/shard_map/self_back/pallas_call | solution.py:532
  232.1 4.6 %self_project_back.1 = (bf16[224,1024]{1,0:T(8,128)(2,1)}, f32[2,16,1024]{2,1,0:T(8,128)}, f32[2,16,512]{2,1,0:T(8,128)}) custom-call(bf16[2,224,512]{2,1,0:T(8,128)(2,1)} %get-tuple-element.118.grad_mine, bf16[2,224,512]{2,1,0:T(8,128)(2,1)} %copy-done.12, bf16[16,8,64,512]{3,2,1,0:T(8,128)(2,1)} %bitcast.51, ...), custom_call_target="tpu_custom_call" | custom-call | flops 50000000 | bytes 184500 | tf_op jit(solution)/shard_map/self_project_back/pallas_call | solution.py:532
  236.7 5.2 %pack.1 = (f32[2,8,128,128]{3,2,1,0:T(8,128)}, f32[2,8,128,128]{3,2,1,0:T(8,128)}) custom-call(s32[3]{0:T(128)} %pad_add_fusion.where.refs_0_, f32[16,1024]{1,0:T(8,128)} %get-tuple-element.122.refs_1_, f32[2,16,1024]{2,1,0:T(8,128)} %get-tuple-element.123.refs_2_, f32[16,1024]{1,0:T(8,128)} %get-tuple-element.124.refs_3_, ...), custom_call_target="tpu_custom_call" | custom-call | flops 50000000 | bytes 184500 | tf_op jit(solution)/shard_map/pack/pallas_call | solution.py:532
  242.0 2.7 collective-permute-done.10
  244.8 7.5 %collective-permute-done.11.other = bf16[750,1024]{1,0:T(8,128)(2,1)} collective-permute-done((bf16[750,1024]{1,0:T(8,128)(2,1)}, bf16[750,1024]{1,0:T(8,128)(2,1)}, u32[]{:S(2)}, u32[]{:S(2)}) %collective-permute-start.11) | collective-permute-done | bytes 1536032 | tf_op jit(solution)/shard_map/ppermute | solution.py:51
  255.5 4.6 %encoder_total.1 = f32[750,1,1024]{2,1,0:T(1,128)} custom-call(bf16[750,1024]{1,0:T(8,128)(2,1)} %get-tuple-element.140.mine, bf16[750,1024]{1,0:T(8,128)(2,1)} %collective-permute-done.11.other), custom_call_target="tpu_custom_call" | custom-call | flops 50000000 | bytes 184500 | tf_op jit(solution)/shard_map/encoder_total/pallas_call | solution.py:532
  260.1 2.5 collective-permute-done.12
  262.6 2.0 fusion
  264.6 3.4 %all-to-all-start = ((bf16[8,128,128]{2,1,0:T(8,128)(2,1)}), bf16[8,128,128]{2,1,0:T(8,128)(2,1)S(1)}, u32[]{:S(2)}, u32[]{:S(2)}) async-start(bf16[8,128,128]{2,1,0:T(8,128)(2,1)} %fusion), calls=%async_computation | async-start | bytes 524288 | tf_op jit(solution)/shard_map/all_to_all | solution.py:673
  268.0 2.8 collective-permute-done.9.grad_other
  270.9 3.2 %hidden_total.1 = f32[224,1024]{1,0:T(8,128)} custom-call(bf16[224,1024]{1,0:T(8,128)(2,1)} %bitcast.61, f32[3,1024]{1,0:T(4,128)} %gains.9, f32[224,1024]{1,0:T(8,128)} %get-tuple-element.117.carried, bf16[224,1024]{1,0:T(8,128)(2,1)} %get-tuple-element.121.grad_mine, bf16[224,1024]{1,0:T(8,128)(2,1)} %collective-permute-done.9.grad_other), custom_call_target="tpu_custom_call" | custom-call | flops 50000000 | bytes 184500 | tf_op jit(solution)/shard_map/hidden_total/pallas_call | solution.py:532
  274.0 2.1 all-to-all-done.parts
  276.9 3.1 %unpack.1 = (f32[8,8,16,32]{3,2,1,0:T(8,128)}, f32[8,8,16,32]{3,2,1,0:T(8,128)}, f32[8,16,32]{2,1,0:T(8,128)}, f32[8,16,128]{2,1,0:T(8,128)}, f32[8,16,128]{2,1,0:T(8,128)}, /*index=5*/f32[8,16,32]{2,1,0:T(8,128)}) custom-call(bf16[8,128,128]{2,1,0:T(8,128)(2,1)} %copy-done.7), custom_call_target="tpu_custom_call" | custom-call | flops 50000000 | bytes 184500 | tf_op jit(solution)/shard_map/unpack/pallas_call | solution.py:532
  (63 shorter events, 23.2 us)
Async XLA Ops:
  7.2 6.4 %copy-start = (bf16[8,8,16,1024]{3,2,1,0:T(8,128)(2,1)S(1)}, bf16[8,8,16,1024]{3,2,1,0:T(8,128)(2,1)}, u32[]{:S(2)}) copy-start(bf16[8,8,16,1024]{3,2,1,0:T(8,128)(2,1)} %param.24) | copy-start | bytes 6291460
  7.2 3.1 %copy-start.14 = (bf16[128,2048]{1,0:T(8,128)(2,1)S(1)}, bf16[128,2048]{1,0:T(8,128)(2,1)}, u32[]{:S(2)}) copy-start(bf16[128,2048]{1,0:T(8,128)(2,1)} %param.23) | copy-start | bytes 1572868
  7.2 3.1 %copy-start.15 = (bf16[128,2048]{1,0:T(8,128)(2,1)S(1)}, bf16[128,2048]{1,0:T(8,128)(2,1)}, u32[]{:S(2)}) copy-start(bf16[128,2048]{1,0:T(8,128)(2,1)} %param.22) | copy-start | bytes 1572868
  7.2 80.6 %all-gather.5.cloned.1.call-start = ((), (), s32[]{:S(2)}) async-start(), calls=%async_computation.1 | async-start | bytes 8912896 | tf_op jit(solution)/shard_map/all_gather | solution.py:584
  10.2 153.2 %all-gather.7.cloned.1.call-start = ((), (), s32[]{:S(2)}) async-start(), calls=%async_computation.2 | async-start | bytes 8912896 | tf_op jit(solution)/shard_map/all_gather | solution.py:585
  94.9 30.4 %collective-permute-start.2 = (bf16[2,752,512]{2,1,0:T(8,128)(2,1)}, bf16[2,752,512]{2,1,0:T(8,128)(2,1)}, u32[]{:S(2)}, u32[]{:S(2)}) collective-permute-start(bf16[2,752,512]{2,1,0:T(8,128)(2,1)} %get-tuple-element.83.mine), channel_id=1, source_target_pairs={{0,2},{2,0},{1,3},{3,1},{4,6},{6,4},{5,7},{7,5},{8,10},{10,8},{9,1... | collective-permute-start | bytes 4620296 | tf_op jit(solution)/shard_map/ppermute | solution.py:51
  101.0 3.4 %collective-permute-start = (bf16[2,224,512]{2,1,0:T(8,128)(2,1)}, bf16[2,224,512]{2,1,0:T(8,128)(2,1)S(1)}, u32[]{:S(2)}, u32[]{:S(2)}) collective-permute-start(bf16[2,224,512]{2,1,0:T(8,128)(2,1)} %get-tuple-element.81.mine.refs_13_), channel_id=1, source_target_pairs={{0,2},{2,0},{1,3},{3,1},{4,6},{6,4},{5,7},{7,5},{8,10},{10,8},{9,1... | collective-permute-start | bytes 1376264 | tf_op jit(solution)/shard_map/ppermute | solution.py:51
  104.3 0.8 copy-start.3
  112.4 12.9 %collective-permute-start.1 = (bf16[224,1024]{1,0:T(8,128)(2,1)}, bf16[224,1024]{1,0:T(8,128)(2,1)S(1)}, u32[]{:S(2)}, u32[]{:S(2)}) collective-permute-start(bf16[224,1024]{1,0:T(8,128)(2,1)} %get-tuple-element.82.branch_mine), channel_id=1, source_target_pairs={{0,1},{1,0},{2,3},{3,2},{4,5},{5,4},{6,7},{7,6},{8,9},{9,8},{10,11... | collective-permute-start | bytes 1376264 | tf_op jit(solution)/shard_map/ppermute | solution.py:51
  125.3 0.8 copy-start.13
  140.3 12.1 %collective-permute-start.3 = (bf16[224,1024]{1,0:T(8,128)(2,1)}, bf16[224,1024]{1,0:T(8,128)(2,1)S(1)}, u32[]{:S(2)}, u32[]{:S(2)}) collective-permute-start(bf16[224,1024]{1,0:T(8,128)(2,1)} %get-tuple-element.85.branch_mine), channel_id=1, source_target_pairs={{0,1},{1,0},{2,3},{3,2},{4,5},{5,4},{6,7},{7,6},{8,9},{9,8},{10,11... | collective-permute-start | bytes 1376264 | tf_op jit(solution)/shard_map/ppermute | solution.py:51
  152.4 0.8 copy-start.9
  173.7 13.0 %collective-permute-start.4 = (bf16[224,1024]{1,0:T(8,128)(2,1)}, bf16[224,1024]{1,0:T(8,128)(2,1)S(1)}, u32[]{:S(2)}, u32[]{:S(2)}) collective-permute-start(bf16[224,1024]{1,0:T(8,128)(2,1)} %get-tuple-element.90.grad_mine), channel_id=1, source_target_pairs={{0,1},{1,0},{2,3},{3,2},{4,5},{5,4},{6,7},{7,6},{8,9},{9,8},{10,11... | collective-permute-start | bytes 1376264 | tf_op jit(solution)/shard_map/ppermute | solution.py:51
  186.7 1.5 copy-start.8
  186.7 16.3 %collective-permute-start.5 = (bf16[224,1024]{1,0:T(8,128)(2,1)}, bf16[224,1024]{1,0:T(8,128)(2,1)S(1)}, u32[]{:S(2)}, u32[]{:S(2)}) collective-permute-start(bf16[224,1024]{1,0:T(8,128)(2,1)} %get-tuple-element.102), channel_id=1, source_target_pairs={{0,1},{1,0},{2,3},{3,2},{4,5},{5,4},{6,7},{7,6},{8,9},{9,8},{10,11... | collective-permute-start | bytes 1376264 | tf_op jit(solution)/shard_map/ppermute | solution.py:51
  203.0 3.6 %collective-permute-start.6 = (bf16[2,752,512]{2,1,0:T(8,128)(2,1)}, bf16[2,752,512]{2,1,0:T(8,128)(2,1)S(1)}, u32[]{:S(2)}, u32[]{:S(2)}) collective-permute-start(bf16[2,752,512]{2,1,0:T(8,128)(2,1)} %get-tuple-element.105), channel_id=1, source_target_pairs={{0,2},{2,0},{1,3},{3,1},{4,6},{6,4},{5,7},{7,5},{8,10},{10,8},{9,1... | collective-permute-start | bytes 4620296 | tf_op jit(solution)/shard_map/ppermute | solution.py:51
  203.1 13.1 %collective-permute-start.7 = (bf16[224,1024]{1,0:T(8,128)(2,1)}, bf16[224,1024]{1,0:T(8,128)(2,1)S(1)}, u32[]{:S(2)}, u32[]{:S(2)}) collective-permute-start(bf16[224,1024]{1,0:T(8,128)(2,1)} %get-tuple-element.103.refs_3_), channel_id=1, source_target_pairs={{0,1},{1,0},{2,3},{3,2},{4,5},{5,4},{6,7},{7,6},{8,9},{9,8},{10,11... | collective-permute-start | bytes 1376264 | tf_op jit(solution)/shard_map/ppermute | solution.py:51
  206.7 1.1 copy-start.4
  216.2 0.8 copy-start.11
  216.2 36.0 %collective-permute-start.11 = (bf16[750,1024]{1,0:T(8,128)(2,1)}, bf16[750,1024]{1,0:T(8,128)(2,1)}, u32[]{:S(2)}, u32[]{:S(2)}) collective-permute-start(bf16[750,1024]{1,0:T(8,128)(2,1)} %get-tuple-element.140.mine), channel_id=1, source_target_pairs={{0,1},{1,0},{2,3},{3,2},{4,5},{5,4},{6,7},{7,6},{8,9},{9,8},{10,11... | collective-permute-start | bytes 4608008 | tf_op jit(solution)/shard_map/ppermute | solution.py:51
  217.0 12.3 %copy-start.2 = (f32[224,1024]{1,0:T(8,128)S(1)}, f32[224,1024]{1,0:T(8,128)}, u32[]{:S(2)}) copy-start(f32[224,1024]{1,0:T(8,128)} %get-tuple-element.86.rows) | copy-start | bytes 2752516
  217.0 12.3 %copy-start.10 = (bf16[224,1024]{1,0:T(8,128)(2,1)S(1)}, bf16[224,1024]{1,0:T(8,128)(2,1)}, u32[]{:S(2)}) copy-start(bf16[224,1024]{1,0:T(8,128)(2,1)} %get-tuple-element.102) | copy-start | bytes 1376260
  229.2 2.1 collective-permute-start.8
  231.3 0.8 copy-start.12
  241.9 2.9 %collective-permute-start.10 = (f32[2,8,128,128]{3,2,1,0:T(8,128)}, f32[2,8,128,128]{3,2,1,0:T(8,128)S(1)}, u32[]{:S(2)}, u32[]{:S(2)}) collective-permute-start(f32[2,8,128,128]{3,2,1,0:T(8,128)} %get-tuple-element.139), channel_id=1, source_target_pairs={{0,2},{2,0},{1,3},{3,1},{4,6},{6,4},{5,7},{7,5},{8,10},{10,8},{9,1... | collective-permute-start | bytes 3145736 | tf_op jit(solution)/shard_map/ppermute | solution.py:51
  244.8 15.3 %copy-start.6 = (f32[2,8,128,128]{3,2,1,0:T(8,128)}, f32[2,8,128,128]{3,2,1,0:T(8,128)S(1)}, u32[]{:S(2)}) copy-start(f32[2,8,128,128]{3,2,1,0:T(8,128)S(1)} %collective-permute-done.10) | copy-start | bytes 3145732
  253.4 9.2 %collective-permute-start.12 = (bf16[8,128,128]{2,1,0:T(8,128)(2,1)S(1)}, bf16[8,128,128]{2,1,0:T(8,128)(2,1)S(1)}, u32[]{:S(2)}, u32[]{:S(2)}) collective-permute-start(bf16[8,128,128]{2,1,0:T(8,128)(2,1)S(1)} %fusion.1), channel_id=1, source_target_pairs={{0,1},{1,0},{2,3},{3,2},{4,5},{5,4},{6,7},{7,6},{8,9},{9,8},{10,11... | collective-permute-start | bytes 786440 | tf_op jit(solution)/shard_map/ppermute | solution.py:51
  254.2 8.4 %copy-start.5 = (f32[2,8,128,128]{3,2,1,0:T(8,128)S(1)}, f32[2,8,128,128]{3,2,1,0:T(8,128)}, u32[]{:S(2)}) copy-start(f32[2,8,128,128]{3,2,1,0:T(8,128)} %get-tuple-element.138) | copy-start | bytes 3145732
  254.2 16.6 %collective-permute-start.9 = (bf16[224,1024]{1,0:T(8,128)(2,1)}, bf16[224,1024]{1,0:T(8,128)(2,1)}, u32[]{:S(2)}, u32[]{:S(2)}) collective-permute-start(bf16[224,1024]{1,0:T(8,128)(2,1)} %get-tuple-element.121.grad_mine), channel_id=1, source_target_pairs={{0,1},{1,0},{2,3},{3,2},{4,5},{5,4},{6,7},{7,6},{8,9},{9,8},{10,11... | collective-permute-start | bytes 1376264 | tf_op jit(solution)/shard_map/ppermute | solution.py:51
  262.6 17.3 %copy-start.1 = (bf16[8,8,16,1024]{3,2,1,0:T(8,128)(2,1)S(1)}, bf16[8,8,16,1024]{3,2,1,0:T(8,128)(2,1)}, u32[]{:S(2)}) copy-start(bf16[8,8,16,1024]{3,2,1,0:T(8,128)(2,1)} %param.24) | copy-start | bytes 6291460
  264.6 11.6 %all-to-all-start = ((bf16[8,128,128]{2,1,0:T(8,128)(2,1)}), bf16[8,128,128]{2,1,0:T(8,128)(2,1)S(1)}, u32[]{:S(2)}, u32[]{:S(2)}) async-start(bf16[8,128,128]{2,1,0:T(8,128)(2,1)} %fusion), calls=%async_computation | async-start | bytes 524288 | tf_op jit(solution)/shard_map/all_to_all | solution.py:673
  276.2 0.7 copy-start.7
Sparse Core Ops, SparseCore 0:
  10.8 77.0 all-gather.4
  90.5 72.8 all-gather.6

commit v4 on v3

--- a/solution.py
+++ b/solution.py
@@ -149,6 +149,12 @@
     return pl.when(pl.program_id(0) == pl.num_programs(0) - 1)
 
 
+def halves_kernel(where, inputs, outputs, joined):
+    count = inputs.shape[0]
+    joined[:count] = inputs[...]
+    joined[count:] = outputs[...]
+
+
 def qkv_kernel(hidden, gains, weight, low_in, low_out, normed, query, key_value, low):
     @at_first()
     def _():
@@ -451,15 +457,18 @@
                 for g in range(4):
                     turned = pltpu.roll(groups[g], (PIECE * (g + 4 - p)) % LANE, 1)
                     value = jnp.where(lane == g, turned, value)
+                if tagged:
+                    spare = 4 * per_group - len(order)
+                    tag = where[2].astype(F32) * 0.25
+                    low = rows - 16 * spare
+                    at_row = lax.broadcasted_iota(jnp.int32, (rows, LANE), 0)
+                    value = jnp.where((lane == 3) & (at_row >= low), tag, value)
                 target[t, f, :rows] = value
                 row = rows
                 for w in broad:
                     at = pl.multiple_of(local * 4 * LANE + p * LANE, LANE)
                     target[t, f, row : row + 16] = jnp.where(owned, w[:, pl.ds(at, LANE)], 0.0)
                     row += 16
-                if tagged:
-                    tag = where[2].astype(F32) * 0.25
-                    target[t, f, row : row + 16] = jnp.full((16, LANE), 1.0, F32) * tag
         return carry
 
     lax.fori_loop(0, blocks, one_block, 0)
@@ -471,13 +480,18 @@
     per_group = (2 * projections + 2 + 3) // 4
     narrow = 16 * per_group
 
+    tags = []
+    for c in range(clips):
+        tag = parts[c, narrow - 16 : narrow, 3 * PIECE :].astype(F32)[0:1, 0:1]
+        tags.append(jnp.broadcast_to(tag, (1, LANE)))
+
     def one(a, carry):
         adapter = a.astype(F32)
-        block = jnp.zeros((rows - 16, LANE), F32)
+        block = jnp.zeros((rows, LANE), F32)
         for c in range(clips):
-            tag = parts[c, rows - 16 : rows - 15, :].astype(F32)
-            same = (tag > adapter - 0.5) & (tag < adapter + 0.5)
-            block = block + jnp.where(same, parts[c, : rows - 16].astype(F32), 0.0)
+            same = (tags[c] > adapter - 0.5) & (tags[c] < adapter + 0.5)
+            weight = jnp.where(same, 1.0, 0.0)
+            block = block + parts[c].astype(F32) * weight
 
         def piece(k):
             g, at = k // per_group, 16 * (k % per_group)
@@ -571,6 +585,9 @@
         [context_index.astype(jnp.int32), tensor_index.astype(jnp.int32), mine]
     )
 
+    def out(dims, dtype):
+        return shape(dims, dtype), fixed_out(*dims)
+
     half_rows = attn_in_weight.shape[1] // ctx_size
     shards = fsdp_size * ctx_size
 
@@ -579,7 +596,18 @@
             table, context_index * half_rows, half_rows, axis=table.ndim - 2
         )
 
-    attn_half = jnp.concatenate([my_half(attn_in_weight), my_half(attn_out_weight)], axis=0)
+    heads_tables = (attn_in_weight, attn_out_weight)
+    (attn_half,) = call(
+        halves_kernel,
+        1,
+        [
+            (t, pl.BlockSpec((t.shape[0], half_rows, cols), lambda i, where: (0, where[0], 0)))
+            for t in heads_tables
+        ],
+        [out((sum(t.shape[0] for t in heads_tables), half_rows, cols), BF)],
+        scalars=context_index.astype(jnp.int32).reshape(1),
+        name="halves",
+    )
     ff_half = jnp.stack([my_half(up_weight), my_half(down_weight)])
     attn_full = lax.all_gather(attn_half, ("fsdp", "ctx"), axis=0)
     ff_full = lax.all_gather(ff_half, ("fsdp", "ctx"), axis=0)
@@ -608,9 +636,6 @@
     def whole(array):
         return array, fixed(array)
 
-    def out(dims, dtype):
-        return shape(dims, dtype), fixed_out(*dims)
-
     def by_pair(count, dtype=BF):
         return shape((count, cols), dtype), pl.BlockSpec((count, PAIR), lambda p, *_: (0, p))
 
@@ -646,7 +671,7 @@
         return lax.optimization_barrier((first, *others))
 
     def pack(full, part, wides, order, tagged, name, after):
-        count = 16 * ((len(order) + 3) // 4 + len(wides) + tagged)
+        count = 16 * ((len(order) + 3) // 4 + len(wides))
         dims = (2, fsdp_size, count, LANE)
 
         def number(arrays):
@@ -660,14 +685,15 @@
             scalars=scalars,
             name=name,
         )
-        recv, after = ordered(swap(send, "ctx"), after)
+        recv = swap(send, "ctx")
 
         def pick(i):
             return lax.dynamic_index_in_dim(keep, i, 0, keepdims=False) + (
                 lax.dynamic_index_in_dim(recv, i, 0, keepdims=False)
             )
 
-        return pick(tensor_index), pick(1 - tensor_index).astype(BF), after
+        kept, away = pick(tensor_index), pick(1 - tensor_index).astype(BF)
+        return ordered(kept, away, after)
 
     def finish(kept, away):
         return lax.all_to_all((kept + away.astype(F32)).astype(BF), "fsdp", 0, 0, tiled=True)
@@ -771,7 +797,7 @@
         cost=13,
     )
     branch, branch_other = with_other(branch, "tp")
-    chunk = min(units, 512)
+    chunk = min(units, 1024)
 
     def unit_weight(slot):
         return ff_full, pl.BlockSpec((shards, 1, half_rows, chunk), lambda i: (0, slot, 0, i))

time: 288 us -> 285 us (0.990)
    pallas_call x14 -> x15, Pallas kernels: 104 us -> 106 us  [call(): return run(*arrays) if scalars is None else run(scalars, *arrays)]
  transfers between devices with their start and end apart: 16 -> 16, of which waited for: 13 -> 13; matrix products, arithmetic and copies ran while one was open for 4% -> 5% of each run, Pallas kernels for 32% -> 32%
where the time goes in v4:
time: 285 us; the launch traced here: 284 us
  waiting for transfers between devices  131 us (46%)
  Pallas kernels  106 us (37%)
  between operations  14.9 us (5%)
  starting transfers between devices  14.1 us (5%)
  local copies, waits for them, and re-layouts  13.6 us (5%)
  other arithmetic  5.55 us (2%)
    pallas_call x15, Pallas kernels, call(): return run(*arrays) if scalars is None else run(scalars, *arrays)  106 us
    all_gather x1, waiting for transfers between devices, on_device(): attn_full = lax.all_gather(attn_half, ('fsdp', 'ctx'), axis=0)  74.4 us
    ppermute x13, waiting for transfers between devices, swap(): return lax.ppermute(value, axis, [(0, 1), (1, 0)])  47.8 us
    ppermute x13, starting transfers between devices, swap(): return lax.ppermute(value, axis, [(0, 1), (1, 0)])  10.7 us
    all_gather x1, waiting for transfers between devices, on_device(): ff_full = lax.all_gather(ff_half, ('fsdp', 'ctx'), axis=0)  7.28 us
    unnamed x32, local copies, waits for them, and re-layouts  5.77 us
  transfers between devices with their start and end apart: 16, of which 13 were waited for; matrix products, arithmetic and copies ran while one was open for 5% of the time, Pallas kernels for 32%

profile of v4, /device:TPU:0, one launch (start us, length us, event | category | flops | bytes accessed | tf_op | source)
XLA Modules:
  0.0 284.5 jit_solution(6442399561249939995)
XLA Ops:
  7.3 2.0 halves.1
  11.0 1.7 dynamic-slice_bitcast_fusion.5.low_out.query_out.refs_10_
  13.4 74.4 %all-gather.5.cloned.1.call-done = bf16[128,64,512]{2,1,0:T(8,128)(2,1)} async-done(((bf16[8,64,512]{2,1,0:T(8,128)(2,1)}), bf16[128,64,512]{2,1,0:T(8,128)(2,1)}) %all-gather.5.cloned.1.call-update) | async-done | bytes 8388624 | tf_op jit(solution)/shard_map/all_gather | solution.py:612
  87.8 7.1 %frames.1 = (bf16[2,752,512]{2,1,0:T(8,128)(2,1)}, bf16[2,750,16]{2,1,0:T(8,128)(2,1)}) custom-call(bf16[750,1024]{1,0:T(8,128)(2,1)} %bitcast.52, bf16[16,8,64,512]{3,2,1,0:T(8,128)(2,1)} %bitcast.39, bf16[8,16,1024]{2,1,0:T(8,128)(2,1)} %dynamic-slice_bitcast_fusion.3.low_in.query_in.refs_9_, ...), custom_call_target="tpu_custom_call" | custom-call | flops 70000000 | bytes 258300 | tf_op jit(solution)/shard_map/frames/pallas_call | solution.py:546
  95.2 5.8 %qkv.1 = (bf16[224,1024]{1,0:T(8,128)(2,1)}, bf16[224,512]{1,0:T(8,128)(2,1)}, bf16[2,224,512]{2,1,0:T(8,128)(2,1)}, bf16[3,224,16]{2,1,0:T(8,128)(2,1)}) custom-call(bf16[224,1024]{1,0:T(8,128)(2,1)} %bitcast.57, f32[3,1024]{1,0:T(4,128)} %gains.9, bf16[16,8,64,512]{3,2,1,0:T(8,128)(2,1)} %bitcast.40, ...), custom_call_target="tpu_custom_call" | custom-call | flops 50000000 | bytes 184500 | tf_op jit(solution)/shard_map/qkv/pallas_call | solution.py:546
  102.7 1.7 dynamic-slice_bitcast_fusion.2.low_out.refs_7_
  105.1 7.3 %self_attention.1 = (bf16[224,512]{1,0:T(8,128)(2,1)}, f32[4,2,224]{2,1,0:T(2,128)}, bf16[224,1024]{1,0:T(8,128)(2,1)}, bf16[224,16]{1,0:T(8,128)(2,1)}) custom-call(s32[3]{0:T(128)} %pad_add_fusion.where.refs_0_, bf16[224,512]{1,0:T(8,128)(2,1)} %get-tuple-element.81.query.refs_11_, bf16[2,224,512]{2,1,0:T(8,128)(2,1)} %get-tuple-element.82.mine.refs_13_, ...), custom_call_target="tpu_custom_call" | custom-call | flops 70000000 | bytes 258300 | tf_op jit(solution)/shard_map/self_attention/pallas_call | solution.py:546
  112.4 1.6 collective-permute-start.1
  114.0 11.3 %collective-permute-done.1.branch_other = bf16[224,1024]{1,0:T(8,128)(2,1)S(1)} collective-permute-done((bf16[224,1024]{1,0:T(8,128)(2,1)}, bf16[224,1024]{1,0:T(8,128)(2,1)S(1)}, u32[]{:S(2)}, u32[]{:S(2)}) %collective-permute-start.1) | collective-permute-done | bytes 458784 | tf_op jit(solution)/shard_map/ppermute | solution.py:51
  126.2 14.1 %cross_attention.1 = (f32[224,1024]{1,0:T(8,128)}, bf16[224,1024]{1,0:T(8,128)(2,1)}, bf16[224,512]{1,0:T(8,128)(2,1)}, bf16[224,16]{1,0:T(8,128)(2,1)}, bf16[22...) custom-call(bf16[224,1024]{1,0:T(8,128)(2,1)} %bitcast.58, ...), custom_call_target="tpu_custom_call" | custom-call | flops 130000000 | bytes 479700 | tf_op jit(solution)/shard_map/cross_attention/pallas_call | solution.py:546
  140.3 1.6 collective-permute-start.3
  144.8 7.6 %collective-permute-done.3.branch_other = bf16[224,1024]{1,0:T(8,128)(2,1)S(1)} collective-permute-done((bf16[224,1024]{1,0:T(8,128)(2,1)}, bf16[224,1024]{1,0:T(8,128)(2,1)S(1)}, u32[]{:S(2)}, u32[]{:S(2)}) %collective-permute-start.3) | collective-permute-done | bytes 458784 | tf_op jit(solution)/shard_map/ppermute | solution.py:51
  153.2 3.0 %third_norm.1 = (f32[224,1024]{1,0:T(8,128)}, bf16[224,1024]{1,0:T(8,128)(2,1)}, bf16[224,16]{1,0:T(8,128)(2,1)}, bf16[224,16]{1,0:T(8,128)(2,1)}) custom-call(f32[224,1024]{1,0:T(8,128)} %get-tuple-element.85.middle.refs_1_, bf16[224,1024]{1,0:T(8,128)(2,1)} %get-tuple-element.86.branch_mine, bf16[224,1024]{1,0:T(8,128)(2,1)} %copy-done.8, ...), custom_call_target="tpu_custom_call" | custom-call | flops 50000000 | bytes 184500 | tf_op jit(solution)/shard_map/third_norm/pallas_call | solution.py:546
  156.2 7.3 %all-gather.7.cloned.1.call-done = bf16[32,64,2048]{2,1,0:T(8,128)(2,1)} async-done(((bf16[2,64,2048]{2,1,0:T(8,128)(2,1)}), bf16[32,64,2048]{2,1,0:T(8,128)(2,1)}) %all-gather.7.cloned.1.call-update) | async-done | bytes 8388624 | tf_op jit(solution)/shard_map/all_gather | solution.py:613
  163.4 10.0 %units.1 = (bf16[224,1024]{1,0:T(8,128)(2,1)}, bf16[224,1024]{1,0:T(8,128)(2,1)}, f32[16,1024]{1,0:T(8,128)}, f32[16,2048]{1,0:T(8,128)}, f32[16,2048]{1,0:T(8,128)}, /*index=5*/f32[16,1024]{1,0:T(8,128)}) custom-call(bf16[224,1024]{1,0:T(8,128)(2,1)} %get-tuple-element.88.normed, bf16[224,16]{1,0:T(8,128)(2,1)} %get-tuple-element.89.up_low, ...), custom_call_target="tpu_custom_call" | custom-call | flops 110000000 | bytes 405900 | tf_op jit(solution)/shard_map/units/pallas_call | solution.py:546
  173.5 1.6 collective-permute-start.4
  175.0 11.4 %collective-permute-done.4.grad_other = bf16[224,1024]{1,0:T(8,128)(2,1)S(1)} collective-permute-done((bf16[224,1024]{1,0:T(8,128)(2,1)}, bf16[224,1024]{1,0:T(8,128)(2,1)S(1)}, u32[]{:S(2)}, u32[]{:S(2)}) %collective-permute-start.4) | collective-permute-done | bytes 458784 | tf_op jit(solution)/shard_map/ppermute | solution.py:51
  187.9 14.9 %cross_back.1 = (f32[224,1024]{1,0:T(8,128)}, bf16[224,1024]{1,0:T(8,128)(2,1)}, bf16[2,752,512]{2,1,0:T(8,128)(2,1)}, bf16[2,752,512]{2,1,0:T(8,128)(2,1)}, f32...) custom-call(bf16[224,1024]{1,0:T(8,128)(2,1)} %bitcast.56, ...), custom_call_target="tpu_custom_call" | custom-call | flops 180000000 | bytes 664200 | tf_op jit(solution)/shard_map/cross_back/pallas_call | solution.py:546
  203.7 2.7 collective-permute-done.6.grad_other
  207.6 8.3 %frames_back.1 = (bf16[750,1024]{1,0:T(8,128)(2,1)}, f32[2,16,1024]{2,1,0:T(8,128)}, f32[2,16,512]{2,1,0:T(8,128)}) custom-call(bf16[2,752,512]{2,1,0:T(8,128)(2,1)} %get-tuple-element.105.grad_mine, bf16[2,752,512]{2,1,0:T(8,128)(2,1)} %copy-done.4, bf16[16,8,64,512]{3,2,1,0:T(8,128)(2,1)} %bitcast.46, ...), custom_call_target="tpu_custom_call" | custom-call | flops 90000000 | bytes 332100 | tf_op jit(solution)/shard_map/frames_back/pallas_call | solution.py:546
  216.8 12.2 %self_back.1 = (f32[224,1024]{1,0:T(8,128)}, f32[224,1024]{1,0:T(8,128)}, bf16[2,224,512]{2,1,0:T(8,128)(2,1)}, bf16[2,224,512]{2,1,0:T(8,128)(2,1)}, f32[16,512...) custom-call(s32[3]{0:T(128)} %pad_add_fusion.where.refs_0_, ...), custom_call_target="tpu_custom_call" | custom-call | flops 120000000 | bytes 442800 | tf_op jit(solution)/shard_map/self_back/pallas_call | solution.py:546
  231.9 4.7 %self_project_back.1 = (bf16[224,1024]{1,0:T(8,128)(2,1)}, f32[2,16,1024]{2,1,0:T(8,128)}, f32[2,16,512]{2,1,0:T(8,128)}) custom-call(bf16[2,224,512]{2,1,0:T(8,128)(2,1)} %get-tuple-element.119.grad_mine, bf16[2,224,512]{2,1,0:T(8,128)(2,1)} %copy-done.12, bf16[16,8,64,512]{3,2,1,0:T(8,128)(2,1)} %bitcast.49, ...), custom_call_target="tpu_custom_call" | custom-call | flops 50000000 | bytes 184500 | tf_op jit(solution)/shard_map/self_project_back/pallas_call | solution.py:546
  236.6 5.2 %pack.1 = (f32[2,8,112,128]{3,2,1,0:T(8,128)}, f32[2,8,112,128]{3,2,1,0:T(8,128)}) custom-call(s32[3]{0:T(128)} %pad_add_fusion.where.refs_0_, f32[16,1024]{1,0:T(8,128)} %get-tuple-element.123.refs_1_, f32[2,16,1024]{2,1,0:T(8,128)} %get-tuple-element.124.refs_2_, f32[16,1024]{1,0:T(8,128)} %get-tuple-element.125.refs_3_, ...), custom_call_target="tpu_custom_call" | custom-call | flops 50000000 | bytes 184500 | tf_op jit(solution)/shard_map/pack/pallas_call | solution.py:546
  241.9 2.5 collective-permute-done.10
  245.7 6.3 %collective-permute-done.11.other = bf16[750,1024]{1,0:T(8,128)(2,1)} collective-permute-done((bf16[750,1024]{1,0:T(8,128)(2,1)}, bf16[750,1024]{1,0:T(8,128)(2,1)}, u32[]{:S(2)}, u32[]{:S(2)}) %collective-permute-start.11) | collective-permute-done | bytes 1536032 | tf_op jit(solution)/shard_map/ppermute | solution.py:51
  254.1 4.6 %encoder_total.1 = f32[750,1,1024]{2,1,0:T(1,128)} custom-call(bf16[750,1024]{1,0:T(8,128)(2,1)} %get-tuple-element.141.mine, bf16[750,1024]{1,0:T(8,128)(2,1)} %collective-permute-done.11.other), custom_call_target="tpu_custom_call" | custom-call | flops 50000000 | bytes 184500 | tf_op jit(solution)/shard_map/encoder_total/pallas_call | solution.py:546
  258.7 1.9 collective-permute-done.12
  260.7 1.8 add_convert_fusion.1
  262.5 3.4 %all-to-all-start = ((bf16[8,112,128]{2,1,0:T(8,128)(2,1)}), bf16[8,112,128]{2,1,0:T(8,128)(2,1)S(1)}, u32[]{:S(2)}, u32[]{:S(2)}) async-start(bf16[8,112,128]{2,1,0:T(8,128)(2,1)} %add_convert_fusion.1), calls=%async_computation | async-start | bytes 458752 | tf_op jit(solution)/shard_map/all_to_all | solution.py:699
  265.9 2.8 collective-permute-done.9.grad_other
  269.4 3.2 %hidden_total.1 = f32[224,1024]{1,0:T(8,128)} custom-call(bf16[224,1024]{1,0:T(8,128)(2,1)} %bitcast.59, f32[3,1024]{1,0:T(4,128)} %gains.9, f32[224,1024]{1,0:T(8,128)} %get-tuple-element.118.carried, bf16[224,1024]{1,0:T(8,128)(2,1)} %get-tuple-element.122.grad_mine, bf16[224,1024]{1,0:T(8,128)(2,1)} %copy-done.9), custom_call_target="tpu_custom_call" | custom-call | flops 50000000 | bytes 184500 | tf_op jit(solution)/shard_map/hidden_total/pallas_call | solution.py:546
  274.5 3.1 %unpack.1 = (f32[8,8,16,32]{3,2,1,0:T(8,128)}, f32[8,8,16,32]{3,2,1,0:T(8,128)}, f32[8,16,32]{2,1,0:T(8,128)}, f32[8,16,128]{2,1,0:T(8,128)}, f32[8,16,128]{2,1,0:T(8,128)}, /*index=5*/f32[8,16,32]{2,1,0:T(8,128)}) custom-call(bf16[8,112,128]{2,1,0:T(8,128)(2,1)} %copy-done.5), custom_call_target="tpu_custom_call" | custom-call | flops 50000000 | bytes 184500 | tf_op jit(solution)/shard_map/unpack/pallas_call | solution.py:546
  (61 shorter events, 22.3 us)
Async XLA Ops:
  7.2 5.5 %copy-start = (bf16[8,8,16,1024]{3,2,1,0:T(8,128)(2,1)S(1)}, bf16[8,8,16,1024]{3,2,1,0:T(8,128)(2,1)}, u32[]{:S(2)}) copy-start(bf16[8,8,16,1024]{3,2,1,0:T(8,128)(2,1)} %param.24) | copy-start | bytes 6291460
  7.2 2.2 copy-start.14
  7.2 2.2 copy-start.15
  7.2 80.6 %all-gather.5.cloned.1.call-start = ((), (), s32[]{:S(2)}) async-start(), calls=%async_computation.1 | async-start | bytes 8912896 | tf_op jit(solution)/shard_map/all_gather | solution.py:612
  9.3 154.2 %all-gather.7.cloned.1.call-start = ((), (), s32[]{:S(2)}) async-start(), calls=%async_computation.2 | async-start | bytes 8912896 | tf_op jit(solution)/shard_map/all_gather | solution.py:613
  94.9 30.5 %collective-permute-start.2 = (bf16[2,752,512]{2,1,0:T(8,128)(2,1)}, bf16[2,752,512]{2,1,0:T(8,128)(2,1)}, u32[]{:S(2)}, u32[]{:S(2)}) collective-permute-start(bf16[2,752,512]{2,1,0:T(8,128)(2,1)} %get-tuple-element.84.mine), channel_id=1, source_target_pairs={{0,2},{2,0},{1,3},{3,1},{4,6},{6,4},{5,7},{7,5},{8,10},{10,8},{9,1... | collective-permute-start | bytes 4620296 | tf_op jit(solution)/shard_map/ppermute | solution.py:51
  101.0 3.4 %collective-permute-start = (bf16[2,224,512]{2,1,0:T(8,128)(2,1)}, bf16[2,224,512]{2,1,0:T(8,128)(2,1)S(1)}, u32[]{:S(2)}, u32[]{:S(2)}) collective-permute-start(bf16[2,224,512]{2,1,0:T(8,128)(2,1)} %get-tuple-element.82.mine.refs_13_), channel_id=1, source_target_pairs={{0,2},{2,0},{1,3},{3,1},{4,6},{6,4},{5,7},{7,5},{8,10},{10,8},{9,1... | collective-permute-start | bytes 1376264 | tf_op jit(solution)/shard_map/ppermute | solution.py:51
  104.4 0.8 copy-start.3
  112.4 12.9 %collective-permute-start.1 = (bf16[224,1024]{1,0:T(8,128)(2,1)}, bf16[224,1024]{1,0:T(8,128)(2,1)S(1)}, u32[]{:S(2)}, u32[]{:S(2)}) collective-permute-start(bf16[224,1024]{1,0:T(8,128)(2,1)} %get-tuple-element.83.branch_mine), channel_id=1, source_target_pairs={{0,1},{1,0},{2,3},{3,2},{4,5},{5,4},{6,7},{7,6},{8,9},{9,8},{10,11... | collective-permute-start | bytes 1376264 | tf_op jit(solution)/shard_map/ppermute | solution.py:51
  125.4 0.8 copy-start.13
  140.3 12.1 %collective-permute-start.3 = (bf16[224,1024]{1,0:T(8,128)(2,1)}, bf16[224,1024]{1,0:T(8,128)(2,1)S(1)}, u32[]{:S(2)}, u32[]{:S(2)}) collective-permute-start(bf16[224,1024]{1,0:T(8,128)(2,1)} %get-tuple-element.86.branch_mine), channel_id=1, source_target_pairs={{0,1},{1,0},{2,3},{3,2},{4,5},{5,4},{6,7},{7,6},{8,9},{9,8},{10,11... | collective-permute-start | bytes 1376264 | tf_op jit(solution)/shard_map/ppermute | solution.py:51
  152.4 0.8 copy-start.8
  173.5 13.0 %collective-permute-start.4 = (bf16[224,1024]{1,0:T(8,128)(2,1)}, bf16[224,1024]{1,0:T(8,128)(2,1)S(1)}, u32[]{:S(2)}, u32[]{:S(2)}) collective-permute-start(bf16[224,1024]{1,0:T(8,128)(2,1)} %get-tuple-element.91.grad_mine), channel_id=1, source_target_pairs={{0,1},{1,0},{2,3},{3,2},{4,5},{5,4},{6,7},{7,6},{8,9},{9,8},{10,11... | collective-permute-start | bytes 1376264 | tf_op jit(solution)/shard_map/ppermute | solution.py:51
  186.4 1.5 copy-start.6
  186.4 16.4 %collective-permute-start.5 = (bf16[224,1024]{1,0:T(8,128)(2,1)}, bf16[224,1024]{1,0:T(8,128)(2,1)S(1)}, u32[]{:S(2)}, u32[]{:S(2)}) collective-permute-start(bf16[224,1024]{1,0:T(8,128)(2,1)} %get-tuple-element.103), channel_id=1, source_target_pairs={{0,1},{1,0},{2,3},{3,2},{4,5},{5,4},{6,7},{7,6},{8,9},{9,8},{10,11... | collective-permute-start | bytes 1376264 | tf_op jit(solution)/shard_map/ppermute | solution.py:51
  202.8 3.6 %collective-permute-start.6 = (bf16[2,752,512]{2,1,0:T(8,128)(2,1)}, bf16[2,752,512]{2,1,0:T(8,128)(2,1)S(1)}, u32[]{:S(2)}, u32[]{:S(2)}) collective-permute-start(bf16[2,752,512]{2,1,0:T(8,128)(2,1)} %get-tuple-element.106), channel_id=1, source_target_pairs={{0,2},{2,0},{1,3},{3,1},{4,6},{6,4},{5,7},{7,5},{8,10},{10,8},{9,1... | collective-permute-start | bytes 4620296 | tf_op jit(solution)/shard_map/ppermute | solution.py:51
  202.9 13.1 %collective-permute-start.7 = (bf16[224,1024]{1,0:T(8,128)(2,1)}, bf16[224,1024]{1,0:T(8,128)(2,1)S(1)}, u32[]{:S(2)}, u32[]{:S(2)}) collective-permute-start(bf16[224,1024]{1,0:T(8,128)(2,1)} %get-tuple-element.104.refs_3_), channel_id=1, source_target_pairs={{0,1},{1,0},{2,3},{3,2},{4,5},{5,4},{6,7},{7,6},{8,9},{9,8},{10,11... | collective-permute-start | bytes 1376264 | tf_op jit(solution)/shard_map/ppermute | solution.py:51
  206.5 1.1 copy-start.4
  216.0 0.8 copy-start.11
  216.0 36.0 %collective-permute-start.11 = (bf16[750,1024]{1,0:T(8,128)(2,1)}, bf16[750,1024]{1,0:T(8,128)(2,1)}, u32[]{:S(2)}, u32[]{:S(2)}) collective-permute-start(bf16[750,1024]{1,0:T(8,128)(2,1)} %get-tuple-element.141.mine), channel_id=1, source_target_pairs={{0,1},{1,0},{2,3},{3,2},{4,5},{5,4},{6,7},{7,6},{8,9},{9,8},{10,11... | collective-permute-start | bytes 4608008 | tf_op jit(solution)/shard_map/ppermute | solution.py:51
  216.8 12.3 %copy-start.2 = (f32[224,1024]{1,0:T(8,128)S(1)}, f32[224,1024]{1,0:T(8,128)}, u32[]{:S(2)}) copy-start(f32[224,1024]{1,0:T(8,128)} %get-tuple-element.87.rows) | copy-start | bytes 2752516
  216.8 12.3 %copy-start.10 = (bf16[224,1024]{1,0:T(8,128)(2,1)S(1)}, bf16[224,1024]{1,0:T(8,128)(2,1)}, u32[]{:S(2)}) copy-start(bf16[224,1024]{1,0:T(8,128)(2,1)} %get-tuple-element.103) | copy-start | bytes 1376260
  229.0 2.1 collective-permute-start.8
  231.1 0.8 copy-start.12
  236.6 16.2 %copy-start.7 = (bf16[224,1024]{1,0:T(8,128)(2,1)S(1)}, bf16[224,1024]{1,0:T(8,128)(2,1)}, u32[]{:S(2)}) copy-start(bf16[224,1024]{1,0:T(8,128)(2,1)} %get-tuple-element.122.grad_mine) | copy-start | bytes 1376260
  241.8 2.7 collective-permute-start.10
  252.1 8.6 %collective-permute-start.12 = (bf16[8,112,128]{2,1,0:T(8,128)(2,1)S(1)}, bf16[8,112,128]{2,1,0:T(8,128)(2,1)}, u32[]{:S(2)}, u32[]{:S(2)}) collective-permute-start(bf16[8,112,128]{2,1,0:T(8,128)(2,1)S(1)} %get-tuple-element.142), channel_id=1, source_target_pairs={{0,1},{1,0},{2,3},{3,2},{4,5},{5,4},{6,7},{7,6},{8,9},{9,8},{10,11... | collective-permute-start | bytes 688136 | tf_op jit(solution)/shard_map/ppermute | solution.py:51
  252.8 15.8 %collective-permute-start.9 = (bf16[224,1024]{1,0:T(8,128)(2,1)S(1)}, bf16[224,1024]{1,0:T(8,128)(2,1)S(1)}, u32[]{:S(2)}, u32[]{:S(2)}) collective-permute-start(bf16[224,1024]{1,0:T(8,128)(2,1)S(1)} %copy-done.7), channel_id=1, source_target_pairs={{0,1},{1,0},{2,3},{3,2},{4,5},{5,4},{6,7},{7,6},{8,9},{9,8},{10,11... | collective-permute-start | bytes 1376264 | tf_op jit(solution)/shard_map/ppermute | solution.py:51
  260.7 17.0 %copy-start.1 = (bf16[8,8,16,1024]{3,2,1,0:T(8,128)(2,1)S(1)}, bf16[8,8,16,1024]{3,2,1,0:T(8,128)(2,1)}, u32[]{:S(2)}) copy-start(bf16[8,8,16,1024]{3,2,1,0:T(8,128)(2,1)} %param.24) | copy-start | bytes 6291460
  262.5 11.3 %all-to-all-start = ((bf16[8,112,128]{2,1,0:T(8,128)(2,1)}), bf16[8,112,128]{2,1,0:T(8,128)(2,1)S(1)}, u32[]{:S(2)}, u32[]{:S(2)}) async-start(bf16[8,112,128]{2,1,0:T(8,128)(2,1)} %add_convert_fusion.1), calls=%async_computation | async-start | bytes 458752 | tf_op jit(solution)/shard_map/all_to_all | solution.py:699
  268.7 0.8 copy-start.9
  273.8 0.7 copy-start.5
Sparse Core Ops, SparseCore 0:
  10.8 77.0 all-gather.4
  90.5 72.8 all-gather.6

commit v5 on v4

--- a/solution.py
+++ b/solution.py
@@ -264,38 +264,53 @@
 
 
 def units_kernel(
-    normed, up_low, down_back, cotangent, up, down, up_in, up_out, down_in, down_out,
-    branch, grad_normed, table_up_in, table_up_out, table_down_in, table_down_out,
-    acc, back, low_acc, back_low,
+    normed, up_low, down_back, cotangent, up, down, up_in, up_out, down_in,
+    grad_normed, table_up_in, active, grad_units,
+    back, back_low,
 ):
     @at_first()
     def _():
-        acc[...] = jnp.zeros_like(acc)
         back[...] = jnp.zeros_like(back)
-        low_acc[...] = jnp.zeros_like(low_acc)
         back_low[...] = jnp.zeros_like(back_low)
 
-    up_rows, down_rows = matrix(up), matrix(down)
+    up_rows = matrix(up)
     value = mm(normed[...], up_rows) + mm(up_low[...], up_out[...])
     spread = 1.0 + lax.erf(value * 0.7071067811865476)
-    act = (0.5 * value * spread).astype(BF)
+    active[...] = (0.5 * value * spread).astype(BF)
     slope = 0.5 * spread + value * (0.3989422804014327 * jnp.exp(-0.5 * value * value))
-    acc[...] += mm_nt(act, down_rows)
-    low_acc[...] += mm_nt(act, down_in[...])
-    grad_act = mm(cotangent[...], down_rows) + mm(down_back[...], down_in[...])
+    grad_act = mm(cotangent[...], matrix(down)) + mm(down_back[...], down_in[...])
     grad = (grad_act * slope).astype(BF)
+    grad_units[...] = grad
     back[...] += mm_nt(grad, up_rows)
     back_low[...] += mm_nt(grad, up_out[...])
-    table_up_out[...] = mm_tn(up_low[...], grad)
-    table_down_in[...] = mm_tn(down_back[...], act)
 
     @at_last()
     def _():
-        down_low = low_acc[...].astype(BF)
-        branch[...] = (acc[...] + mm(down_low, down_out[...])).astype(BF)
         up_back = back_low[...].astype(BF)
         grad_normed[...] = (back[...] + mm(up_back, up_in[...])).astype(BF)
         table_up_in[...] = mm_tn(up_back, normed[...])
+
+
+def units_out_kernel(
+    active, grad_units, up_low, down_back, cotangent, down, down_in, down_out,
+    branch, table_up_out, table_down_in, table_down_out,
+    acc, low_acc,
+):
+    @at_first()
+    def _():
+        acc[...] = jnp.zeros_like(acc)
+        low_acc[...] = jnp.zeros_like(low_acc)
+
+    act = active[...]
+    acc[...] += mm_nt(act, matrix(down))
+    low_acc[...] += mm_nt(act, down_in[...])
+    table_up_out[...] = mm_tn(up_low[...], grad_units[...])
+    table_down_in[...] = mm_tn(down_back[...], act)
+
+    @at_last()
+    def _():
+        down_low = low_acc[...].astype(BF)
+        branch[...] = (acc[...] + mm(down_low, down_out[...])).astype(BF)
         table_down_out[...] = mm_tn(down_low, cotangent[...])
 
 
@@ -822,7 +837,10 @@
         ],
         name="third_norm",
     )
-    branch, grad_n3, up_in_t, up_out_t, down_in_t, down_out_t = call(
+    def unit_rows(array):
+        return array, pl.BlockSpec((rows, chunk), lambda i: (0, i))
+
+    grad_n3, up_in_t, active, grad_units = call(
         units_kernel,
         units // chunk,
         [
@@ -835,19 +853,38 @@
             whole(up_in),
             unit_cols(up_out),
             unit_cols(down_in),
-            whole(down_out),
-        ],
-        [
-            out((rows, width), BF),
+        ],
+        [
             out((rows, width), BF),
             out((rank, width), F32),
+            unit_rows(shape((rows, units), BF)),
+            unit_rows(shape((rows, units), BF)),
+        ],
+        [wide_acc, rank_acc],
+        name="units",
+        cost=11,
+    )
+    branch, up_out_t, down_in_t, down_out_t = call(
+        units_out_kernel,
+        units // chunk,
+        [
+            unit_rows(active),
+            unit_rows(grad_units),
+            whole(up_low),
+            whole(down_back),
+            whole(cotangent),
+            unit_weight(1),
+            unit_cols(down_in),
+            whole(down_out),
+        ],
+        [
+            out((rows, width), BF),
             unit_cols(shape((rank, units), F32)),
             unit_cols(shape((rank, units), F32)),
             out((rank, width), F32),
         ],
-        [wide_acc, wide_acc, rank_acc, rank_acc],
-        name="units",
-        cost=11,
+        [wide_acc, rank_acc],
+        name="units_out",
     )
     grad_n3, grad_n3_other = with_other(grad_n3, "tp")
     branch, grad_n3_other = ordered(branch, grad_n3_other)

time: 285 us -> 284 us (level)
  waiting for transfers between devices: 131 us -> 126 us
  Pallas kernels: 106 us -> 109 us
    ppermute x13, waiting for transfers between devices: 47.8 us -> 42.6 us  [swap(): return lax.ppermute(value, axis, [(0, 1), (1, 0)])]
    pallas_call x15 -> x16, Pallas kernels: 106 us -> 109 us  [call(): return run(*arrays) if scalars is None else run(scalars, *arrays)]
  transfers between devices with their start and end apart: 16 -> 16, of which waited for: 13 -> 13; matrix products, arithmetic and copies ran while one was open for 5% -> 5% of each run, Pallas kernels for 32% -> 34%
where the time goes in v5:
time: 284 us; the launch traced here: 283 us
  waiting for transfers between devices  126 us (44%)
  Pallas kernels  109 us (38%)
  between operations  14.9 us (5%)
  starting transfers between devices  14 us (5%)
  local copies, waits for them, and re-layouts  13.5 us (5%)
  other arithmetic  5.55 us (2%)
    pallas_call x16, Pallas kernels, call(): return run(*arrays) if scalars is None else run(scalars, *arrays)  109 us
    all_gather x1, waiting for transfers between devices, on_device(): attn_full = lax.all_gather(attn_half, ('fsdp', 'ctx'), axis=0)  74.4 us
    ppermute x13, waiting for transfers between devices, swap(): return lax.ppermute(value, axis, [(0, 1), (1, 0)])  42.6 us
    ppermute x13, starting transfers between devices, swap(): return lax.ppermute(value, axis, [(0, 1), (1, 0)])  10.6 us
    all_gather x1, waiting for transfers between devices, on_device(): ff_full = lax.all_gather(ff_half, ('fsdp', 'ctx'), axis=0)  7.36 us
    unnamed x32, local copies, waits for them, and re-layouts  5.74 us
  transfers between devices with their start and end apart: 16, of which 13 were waited for; matrix products, arithmetic and copies ran while one was open for 5% of the time, Pallas kernels for 34%

profile of v5, /device:TPU:0, one launch (start us, length us, event | category | flops | bytes accessed | tf_op | source)
XLA Modules:
  0.0 282.7 jit_solution(574117882929088676)
XLA Ops:
  7.3 2.0 halves.1
  11.0 1.7 dynamic-slice_bitcast_fusion.5.low_out.query_out.refs_10_
  13.4 74.4 %all-gather.5.cloned.1.call-done = bf16[128,64,512]{2,1,0:T(8,128)(2,1)} async-done(((bf16[8,64,512]{2,1,0:T(8,128)(2,1)}), bf16[128,64,512]{2,1,0:T(8,128)(2,1)}) %all-gather.5.cloned.1.call-update) | async-done | bytes 8388624 | tf_op jit(solution)/shard_map/all_gather | solution.py:627
  87.8 7.1 %frames.1 = (bf16[2,752,512]{2,1,0:T(8,128)(2,1)}, bf16[2,750,16]{2,1,0:T(8,128)(2,1)}) custom-call(bf16[750,1024]{1,0:T(8,128)(2,1)} %bitcast.57, bf16[16,8,64,512]{3,2,1,0:T(8,128)(2,1)} %bitcast.39, bf16[8,16,1024]{2,1,0:T(8,128)(2,1)} %dynamic-slice_bitcast_fusion.3.low_in.query_in.refs_9_, ...), custom_call_target="tpu_custom_call" | custom-call | flops 70000000 | bytes 258300 | tf_op jit(solution)/shard_map/frames/pallas_call | solution.py:561
  95.2 5.8 %qkv.1 = (bf16[224,1024]{1,0:T(8,128)(2,1)}, bf16[224,512]{1,0:T(8,128)(2,1)}, bf16[2,224,512]{2,1,0:T(8,128)(2,1)}, bf16[3,224,16]{2,1,0:T(8,128)(2,1)}) custom-call(bf16[224,1024]{1,0:T(8,128)(2,1)} %bitcast.59, f32[3,1024]{1,0:T(4,128)} %gains.9, bf16[16,8,64,512]{3,2,1,0:T(8,128)(2,1)} %bitcast.40, ...), custom_call_target="tpu_custom_call" | custom-call | flops 50000000 | bytes 184500 | tf_op jit(solution)/shard_map/qkv/pallas_call | solution.py:561
  102.7 1.7 dynamic-slice_bitcast_fusion.2.low_out.refs_7_
  105.1 7.3 %self_attention.1 = (bf16[224,512]{1,0:T(8,128)(2,1)}, f32[4,2,224]{2,1,0:T(2,128)}, bf16[224,1024]{1,0:T(8,128)(2,1)}, bf16[224,16]{1,0:T(8,128)(2,1)}) custom-call(s32[3]{0:T(128)} %pad_add_fusion.where.refs_0_, bf16[224,512]{1,0:T(8,128)(2,1)} %get-tuple-element.83.query.refs_11_, bf16[2,224,512]{2,1,0:T(8,128)(2,1)} %get-tuple-element.84.mine.refs_13_, ...), custom_call_target="tpu_custom_call" | custom-call | flops 70000000 | bytes 258300 | tf_op jit(solution)/shard_map/self_attention/pallas_call | solution.py:561
  112.4 1.6 collective-permute-start.1
  114.0 11.4 %collective-permute-done.1.branch_other = bf16[224,1024]{1,0:T(8,128)(2,1)S(1)} collective-permute-done((bf16[224,1024]{1,0:T(8,128)(2,1)}, bf16[224,1024]{1,0:T(8,128)(2,1)S(1)}, u32[]{:S(2)}, u32[]{:S(2)}) %collective-permute-start.1) | collective-permute-done | bytes 458784 | tf_op jit(solution)/shard_map/ppermute | solution.py:51
  126.2 14.1 %cross_attention.1 = (f32[224,1024]{1,0:T(8,128)}, bf16[224,1024]{1,0:T(8,128)(2,1)}, bf16[224,512]{1,0:T(8,128)(2,1)}, bf16[224,16]{1,0:T(8,128)(2,1)}, bf16[22...) custom-call(bf16[224,1024]{1,0:T(8,128)(2,1)} %bitcast.60, ...), custom_call_target="tpu_custom_call" | custom-call | flops 130000000 | bytes 479700 | tf_op jit(solution)/shard_map/cross_attention/pallas_call | solution.py:561
  140.3 1.6 collective-permute-start.3
  144.8 7.6 %collective-permute-done.3.branch_other = bf16[224,1024]{1,0:T(8,128)(2,1)S(1)} collective-permute-done((bf16[224,1024]{1,0:T(8,128)(2,1)}, bf16[224,1024]{1,0:T(8,128)(2,1)S(1)}, u32[]{:S(2)}, u32[]{:S(2)}) %collective-permute-start.3) | collective-permute-done | bytes 458784 | tf_op jit(solution)/shard_map/ppermute | solution.py:51
  153.1 2.9 %third_norm.1 = (f32[224,1024]{1,0:T(8,128)}, bf16[224,1024]{1,0:T(8,128)(2,1)}, bf16[224,16]{1,0:T(8,128)(2,1)}, bf16[224,16]{1,0:T(8,128)(2,1)}) custom-call(f32[224,1024]{1,0:T(8,128)} %get-tuple-element.87.middle.refs_1_, bf16[224,1024]{1,0:T(8,128)(2,1)} %get-tuple-element.88.branch_mine, bf16[224,1024]{1,0:T(8,128)(2,1)} %copy-done.8, ...), custom_call_target="tpu_custom_call" | custom-call | flops 50000000 | bytes 184500 | tf_op jit(solution)/shard_map/third_norm/pallas_call | solution.py:561
  156.1 7.4 %all-gather.7.cloned.1.call-done = bf16[32,64,2048]{2,1,0:T(8,128)(2,1)} async-done(((bf16[2,64,2048]{2,1,0:T(8,128)(2,1)}), bf16[32,64,2048]{2,1,0:T(8,128)(2,1)}) %all-gather.7.cloned.1.call-update) | async-done | bytes 8388624 | tf_op jit(solution)/shard_map/all_gather | solution.py:628
  163.4 8.2 %units.1 = (bf16[224,1024]{1,0:T(8,128)(2,1)}, f32[16,1024]{1,0:T(8,128)}, bf16[224,2048]{1,0:T(8,128)(2,1)}, bf16[224,2048]{1,0:T(8,128)(2,1)}) custom-call(bf16[224,1024]{1,0:T(8,128)(2,1)} %get-tuple-element.90.normed, bf16[224,16]{1,0:T(8,128)(2,1)} %get-tuple-element.91.up_low, bf16[224,16]{1,0:T(8,128)(2,1)} %get-tuple-element.92.down_back, ...), custom_call_target="tpu_custom_call" | custom-call | flops 110000000 | bytes 405900 | tf_op jit(solution)/shard_map/units/pallas_call | solution.py:561
  173.1 5.2 %units_out.1 = (bf16[224,1024]{1,0:T(8,128)(2,1)}, f32[16,2048]{1,0:T(8,128)}, f32[16,2048]{1,0:T(8,128)}, f32[16,1024]{1,0:T(8,128)}) custom-call(bf16[224,2048]{1,0:T(8,128)(2,1)} %get-tuple-element.94.active, bf16[224,2048]{1,0:T(8,128)(2,1)} %get-tuple-element.95.grad_units, bf16[224,16]{1,0:T(8,128)(2,1)} %get-tuple-element.91.up_low, ...), custom_call_target="tpu_custom_call" | custom-call | flops 50000000 | bytes 184500 | tf_op jit(solution)/shard_map/units_out/pallas_call | solution.py:561
  178.4 6.2 %collective-permute-done.4.grad_other = bf16[224,1024]{1,0:T(8,128)(2,1)S(1)} collective-permute-done((bf16[224,1024]{1,0:T(8,128)(2,1)}, bf16[224,1024]{1,0:T(8,128)(2,1)S(1)}, u32[]{:S(2)}, u32[]{:S(2)}) %collective-permute-start.4) | collective-permute-done | bytes 458784 | tf_op jit(solution)/shard_map/ppermute | solution.py:51
  186.0 15.0 %cross_back.1 = (f32[224,1024]{1,0:T(8,128)}, bf16[224,1024]{1,0:T(8,128)(2,1)}, bf16[2,752,512]{2,1,0:T(8,128)(2,1)}, bf16[2,752,512]{2,1,0:T(8,128)(2,1)}, f32...) custom-call(bf16[224,1024]{1,0:T(8,128)(2,1)} %bitcast.56, ...), custom_call_target="tpu_custom_call" | custom-call | flops 180000000 | bytes 664200 | tf_op jit(solution)/shard_map/cross_back/pallas_call | solution.py:561
  201.9 2.7 collective-permute-done.6.grad_other
  205.8 8.4 %frames_back.1 = (bf16[750,1024]{1,0:T(8,128)(2,1)}, f32[2,16,1024]{2,1,0:T(8,128)}, f32[2,16,512]{2,1,0:T(8,128)}) custom-call(bf16[2,752,512]{2,1,0:T(8,128)(2,1)} %get-tuple-element.109.grad_mine, bf16[2,752,512]{2,1,0:T(8,128)(2,1)} %copy-done.4, bf16[16,8,64,512]{3,2,1,0:T(8,128)(2,1)} %bitcast.46, ...), custom_call_target="tpu_custom_call" | custom-call | flops 90000000 | bytes 332100 | tf_op jit(solution)/shard_map/frames_back/pallas_call | solution.py:561
  215.0 12.2 %self_back.1 = (f32[224,1024]{1,0:T(8,128)}, f32[224,1024]{1,0:T(8,128)}, bf16[2,224,512]{2,1,0:T(8,128)(2,1)}, bf16[2,224,512]{2,1,0:T(8,128)(2,1)}, f32[16,512...) custom-call(s32[3]{0:T(128)} %pad_add_fusion.where.refs_0_, ...), custom_call_target="tpu_custom_call" | custom-call | flops 120000000 | bytes 442800 | tf_op jit(solution)/shard_map/self_back/pallas_call | solution.py:561
  230.1 4.7 %self_project_back.1 = (bf16[224,1024]{1,0:T(8,128)(2,1)}, f32[2,16,1024]{2,1,0:T(8,128)}, f32[2,16,512]{2,1,0:T(8,128)}) custom-call(bf16[2,224,512]{2,1,0:T(8,128)(2,1)} %get-tuple-element.123.grad_mine, bf16[2,224,512]{2,1,0:T(8,128)(2,1)} %copy-done.12, bf16[16,8,64,512]{3,2,1,0:T(8,128)(2,1)} %bitcast.49, ...), custom_call_target="tpu_custom_call" | custom-call | flops 50000000 | bytes 184500 | tf_op jit(solution)/shard_map/self_project_back/pallas_call | solution.py:561
  234.7 5.2 %pack.1 = (f32[2,8,112,128]{3,2,1,0:T(8,128)}, f32[2,8,112,128]{3,2,1,0:T(8,128)}) custom-call(s32[3]{0:T(128)} %pad_add_fusion.where.refs_0_, f32[16,1024]{1,0:T(8,128)} %get-tuple-element.127.refs_1_, f32[2,16,1024]{2,1,0:T(8,128)} %get-tuple-element.128.refs_2_, f32[16,1024]{1,0:T(8,128)} %get-tuple-element.129.refs_3_, ...), custom_call_target="tpu_custom_call" | custom-call | flops 50000000 | bytes 184500 | tf_op jit(solution)/shard_map/pack/pallas_call | solution.py:561
  240.1 2.5 collective-permute-done.10
  243.9 6.4 %collective-permute-done.11.other = bf16[750,1024]{1,0:T(8,128)(2,1)} collective-permute-done((bf16[750,1024]{1,0:T(8,128)(2,1)}, bf16[750,1024]{1,0:T(8,128)(2,1)}, u32[]{:S(2)}, u32[]{:S(2)}) %collective-permute-start.11) | collective-permute-done | bytes 1536032 | tf_op jit(solution)/shard_map/ppermute | solution.py:51
  252.3 4.6 %encoder_total.1 = f32[750,1,1024]{2,1,0:T(1,128)} custom-call(bf16[750,1024]{1,0:T(8,128)(2,1)} %get-tuple-element.145.mine, bf16[750,1024]{1,0:T(8,128)(2,1)} %collective-permute-done.11.other), custom_call_target="tpu_custom_call" | custom-call | flops 50000000 | bytes 184500 | tf_op jit(solution)/shard_map/encoder_total/pallas_call | solution.py:561
  256.9 1.9 collective-permute-done.12
  258.8 1.8 add_convert_fusion.1
  260.7 3.4 %all-to-all-start = ((bf16[8,112,128]{2,1,0:T(8,128)(2,1)}), bf16[8,112,128]{2,1,0:T(8,128)(2,1)S(1)}, u32[]{:S(2)}, u32[]{:S(2)}) async-start(bf16[8,112,128]{2,1,0:T(8,128)(2,1)} %add_convert_fusion.1), calls=%async_computation | async-start | bytes 458752 | tf_op jit(solution)/shard_map/all_to_all | solution.py:714
  264.1 2.8 collective-permute-done.9.grad_other
  267.6 3.2 %hidden_total.1 = f32[224,1024]{1,0:T(8,128)} custom-call(bf16[224,1024]{1,0:T(8,128)(2,1)} %bitcast.61, f32[3,1024]{1,0:T(4,128)} %gains.9, f32[224,1024]{1,0:T(8,128)} %get-tuple-element.122.carried, bf16[224,1024]{1,0:T(8,128)(2,1)} %get-tuple-element.126.grad_mine, bf16[224,1024]{1,0:T(8,128)(2,1)} %copy-done.9), custom_call_target="tpu_custom_call" | custom-call | flops 50000000 | bytes 184500 | tf_op jit(solution)/shard_map/hidden_total/pallas_call | solution.py:561
  272.7 3.1 %unpack.1 = (f32[8,8,16,32]{3,2,1,0:T(8,128)}, f32[8,8,16,32]{3,2,1,0:T(8,128)}, f32[8,16,32]{2,1,0:T(8,128)}, f32[8,16,128]{2,1,0:T(8,128)}, f32[8,16,128]{2,1,0:T(8,128)}, /*index=5*/f32[8,16,32]{2,1,0:T(8,128)}) custom-call(bf16[8,112,128]{2,1,0:T(8,128)(2,1)} %copy-done.5), custom_call_target="tpu_custom_call" | custom-call | flops 50000000 | bytes 184500 | tf_op jit(solution)/shard_map/unpack/pallas_call | solution.py:561
  (62 shorter events, 23.8 us)
Async XLA Ops:
  7.2 5.5 %copy-start = (bf16[8,8,16,1024]{3,2,1,0:T(8,128)(2,1)S(1)}, bf16[8,8,16,1024]{3,2,1,0:T(8,128)(2,1)}, u32[]{:S(2)}) copy-start(bf16[8,8,16,1024]{3,2,1,0:T(8,128)(2,1)} %param.24) | copy-start | bytes 6291460
  7.2 2.2 copy-start.14
  7.2 2.2 copy-start.15
  7.2 80.6 %all-gather.5.cloned.1.call-start = ((), (), s32[]{:S(2)}) async-start(), calls=%async_computation.1 | async-start | bytes 8912896 | tf_op jit(solution)/shard_map/all_gather | solution.py:627
  9.3 154.2 %all-gather.7.cloned.1.call-start = ((), (), s32[]{:S(2)}) async-start(), calls=%async_computation.2 | async-start | bytes 8912896 | tf_op jit(solution)/shard_map/all_gather | solution.py:628
  94.9 30.4 %collective-permute-start.2 = (bf16[2,752,512]{2,1,0:T(8,128)(2,1)}, bf16[2,752,512]{2,1,0:T(8,128)(2,1)}, u32[]{:S(2)}, u32[]{:S(2)}) collective-permute-start(bf16[2,752,512]{2,1,0:T(8,128)(2,1)} %get-tuple-element.86.mine), channel_id=1, source_target_pairs={{0,2},{2,0},{1,3},{3,1},{4,6},{6,4},{5,7},{7,5},{8,10},{10,8},{9,1... | collective-permute-start | bytes 4620296 | tf_op jit(solution)/shard_map/ppermute | solution.py:51
  101.0 3.4 %collective-permute-start = (bf16[2,224,512]{2,1,0:T(8,128)(2,1)}, bf16[2,224,512]{2,1,0:T(8,128)(2,1)S(1)}, u32[]{:S(2)}, u32[]{:S(2)}) collective-permute-start(bf16[2,224,512]{2,1,0:T(8,128)(2,1)} %get-tuple-element.84.mine.refs_13_), channel_id=1, source_target_pairs={{0,2},{2,0},{1,3},{3,1},{4,6},{6,4},{5,7},{7,5},{8,10},{10,8},{9,1... | collective-permute-start | bytes 1376264 | tf_op jit(solution)/shard_map/ppermute | solution.py:51
  104.4 0.8 copy-start.3
  112.4 12.9 %collective-permute-start.1 = (bf16[224,1024]{1,0:T(8,128)(2,1)}, bf16[224,1024]{1,0:T(8,128)(2,1)S(1)}, u32[]{:S(2)}, u32[]{:S(2)}) collective-permute-start(bf16[224,1024]{1,0:T(8,128)(2,1)} %get-tuple-element.85.branch_mine), channel_id=1, source_target_pairs={{0,1},{1,0},{2,3},{3,2},{4,5},{5,4},{6,7},{7,6},{8,9},{9,8},{10,11... | collective-permute-start | bytes 1376264 | tf_op jit(solution)/shard_map/ppermute | solution.py:51
  125.4 0.8 copy-start.13
  140.3 12.1 %collective-permute-start.3 = (bf16[224,1024]{1,0:T(8,128)(2,1)}, bf16[224,1024]{1,0:T(8,128)(2,1)S(1)}, u32[]{:S(2)}, u32[]{:S(2)}) collective-permute-start(bf16[224,1024]{1,0:T(8,128)(2,1)} %get-tuple-element.88.branch_mine), channel_id=1, source_target_pairs={{0,1},{1,0},{2,3},{3,2},{4,5},{5,4},{6,7},{7,6},{8,9},{9,8},{10,11... | collective-permute-start | bytes 1376264 | tf_op jit(solution)/shard_map/ppermute | solution.py:51
  152.4 0.8 copy-start.8
  171.6 12.9 %collective-permute-start.4 = (bf16[224,1024]{1,0:T(8,128)(2,1)}, bf16[224,1024]{1,0:T(8,128)(2,1)S(1)}, u32[]{:S(2)}, u32[]{:S(2)}) collective-permute-start(bf16[224,1024]{1,0:T(8,128)(2,1)} %get-tuple-element.93.grad_mine), channel_id=1, source_target_pairs={{0,1},{1,0},{2,3},{3,2},{4,5},{5,4},{6,7},{7,6},{8,9},{9,8},{10,11... | collective-permute-start | bytes 1376264 | tf_op jit(solution)/shard_map/ppermute | solution.py:51
  184.5 1.5 copy-start.6
  184.5 16.5 %collective-permute-start.5 = (bf16[224,1024]{1,0:T(8,128)(2,1)}, bf16[224,1024]{1,0:T(8,128)(2,1)S(1)}, u32[]{:S(2)}, u32[]{:S(2)}) collective-permute-start(bf16[224,1024]{1,0:T(8,128)(2,1)} %get-tuple-element.107), channel_id=1, source_target_pairs={{0,1},{1,0},{2,3},{3,2},{4,5},{5,4},{6,7},{7,6},{8,9},{9,8},{10,11... | collective-permute-start | bytes 1376264 | tf_op jit(solution)/shard_map/ppermute | solution.py:51
  201.0 3.6 %collective-permute-start.6 = (bf16[2,752,512]{2,1,0:T(8,128)(2,1)}, bf16[2,752,512]{2,1,0:T(8,128)(2,1)S(1)}, u32[]{:S(2)}, u32[]{:S(2)}) collective-permute-start(bf16[2,752,512]{2,1,0:T(8,128)(2,1)} %get-tuple-element.110), channel_id=1, source_target_pairs={{0,2},{2,0},{1,3},{3,1},{4,6},{6,4},{5,7},{7,5},{8,10},{10,8},{9,1... | collective-permute-start | bytes 4620296 | tf_op jit(solution)/shard_map/ppermute | solution.py:51
  201.1 13.1 %collective-permute-start.7 = (bf16[224,1024]{1,0:T(8,128)(2,1)}, bf16[224,1024]{1,0:T(8,128)(2,1)S(1)}, u32[]{:S(2)}, u32[]{:S(2)}) collective-permute-start(bf16[224,1024]{1,0:T(8,128)(2,1)} %get-tuple-element.108.refs_3_), channel_id=1, source_target_pairs={{0,1},{1,0},{2,3},{3,2},{4,5},{5,4},{6,7},{7,6},{8,9},{9,8},{10,11... | collective-permute-start | bytes 1376264 | tf_op jit(solution)/shard_map/ppermute | solution.py:51
  204.6 1.1 copy-start.4
  214.2 0.8 copy-start.11
  214.2 36.0 %collective-permute-start.11 = (bf16[750,1024]{1,0:T(8,128)(2,1)}, bf16[750,1024]{1,0:T(8,128)(2,1)}, u32[]{:S(2)}, u32[]{:S(2)}) collective-permute-start(bf16[750,1024]{1,0:T(8,128)(2,1)} %get-tuple-element.145.mine), channel_id=1, source_target_pairs={{0,1},{1,0},{2,3},{3,2},{4,5},{5,4},{6,7},{7,6},{8,9},{9,8},{10,11... | collective-permute-start | bytes 4608008 | tf_op jit(solution)/shard_map/ppermute | solution.py:51
  215.0 12.4 %copy-start.2 = (f32[224,1024]{1,0:T(8,128)S(1)}, f32[224,1024]{1,0:T(8,128)}, u32[]{:S(2)}) copy-start(f32[224,1024]{1,0:T(8,128)} %get-tuple-element.89.rows) | copy-start | bytes 2752516
  215.0 12.4 %copy-start.10 = (bf16[224,1024]{1,0:T(8,128)(2,1)S(1)}, bf16[224,1024]{1,0:T(8,128)(2,1)}, u32[]{:S(2)}) copy-start(bf16[224,1024]{1,0:T(8,128)(2,1)} %get-tuple-element.107) | copy-start | bytes 1376260
  227.2 2.1 collective-permute-start.8
  229.3 0.8 copy-start.12
  234.7 16.3 %copy-start.7 = (bf16[224,1024]{1,0:T(8,128)(2,1)S(1)}, bf16[224,1024]{1,0:T(8,128)(2,1)}, u32[]{:S(2)}) copy-start(bf16[224,1024]{1,0:T(8,128)(2,1)} %get-tuple-element.126.grad_mine) | copy-start | bytes 1376260
  239.9 2.7 collective-permute-start.10
  250.3 8.6 %collective-permute-start.12 = (bf16[8,112,128]{2,1,0:T(8,128)(2,1)S(1)}, bf16[8,112,128]{2,1,0:T(8,128)(2,1)}, u32[]{:S(2)}, u32[]{:S(2)}) collective-permute-start(bf16[8,112,128]{2,1,0:T(8,128)(2,1)S(1)} %get-tuple-element.146), channel_id=1, source_target_pairs={{0,1},{1,0},{2,3},{3,2},{4,5},{5,4},{6,7},{7,6},{8,9},{9,8},{10,11... | collective-permute-start | bytes 688136 | tf_op jit(solution)/shard_map/ppermute | solution.py:51
  251.0 15.9 %collective-permute-start.9 = (bf16[224,1024]{1,0:T(8,128)(2,1)S(1)}, bf16[224,1024]{1,0:T(8,128)(2,1)S(1)}, u32[]{:S(2)}, u32[]{:S(2)}) collective-permute-start(bf16[224,1024]{1,0:T(8,128)(2,1)S(1)} %copy-done.7), channel_id=1, source_target_pairs={{0,1},{1,0},{2,3},{3,2},{4,5},{5,4},{6,7},{7,6},{8,9},{9,8},{10,11... | collective-permute-start | bytes 1376264 | tf_op jit(solution)/shard_map/ppermute | solution.py:51
  258.8 17.0 %copy-start.1 = (bf16[8,8,16,1024]{3,2,1,0:T(8,128)(2,1)S(1)}, bf16[8,8,16,1024]{3,2,1,0:T(8,128)(2,1)}, u32[]{:S(2)}) copy-start(bf16[8,8,16,1024]{3,2,1,0:T(8,128)(2,1)} %param.24) | copy-start | bytes 6291460
  260.7 11.3 %all-to-all-start = ((bf16[8,112,128]{2,1,0:T(8,128)(2,1)}), bf16[8,112,128]{2,1,0:T(8,128)(2,1)S(1)}, u32[]{:S(2)}, u32[]{:S(2)}) async-start(bf16[8,112,128]{2,1,0:T(8,128)(2,1)} %add_convert_fusion.1), calls=%async_computation | async-start | bytes 458752 | tf_op jit(solution)/shard_map/all_to_all | solution.py:714
  266.9 0.8 copy-start.9
  272.0 0.7 copy-start.5
Sparse Core Ops, SparseCore 0:
  10.8 77.0 all-gather.4
  90.5 72.8 all-gather.6

commit v6 on v5

--- a/solution.py
+++ b/solution.py
@@ -265,7 +265,7 @@
 
 def units_kernel(
     normed, up_low, down_back, cotangent, up, down, up_in, up_out, down_in,
-    grad_normed, table_up_in, active, grad_units,
+    grad_normed, up_back, active, grad_units,
     back, back_low,
 ):
     @at_first()
@@ -286,14 +286,14 @@
 
     @at_last()
     def _():
-        up_back = back_low[...].astype(BF)
-        grad_normed[...] = (back[...] + mm(up_back, up_in[...])).astype(BF)
-        table_up_in[...] = mm_tn(up_back, normed[...])
+        rank_rows = back_low[...].astype(BF)
+        up_back[...] = rank_rows
+        grad_normed[...] = (back[...] + mm(rank_rows, up_in[...])).astype(BF)
 
 
 def units_out_kernel(
-    active, grad_units, up_low, down_back, cotangent, down, down_in, down_out,
-    branch, table_up_out, table_down_in, table_down_out,
+    active, grad_units, normed, up_low, up_back, down_back, cotangent, down, down_in, down_out,
+    branch, table_up_in, table_up_out, table_down_in, table_down_out,
     acc, low_acc,
 ):
     @at_first()
@@ -312,6 +312,7 @@
         down_low = low_acc[...].astype(BF)
         branch[...] = (acc[...] + mm(down_low, down_out[...])).astype(BF)
         table_down_out[...] = mm_tn(down_low, cotangent[...])
+        table_up_in[...] = mm_tn(up_back[...], normed[...])
 
 
 def attention_back(
@@ -840,7 +841,7 @@
     def unit_rows(array):
         return array, pl.BlockSpec((rows, chunk), lambda i: (0, i))
 
-    grad_n3, up_in_t, active, grad_units = call(
+    grad_n3, up_back, active, grad_units = call(
         units_kernel,
         units // chunk,
         [
@@ -856,7 +857,7 @@
         ],
         [
             out((rows, width), BF),
-            out((rank, width), F32),
+            out((rows, rank), BF),
             unit_rows(shape((rows, units), BF)),
             unit_rows(shape((rows, units), BF)),
         ],
@@ -864,13 +865,15 @@
         name="units",
         cost=11,
     )
-    branch, up_out_t, down_in_t, down_out_t = call(
+    branch, up_in_t, up_out_t, down_in_t, down_out_t = call(
         units_out_kernel,
         units // chunk,
         [
             unit_rows(active),
             unit_rows(grad_units),
+            whole(n3),
             whole(up_low),
+            whole(up_back),
             whole(down_back),
             whole(cotangent),
             unit_weight(1),
@@ -879,6 +882,7 @@
         ],
         [
             out((rows, width), BF),
+            out((rank, width), F32),
             unit_cols(shape((rank, units), F32)),
             unit_cols(shape((rank, units), F32)),
             out((rank, width), F32),

time: 284 us -> 283 us (level)
  no operation moved by 1% of the time
where the time goes in v6:
time: 283 us
  waiting for transfers between devices  125 us (44%)
  Pallas kernels  109 us (39%)
  between operations  14.9 us (5%)
  starting transfers between devices  14.1 us (5%)
  local copies, waits for them, and re-layouts  13.6 us (5%)
  other arithmetic  5.55 us (2%)
    pallas_call x16, Pallas kernels, call(): return run(*arrays) if scalars is None else run(scalars, *arrays)  109 us
    all_gather x1, waiting for transfers between devices, on_device(): attn_full = lax.all_gather(attn_half, ('fsdp', 'ctx'), axis=0)  74.4 us
    ppermute x13, waiting for transfers between devices, swap(): return lax.ppermute(value, axis, [(0, 1), (1, 0)])  42.4 us
    ppermute x13, starting transfers between devices, swap(): return lax.ppermute(value, axis, [(0, 1), (1, 0)])  10.6 us
    all_gather x1, waiting for transfers between devices, on_device(): ff_full = lax.all_gather(ff_half, ('fsdp', 'ctx'), axis=0)  7.39 us
    unnamed x32, local copies, waits for them, and re-layouts  5.75 us
  transfers between devices with their start and end apart: 16, of which 13 were waited for; matrix products, arithmetic and copies ran while one was open for 5% of the time, Pallas kernels for 34%

profile of v6, /device:TPU:0, one launch (start us, length us, event | category | flops | bytes accessed | tf_op | source)
XLA Modules:
  0.0 282.6 jit_solution(7888659133003800141)
XLA Ops:
  7.3 2.0 halves.1
  11.0 1.7 dynamic-slice_bitcast_fusion.5.low_out.query_out.refs_10_
  13.4 74.4 %all-gather.5.cloned.1.call-done = bf16[128,64,512]{2,1,0:T(8,128)(2,1)} async-done(((bf16[8,64,512]{2,1,0:T(8,128)(2,1)}), bf16[128,64,512]{2,1,0:T(8,128)(2,1)}) %all-gather.5.cloned.1.call-update) | async-done | bytes 8388624 | tf_op jit(solution)/shard_map/all_gather | solution.py:628
  87.8 7.1 %frames.1 = (bf16[2,752,512]{2,1,0:T(8,128)(2,1)}, bf16[2,750,16]{2,1,0:T(8,128)(2,1)}) custom-call(bf16[750,1024]{1,0:T(8,128)(2,1)} %bitcast.57, bf16[16,8,64,512]{3,2,1,0:T(8,128)(2,1)} %bitcast.39, bf16[8,16,1024]{2,1,0:T(8,128)(2,1)} %dynamic-slice_bitcast_fusion.3.low_in.query_in.refs_9_, ...), custom_call_target="tpu_custom_call" | custom-call | flops 70000000 | bytes 258300 | tf_op jit(solution)/shard_map/frames/pallas_call | solution.py:562
  95.2 5.8 %qkv.1 = (bf16[224,1024]{1,0:T(8,128)(2,1)}, bf16[224,512]{1,0:T(8,128)(2,1)}, bf16[2,224,512]{2,1,0:T(8,128)(2,1)}, bf16[3,224,16]{2,1,0:T(8,128)(2,1)}) custom-call(bf16[224,1024]{1,0:T(8,128)(2,1)} %bitcast.59, f32[3,1024]{1,0:T(4,128)} %gains.9, bf16[16,8,64,512]{3,2,1,0:T(8,128)(2,1)} %bitcast.40, ...), custom_call_target="tpu_custom_call" | custom-call | flops 50000000 | bytes 184500 | tf_op jit(solution)/shard_map/qkv/pallas_call | solution.py:562
  102.7 1.7 dynamic-slice_bitcast_fusion.2.low_out.refs_7_
  105.1 7.3 %self_attention.1 = (bf16[224,512]{1,0:T(8,128)(2,1)}, f32[4,2,224]{2,1,0:T(2,128)}, bf16[224,1024]{1,0:T(8,128)(2,1)}, bf16[224,16]{1,0:T(8,128)(2,1)}) custom-call(s32[3]{0:T(128)} %pad_add_fusion.where.refs_0_, bf16[224,512]{1,0:T(8,128)(2,1)} %get-tuple-element.84.query.refs_11_, bf16[2,224,512]{2,1,0:T(8,128)(2,1)} %get-tuple-element.85.mine.refs_13_, ...), custom_call_target="tpu_custom_call" | custom-call | flops 70000000 | bytes 258300 | tf_op jit(solution)/shard_map/self_attention/pallas_call | solution.py:562
  112.4 1.6 collective-permute-start.1
  114.0 11.3 %collective-permute-done.1.branch_other = bf16[224,1024]{1,0:T(8,128)(2,1)S(1)} collective-permute-done((bf16[224,1024]{1,0:T(8,128)(2,1)}, bf16[224,1024]{1,0:T(8,128)(2,1)S(1)}, u32[]{:S(2)}, u32[]{:S(2)}) %collective-permute-start.1) | collective-permute-done | bytes 458784 | tf_op jit(solution)/shard_map/ppermute | solution.py:51
  126.2 14.1 %cross_attention.1 = (f32[224,1024]{1,0:T(8,128)}, bf16[224,1024]{1,0:T(8,128)(2,1)}, bf16[224,512]{1,0:T(8,128)(2,1)}, bf16[224,16]{1,0:T(8,128)(2,1)}, bf16[22...) custom-call(bf16[224,1024]{1,0:T(8,128)(2,1)} %bitcast.60, ...), custom_call_target="tpu_custom_call" | custom-call | flops 130000000 | bytes 479700 | tf_op jit(solution)/shard_map/cross_attention/pallas_call | solution.py:562
  140.3 1.6 collective-permute-start.3
  144.8 7.6 %collective-permute-done.3.branch_other = bf16[224,1024]{1,0:T(8,128)(2,1)S(1)} collective-permute-done((bf16[224,1024]{1,0:T(8,128)(2,1)}, bf16[224,1024]{1,0:T(8,128)(2,1)S(1)}, u32[]{:S(2)}, u32[]{:S(2)}) %collective-permute-start.3) | collective-permute-done | bytes 458784 | tf_op jit(solution)/shard_map/ppermute | solution.py:51
  153.1 2.9 %third_norm.1 = (f32[224,1024]{1,0:T(8,128)}, bf16[224,1024]{1,0:T(8,128)(2,1)}, bf16[224,16]{1,0:T(8,128)(2,1)}, bf16[224,16]{1,0:T(8,128)(2,1)}) custom-call(f32[224,1024]{1,0:T(8,128)} %get-tuple-element.88.middle.refs_1_, bf16[224,1024]{1,0:T(8,128)(2,1)} %get-tuple-element.89.branch_mine, bf16[224,1024]{1,0:T(8,128)(2,1)} %copy-done.8, ...), custom_call_target="tpu_custom_call" | custom-call | flops 50000000 | bytes 184500 | tf_op jit(solution)/shard_map/third_norm/pallas_call | solution.py:562
  156.1 7.4 %all-gather.7.cloned.1.call-done = bf16[32,64,2048]{2,1,0:T(8,128)(2,1)} async-done(((bf16[2,64,2048]{2,1,0:T(8,128)(2,1)}), bf16[32,64,2048]{2,1,0:T(8,128)(2,1)}) %all-gather.7.cloned.1.call-update) | async-done | bytes 8388624 | tf_op jit(solution)/shard_map/all_gather | solution.py:629
  163.4 8.1 %units.1 = (bf16[224,1024]{1,0:T(8,128)(2,1)}, bf16[224,16]{1,0:T(8,128)(2,1)}, bf16[224,2048]{1,0:T(8,128)(2,1)}, bf16[224,2048]{1,0:T(8,128)(2,1)}) custom-call(bf16[224,1024]{1,0:T(8,128)(2,1)} %get-tuple-element.91.normed, bf16[224,16]{1,0:T(8,128)(2,1)} %get-tuple-element.92.up_low, bf16[224,16]{1,0:T(8,128)(2,1)} %get-tuple-element.93.down_back, ...), custom_call_target="tpu_custom_call" | custom-call | flops 110000000 | bytes 405900 | tf_op jit(solution)/shard_map/units/pallas_call | solution.py:562
  173.1 5.4 %units_out.1 = (bf16[224,1024]{1,0:T(8,128)(2,1)}, f32[16,1024]{1,0:T(8,128)}, f32[16,2048]{1,0:T(8,128)}, f32[16,2048]{1,0:T(8,128)}, f32[16,1024]{1,0:T(8,128)}) custom-call(bf16[224,2048]{1,0:T(8,128)(2,1)} %get-tuple-element.95.active, bf16[224,2048]{1,0:T(8,128)(2,1)} %get-tuple-element.96.grad_units, bf16[224,1024]{1,0:T(8,128)(2,1)} %get-tuple-element.91.normed, ...), custom_call_target="tpu_custom_call" | custom-call | flops 50000000 | bytes 184500 | tf_op jit(solution)/shard_map/units_out/pallas_call | solution.py:562
  178.5 6.0 %collective-permute-done.4.grad_other = bf16[224,1024]{1,0:T(8,128)(2,1)S(1)} collective-permute-done((bf16[224,1024]{1,0:T(8,128)(2,1)}, bf16[224,1024]{1,0:T(8,128)(2,1)S(1)}, u32[]{:S(2)}, u32[]{:S(2)}) %collective-permute-start.4) | collective-permute-done | bytes 458784 | tf_op jit(solution)/shard_map/ppermute | solution.py:51
  186.0 15.0 %cross_back.1 = (f32[224,1024]{1,0:T(8,128)}, bf16[224,1024]{1,0:T(8,128)(2,1)}, bf16[2,752,512]{2,1,0:T(8,128)(2,1)}, bf16[2,752,512]{2,1,0:T(8,128)(2,1)}, f32...) custom-call(bf16[224,1024]{1,0:T(8,128)(2,1)} %bitcast.56, ...), custom_call_target="tpu_custom_call" | custom-call | flops 180000000 | bytes 664200 | tf_op jit(solution)/shard_map/cross_back/pallas_call | solution.py:562
  201.9 2.7 collective-permute-done.6.grad_other
  205.7 8.4 %frames_back.1 = (bf16[750,1024]{1,0:T(8,128)(2,1)}, f32[2,16,1024]{2,1,0:T(8,128)}, f32[2,16,512]{2,1,0:T(8,128)}) custom-call(bf16[2,752,512]{2,1,0:T(8,128)(2,1)} %get-tuple-element.111.grad_mine, bf16[2,752,512]{2,1,0:T(8,128)(2,1)} %copy-done.4, bf16[16,8,64,512]{3,2,1,0:T(8,128)(2,1)} %bitcast.46, ...), custom_call_target="tpu_custom_call" | custom-call | flops 90000000 | bytes 332100 | tf_op jit(solution)/shard_map/frames_back/pallas_call | solution.py:562
  214.9 12.2 %self_back.1 = (f32[224,1024]{1,0:T(8,128)}, f32[224,1024]{1,0:T(8,128)}, bf16[2,224,512]{2,1,0:T(8,128)(2,1)}, bf16[2,224,512]{2,1,0:T(8,128)(2,1)}, f32[16,512...) custom-call(s32[3]{0:T(128)} %pad_add_fusion.where.refs_0_, ...), custom_call_target="tpu_custom_call" | custom-call | flops 120000000 | bytes 442800 | tf_op jit(solution)/shard_map/self_back/pallas_call | solution.py:562
  230.0 4.7 %self_project_back.1 = (bf16[224,1024]{1,0:T(8,128)(2,1)}, f32[2,16,1024]{2,1,0:T(8,128)}, f32[2,16,512]{2,1,0:T(8,128)}) custom-call(bf16[2,224,512]{2,1,0:T(8,128)(2,1)} %get-tuple-element.125.grad_mine, bf16[2,224,512]{2,1,0:T(8,128)(2,1)} %copy-done.12, bf16[16,8,64,512]{3,2,1,0:T(8,128)(2,1)} %bitcast.49, ...), custom_call_target="tpu_custom_call" | custom-call | flops 50000000 | bytes 184500 | tf_op jit(solution)/shard_map/self_project_back/pallas_call | solution.py:562
  234.7 5.2 %pack.1 = (f32[2,8,112,128]{3,2,1,0:T(8,128)}, f32[2,8,112,128]{3,2,1,0:T(8,128)}) custom-call(s32[3]{0:T(128)} %pad_add_fusion.where.refs_0_, f32[16,1024]{1,0:T(8,128)} %get-tuple-element.129.refs_1_, f32[2,16,1024]{2,1,0:T(8,128)} %get-tuple-element.130.refs_2_, f32[16,1024]{1,0:T(8,128)} %get-tuple-element.131.refs_3_, ...), custom_call_target="tpu_custom_call" | custom-call | flops 50000000 | bytes 184500 | tf_op jit(solution)/shard_map/pack/pallas_call | solution.py:562
  240.0 2.5 collective-permute-done.10
  243.8 6.4 %collective-permute-done.11.other = bf16[750,1024]{1,0:T(8,128)(2,1)} collective-permute-done((bf16[750,1024]{1,0:T(8,128)(2,1)}, bf16[750,1024]{1,0:T(8,128)(2,1)}, u32[]{:S(2)}, u32[]{:S(2)}) %collective-permute-start.11) | collective-permute-done | bytes 1536032 | tf_op jit(solution)/shard_map/ppermute | solution.py:51
  252.3 4.6 %encoder_total.1 = f32[750,1,1024]{2,1,0:T(1,128)} custom-call(bf16[750,1024]{1,0:T(8,128)(2,1)} %get-tuple-element.147.mine, bf16[750,1024]{1,0:T(8,128)(2,1)} %collective-permute-done.11.other), custom_call_target="tpu_custom_call" | custom-call | flops 50000000 | bytes 184500 | tf_op jit(solution)/shard_map/encoder_total/pallas_call | solution.py:562
  256.9 1.9 collective-permute-done.12
  258.8 1.8 add_convert_fusion.1
  260.6 3.4 %all-to-all-start = ((bf16[8,112,128]{2,1,0:T(8,128)(2,1)}), bf16[8,112,128]{2,1,0:T(8,128)(2,1)S(1)}, u32[]{:S(2)}, u32[]{:S(2)}) async-start(bf16[8,112,128]{2,1,0:T(8,128)(2,1)} %add_convert_fusion.1), calls=%async_computation | async-start | bytes 458752 | tf_op jit(solution)/shard_map/all_to_all | solution.py:715
  264.0 2.8 collective-permute-done.9.grad_other
  267.6 3.2 %hidden_total.1 = f32[224,1024]{1,0:T(8,128)} custom-call(bf16[224,1024]{1,0:T(8,128)(2,1)} %bitcast.61, f32[3,1024]{1,0:T(4,128)} %gains.9, f32[224,1024]{1,0:T(8,128)} %get-tuple-element.124.carried, bf16[224,1024]{1,0:T(8,128)(2,1)} %get-tuple-element.128.grad_mine, bf16[224,1024]{1,0:T(8,128)(2,1)} %copy-done.9), custom_call_target="tpu_custom_call" | custom-call | flops 50000000 | bytes 184500 | tf_op jit(solution)/shard_map/hidden_total/pallas_call | solution.py:562
  272.7 3.1 %unpack.1 = (f32[8,8,16,32]{3,2,1,0:T(8,128)}, f32[8,8,16,32]{3,2,1,0:T(8,128)}, f32[8,16,32]{2,1,0:T(8,128)}, f32[8,16,128]{2,1,0:T(8,128)}, f32[8,16,128]{2,1,0:T(8,128)}, /*index=5*/f32[8,16,32]{2,1,0:T(8,128)}) custom-call(bf16[8,112,128]{2,1,0:T(8,128)(2,1)} %copy-done.5), custom_call_target="tpu_custom_call" | custom-call | flops 50000000 | bytes 184500 | tf_op jit(solution)/shard_map/unpack/pallas_call | solution.py:562
  (62 shorter events, 23.7 us)
Async XLA Ops:
  7.2 5.5 %copy-start = (bf16[8,8,16,1024]{3,2,1,0:T(8,128)(2,1)S(1)}, bf16[8,8,16,1024]{3,2,1,0:T(8,128)(2,1)}, u32[]{:S(2)}) copy-start(bf16[8,8,16,1024]{3,2,1,0:T(8,128)(2,1)} %param.24) | copy-start | bytes 6291460
  7.2 2.2 copy-start.14
  7.2 2.2 copy-start.15
  7.2 80.6 %all-gather.5.cloned.1.call-start = ((), (), s32[]{:S(2)}) async-start(), calls=%async_computation.1 | async-start | bytes 8912896 | tf_op jit(solution)/shard_map/all_gather | solution.py:628
  9.3 154.1 %all-gather.7.cloned.1.call-start = ((), (), s32[]{:S(2)}) async-start(), calls=%async_computation.2 | async-start | bytes 8912896 | tf_op jit(solution)/shard_map/all_gather | solution.py:629
  94.9 30.4 %collective-permute-start.2 = (bf16[2,752,512]{2,1,0:T(8,128)(2,1)}, bf16[2,752,512]{2,1,0:T(8,128)(2,1)}, u32[]{:S(2)}, u32[]{:S(2)}) collective-permute-start(bf16[2,752,512]{2,1,0:T(8,128)(2,1)} %get-tuple-element.87.mine), channel_id=1, source_target_pairs={{0,2},{2,0},{1,3},{3,1},{4,6},{6,4},{5,7},{7,5},{8,10},{10,8},{9,1... | collective-permute-start | bytes 4620296 | tf_op jit(solution)/shard_map/ppermute | solution.py:51
  101.0 3.4 %collective-permute-start = (bf16[2,224,512]{2,1,0:T(8,128)(2,1)}, bf16[2,224,512]{2,1,0:T(8,128)(2,1)S(1)}, u32[]{:S(2)}, u32[]{:S(2)}) collective-permute-start(bf16[2,224,512]{2,1,0:T(8,128)(2,1)} %get-tuple-element.85.mine.refs_13_), channel_id=1, source_target_pairs={{0,2},{2,0},{1,3},{3,1},{4,6},{6,4},{5,7},{7,5},{8,10},{10,8},{9,1... | collective-permute-start | bytes 1376264 | tf_op jit(solution)/shard_map/ppermute | solution.py:51
  104.4 0.8 copy-start.3
  112.4 12.9 %collective-permute-start.1 = (bf16[224,1024]{1,0:T(8,128)(2,1)}, bf16[224,1024]{1,0:T(8,128)(2,1)S(1)}, u32[]{:S(2)}, u32[]{:S(2)}) collective-permute-start(bf16[224,1024]{1,0:T(8,128)(2,1)} %get-tuple-element.86.branch_mine), channel_id=1, source_target_pairs={{0,1},{1,0},{2,3},{3,2},{4,5},{5,4},{6,7},{7,6},{8,9},{9,8},{10,11... | collective-permute-start | bytes 1376264 | tf_op jit(solution)/shard_map/ppermute | solution.py:51
  125.4 0.8 copy-start.13
  140.3 12.1 %collective-permute-start.3 = (bf16[224,1024]{1,0:T(8,128)(2,1)}, bf16[224,1024]{1,0:T(8,128)(2,1)S(1)}, u32[]{:S(2)}, u32[]{:S(2)}) collective-permute-start(bf16[224,1024]{1,0:T(8,128)(2,1)} %get-tuple-element.89.branch_mine), channel_id=1, source_target_pairs={{0,1},{1,0},{2,3},{3,2},{4,5},{5,4},{6,7},{7,6},{8,9},{9,8},{10,11... | collective-permute-start | bytes 1376264 | tf_op jit(solution)/shard_map/ppermute | solution.py:51
  152.4 0.8 copy-start.8
  171.6 12.9 %collective-permute-start.4 = (bf16[224,1024]{1,0:T(8,128)(2,1)}, bf16[224,1024]{1,0:T(8,128)(2,1)S(1)}, u32[]{:S(2)}, u32[]{:S(2)}) collective-permute-start(bf16[224,1024]{1,0:T(8,128)(2,1)} %get-tuple-element.94.grad_mine), channel_id=1, source_target_pairs={{0,1},{1,0},{2,3},{3,2},{4,5},{5,4},{6,7},{7,6},{8,9},{9,8},{10,11... | collective-permute-start | bytes 1376264 | tf_op jit(solution)/shard_map/ppermute | solution.py:51
  184.5 1.5 copy-start.6
  184.5 16.5 %collective-permute-start.5 = (bf16[224,1024]{1,0:T(8,128)(2,1)}, bf16[224,1024]{1,0:T(8,128)(2,1)S(1)}, u32[]{:S(2)}, u32[]{:S(2)}) collective-permute-start(bf16[224,1024]{1,0:T(8,128)(2,1)} %get-tuple-element.109), channel_id=1, source_target_pairs={{0,1},{1,0},{2,3},{3,2},{4,5},{5,4},{6,7},{7,6},{8,9},{9,8},{10,11... | collective-permute-start | bytes 1376264 | tf_op jit(solution)/shard_map/ppermute | solution.py:51
  201.0 3.6 %collective-permute-start.6 = (bf16[2,752,512]{2,1,0:T(8,128)(2,1)}, bf16[2,752,512]{2,1,0:T(8,128)(2,1)S(1)}, u32[]{:S(2)}, u32[]{:S(2)}) collective-permute-start(bf16[2,752,512]{2,1,0:T(8,128)(2,1)} %get-tuple-element.112), channel_id=1, source_target_pairs={{0,2},{2,0},{1,3},{3,1},{4,6},{6,4},{5,7},{7,5},{8,10},{10,8},{9,1... | collective-permute-start | bytes 4620296 | tf_op jit(solution)/shard_map/ppermute | solution.py:51
  201.0 13.1 %collective-permute-start.7 = (bf16[224,1024]{1,0:T(8,128)(2,1)}, bf16[224,1024]{1,0:T(8,128)(2,1)S(1)}, u32[]{:S(2)}, u32[]{:S(2)}) collective-permute-start(bf16[224,1024]{1,0:T(8,128)(2,1)} %get-tuple-element.110.refs_3_), channel_id=1, source_target_pairs={{0,1},{1,0},{2,3},{3,2},{4,5},{5,4},{6,7},{7,6},{8,9},{9,8},{10,11... | collective-permute-start | bytes 1376264 | tf_op jit(solution)/shard_map/ppermute | solution.py:51
  204.6 1.1 copy-start.4
  214.2 0.8 copy-start.11
  214.2 36.0 %collective-permute-start.11 = (bf16[750,1024]{1,0:T(8,128)(2,1)}, bf16[750,1024]{1,0:T(8,128)(2,1)}, u32[]{:S(2)}, u32[]{:S(2)}) collective-permute-start(bf16[750,1024]{1,0:T(8,128)(2,1)} %get-tuple-element.147.mine), channel_id=1, source_target_pairs={{0,1},{1,0},{2,3},{3,2},{4,5},{5,4},{6,7},{7,6},{8,9},{9,8},{10,11... | collective-permute-start | bytes 4608008 | tf_op jit(solution)/shard_map/ppermute | solution.py:51
  214.9 12.4 %copy-start.2 = (f32[224,1024]{1,0:T(8,128)S(1)}, f32[224,1024]{1,0:T(8,128)}, u32[]{:S(2)}) copy-start(f32[224,1024]{1,0:T(8,128)} %get-tuple-element.90.rows) | copy-start | bytes 2752516
  214.9 12.4 %copy-start.10 = (bf16[224,1024]{1,0:T(8,128)(2,1)S(1)}, bf16[224,1024]{1,0:T(8,128)(2,1)}, u32[]{:S(2)}) copy-start(bf16[224,1024]{1,0:T(8,128)(2,1)} %get-tuple-element.109) | copy-start | bytes 1376260
  227.2 2.1 collective-permute-start.8
  229.3 0.8 copy-start.12
  234.7 16.3 %copy-start.7 = (bf16[224,1024]{1,0:T(8,128)(2,1)S(1)}, bf16[224,1024]{1,0:T(8,128)(2,1)}, u32[]{:S(2)}) copy-start(bf16[224,1024]{1,0:T(8,128)(2,1)} %get-tuple-element.128.grad_mine) | copy-start | bytes 1376260
  239.9 2.7 collective-permute-start.10
  250.2 8.6 %collective-permute-start.12 = (bf16[8,112,128]{2,1,0:T(8,128)(2,1)S(1)}, bf16[8,112,128]{2,1,0:T(8,128)(2,1)}, u32[]{:S(2)}, u32[]{:S(2)}) collective-permute-start(bf16[8,112,128]{2,1,0:T(8,128)(2,1)S(1)} %get-tuple-element.148), channel_id=1, source_target_pairs={{0,1},{1,0},{2,3},{3,2},{4,5},{5,4},{6,7},{7,6},{8,9},{9,8},{10,11... | collective-permute-start | bytes 688136 | tf_op jit(solution)/shard_map/ppermute | solution.py:51
  251.0 15.9 %collective-permute-start.9 = (bf16[224,1024]{1,0:T(8,128)(2,1)S(1)}, bf16[224,1024]{1,0:T(8,128)(2,1)S(1)}, u32[]{:S(2)}, u32[]{:S(2)}) collective-permute-start(bf16[224,1024]{1,0:T(8,128)(2,1)S(1)} %copy-done.7), channel_id=1, source_target_pairs={{0,1},{1,0},{2,3},{3,2},{4,5},{5,4},{6,7},{7,6},{8,9},{9,8},{10,11... | collective-permute-start | bytes 1376264 | tf_op jit(solution)/shard_map/ppermute | solution.py:51
  258.8 17.0 %copy-start.1 = (bf16[8,8,16,1024]{3,2,1,0:T(8,128)(2,1)S(1)}, bf16[8,8,16,1024]{3,2,1,0:T(8,128)(2,1)}, u32[]{:S(2)}) copy-start(bf16[8,8,16,1024]{3,2,1,0:T(8,128)(2,1)} %param.24) | copy-start | bytes 6291460
  260.6 11.3 %all-to-all-start = ((bf16[8,112,128]{2,1,0:T(8,128)(2,1)}), bf16[8,112,128]{2,1,0:T(8,128)(2,1)S(1)}, u32[]{:S(2)}, u32[]{:S(2)}) async-start(bf16[8,112,128]{2,1,0:T(8,128)(2,1)} %add_convert_fusion.1), calls=%async_computation | async-start | bytes 458752 | tf_op jit(solution)/shard_map/all_to_all | solution.py:715
  266.8 0.8 copy-start.9
  272.0 0.7 copy-start.5
Sparse Core Ops, SparseCore 0:
  10.8 77.0 all-gather.4
  90.5 72.8 all-gather.6
